TPU v7x, 512 devices: a whole 4x8x8 slice. The times are simulated.
512 devices in a mesh: refl: 8 (over y), slab: 64 (over z, x, core).
Axes of the slice: x: 4, y: 8, z: 8, core: 2. Of those that a mesh axis runs over, the one named last changes fastest.
Arguments:
- detector: bfloat16 [8, 65536, 2, 128], P('refl', 'slab'), may hold values from -6 to 6
- owners: int32 [8, 65536, 1], P('refl', 'slab'), may hold values from 0 to 63; in each aligned block of 1024 rows (0 to 1023, 1024 to 2047, ..., all dimensions but the last counted through in order) at most 32 rows name the same one
- block_ids: int32 [8, 65536], P('refl', 'slab'), may hold values from 0 to 63
- kernel_ids: int32 [8, 65536], P('refl', 'slab'), may hold values from 0 to 7
- kernels: bfloat16 [8, 128, 128], replicated, may hold values from -0.5 to 0.5
- bragg_vectors: float32 [8, 3], replicated, may hold values from -3 to 3
- object_field: float32 [8, 128, 32, 2, 128], P('refl', 'slab'), may hold values from -6 to 6
Outputs:
- updated: float32 [8, 128, 32, 2, 128], P('refl', 'slab')
Inputs may be any that keep to these rules, and one draw needn't show every extreme that they name: `owners`: among the tiles of one device and one reflection, at most 32 name the same owner, a bound that some block reaches.
All inputs are finite; a program needn't handle non-finite values.
Results may differ from a plain program's by a relative error of at most 0.0003.
Values may be sent and summed in bfloat16 or wider, within the bound.
A program may use at most 64 MiB of HBM per device.

v0:
```python
import jax
import jax.numpy as jnp
from jax import lax
from jax.sharding import PartitionSpec as P


def extended(block, sides, width):
    for axis, dim in sides:
        count = lax.axis_size(axis)
        forward = [(i, i + 1) for i in range(count - 1)]
        backward = [(target, source) for source, target in forward]
        low = lax.ppermute(
            lax.slice_in_dim(block, block.shape[dim] - width, None, axis=dim), axis, forward
        )
        high = lax.ppermute(lax.slice_in_dim(block, 0, width, axis=dim), axis, backward)
        block = jnp.concatenate([low, block, high], axis=dim)
    return block


def central(field, dimension):
    widths = [(0, 0)] * field.ndim
    widths[dimension] = (1, 1)
    padded = jnp.pad(field, widths)
    length = field.shape[dimension]
    return 0.5 * (
        lax.slice_in_dim(padded, 2, length + 2, axis=dimension)
        - lax.slice_in_dim(padded, 0, length, axis=dimension)
    )


def phase_term(obj_real, obj_imag, grad_x, grad_y, grad_z, qrow):
    term_x = obj_real * grad_x[:, :, 1] - obj_imag * grad_x[:, :, 0]
    term_y = obj_real * grad_y[:, :, 1] - obj_imag * grad_y[:, :, 0]
    term_z = obj_real * grad_z[:, :, 1] - obj_imag * grad_z[:, :, 0]
    return qrow[0] * term_x + qrow[1] * term_y + qrow[2] * term_z


def project_rows(row_values, row_codes, kernels):
    kernel_count = kernels.shape[0]
    tile_width = kernels.shape[2]
    shaped = row_values.reshape(row_values.shape[:-1] + (2, tile_width))
    kernel_of = jnp.maximum(row_codes, 0) % kernel_count
    result = jnp.zeros(shaped.shape, jnp.float32)
    for kernel_index in range(kernel_count):
        product = jnp.einsum(
            "...cz,zw->...cw", shaped, kernels[kernel_index], preferred_element_type=jnp.float32
        )
        result = jnp.where((kernel_of == kernel_index)[..., None, None], product, result)
    return result


def per_device(detector, owners, block_ids, kernel_ids, kernels, bragg_vectors, object_field):
    slab_count = lax.axis_size("slab")
    plane_count = object_field.shape[1]
    row_count = object_field.shape[2]
    block_count = plane_count * row_count
    kernel_count = kernels.shape[0]
    tile_count = detector.shape[1]
    tile_width = detector.shape[3]
    capacity = 2 * tile_count // slab_count
    values = detector[0].reshape(tile_count, 2 * tile_width)
    codes = block_ids[0] * kernel_count + kernel_ids[0]
    owner = owners[0, :, 0]
    owner_hot = (owner[:, None] == jnp.arange(slab_count, dtype=jnp.int32)[None, :]).astype(
        jnp.int32
    )
    ranks = jnp.cumsum(owner_hot, axis=0) - owner_hot
    slots = jnp.sum(ranks * owner_hot, axis=1)
    flat_slot = owner * capacity + slots
    placed = flat_slot[None, :] == jnp.arange(slab_count * capacity, dtype=jnp.int32)[:, None]
    sent = jnp.dot(placed.astype(jnp.bfloat16), values, preferred_element_type=jnp.float32).astype(
        jnp.bfloat16
    )
    sent = sent.reshape(slab_count, capacity, 2 * tile_width)
    sent_codes = jnp.max(jnp.where(placed, codes[None, :], -1), axis=1).reshape(
        slab_count, capacity
    )
    got_values, got_codes = (
        lax.all_to_all(sent, "slab", split_axis=0, concat_axis=0, tiled=True),
        lax.all_to_all(sent_codes, "slab", split_axis=0, concat_axis=0, tiled=True),
    )
    projected = project_rows(got_values, got_codes, kernels)
    row_total = slab_count * capacity
    blocks = (jnp.maximum(got_codes, 0) // kernel_count).reshape(row_total).astype(jnp.int32)
    gridded = jax.ops.segment_sum(
        projected.reshape(row_total, 2 * tile_width), blocks, num_segments=block_count
    )
    gridded = gridded.reshape(plane_count, row_count, 2, tile_width)
    padded = extended(gridded, (("slab", 0),), 1)
    grad_x = 0.5 * (padded[2:] - padded[:-2])
    grad_y = central(gridded, 1)
    grad_z = central(gridded, 3)
    refl_count = bragg_vectors.shape[0]
    places = jnp.arange(refl_count, dtype=jnp.int32)
    my_refl = lax.axis_index("refl")
    q_self = jnp.sum(jnp.where((places == my_refl)[:, None], bragg_vectors, 0.0), axis=0)
    mate = my_refl + 1 - 2 * (my_refl % 2)
    q_other = jnp.sum(jnp.where((places == mate)[:, None], bragg_vectors, 0.0), axis=0)
    obj = object_field[0]
    obj_real = obj[:, :, 0]
    obj_imag = obj[:, :, 1]
    phase = phase_term(obj_real, obj_imag, grad_x, grad_y, grad_z, q_self)
    diff = q_self - q_other
    total = lax.psum(q_self[:, None, None, None] * phase[None], "refl")
    shift = diff[0] * total[0] + diff[1] * total[1] + diff[2] * total[2]
    new_real = obj_real - 0.5 * (gridded[:, :, 0] - obj_imag * shift)
    new_imag = obj_imag - 0.5 * (gridded[:, :, 1] + obj_real * shift)
    return jnp.stack([new_real, new_imag], axis=2)[None]


def solution(mesh):
    in_specs = (
        P("refl", "slab", None, None),
        P("refl", "slab", None),
        P("refl", "slab"),
        P("refl", "slab"),
        P(),
        P(),
        P("refl", "slab", None, None, None),
    )
    out_specs = P("refl", "slab", None, None, None)
    return jax.shard_map(
        per_device, mesh=mesh, in_specs=in_specs, out_specs=out_specs, check_vma=False
    )
```

profile of v0, /device:TPU:6, one launch (start us, length us, event | category | flops | bytes accessed | tf_op | source)
XLA Modules:
  0.0 202.7 jit_solution(3129111525196096864)
XLA Ops:
  6.5 0.8 fusion.26
  7.3 18.0 %reduce-window.6 = s32[64,8,128]{2,1,0:T(8,128)S(1)} reduce-window(s32[64,8,128]{2,1,0:T(8,128)S(1)} %fusion.26, s32[]{:T(128)} %constant.65.clone.1), window={size=1x1x128 pad=0_0x0_0x127_0}, to_apply=%region_0.0 | reduce-window | flops 8323072 | bytes 524292 | tf_op jit(solution)/shard_map/reduce-window
  26.0 1.2 select_reduce_fusion
  27.2 0.7 all_to_all.9
  27.9 13.8 %all-to-all-start = ((s32[64,1,32]{2,1,0:T(1,128)}), s32[64,1,32]{2,1,0:T(1,128)S(1)}, u32[]{:S(2)}, u32[]{:S(2)}) async-start(s32[64,1,32]{2,1,0:T(1,128)} %bitcast.6), calls=%async_computation | async-start | bytes 65536 | tf_op jit(solution)/shard_map/all_to_all | solution.py:80
  41.7 2.6 %fusion.2 = bf16[2048,256]{1,0:T(8,128)(2,1)} fusion(s32[1024]{0:T(1024)S(1)} %multiply_add_fusion.1, bf16[128,8,2,128]{3,2,1,0:T(2,128)(2,1)S(1)} %bitcast.161), kind=kOutput, calls=%fused_computation.5 | convolution fusion | flops 1076363264 | bytes 1576960 | tf_op jit(solution)/shard_map/dot_general | solution.py:71
  44.4 5.2 %all-to-all-done = s32[64,1,32]{2,1,0:T(1,128)S(1)} async-done(((s32[64,1,32]{2,1,0:T(1,128)}), s32[64,1,32]{2,1,0:T(1,128)S(1)}, u32[]{:S(2)}, u32[]{:S(2)}) %all-to-all-start) | async-done | bytes 8224 | tf_op jit(solution)/shard_map/all_to_all | solution.py:80
  49.5 6.3 %all-to-all-start.1 = ((bf16[64,32,256]{2,1,0:T(8,128)(2,1)}), bf16[64,32,256]{2,1,0:T(8,128)(2,1)S(1)}, u32[]{:S(2)}, u32[]{:S(2)}) async-start(bf16[64,32,256]{2,1,0:T(8,128)(2,1)} %bitcast.9), calls=%async_computation.1 | async-start | bytes 2097152 | tf_op jit(solution)/shard_map/all_to_all | solution.py:79
  56.8 27.9 %all-to-all-done.1 = bf16[64,32,256]{2,1,0:T(8,128)(2,1)S(1)} async-done(((bf16[64,32,256]{2,1,0:T(8,128)(2,1)}), bf16[64,32,256]{2,1,0:T(8,128)(2,1)S(1)}, u32[]{:S(2)}, u32[]{:S(2)}) %all-to-all-start.1) | async-done | bytes 1048608 | tf_op jit(solution)/shard_map/all_to_all | solution.py:79
  85.1 0.4 fusion.17
  86.4 0.4 fusion.11
  87.7 2.3 %select_select_fusion = f32[64,32,2,128]{3,1,2,0:T(8,128)S(1)} fusion(f32[64,32,2,128]{3,1,2,0:T(8,128)S(1)} %fusion.19, f32[64,32,2,128]{3,1,2,0:T(8,128)S(1)} %fusion.17, f32[64,32,2,128]{3,1,2,0:T(8,128)S(1)} %fusion.15, f32[64,32,2,128]{3,1,2,0:T(8,128)S(1)} %fusion.13, f32[64,32,2,128]{3,1,2,0:T(8,128)S(1)} %fusion.11, ...), kind=kOutput, calls=%fused_computation.9 | convolution fusion | flops 138412032 | bytes 17924096 | tf_op jit(solution)/shard_map/...cz,zw->...cw/dot_general | solution.py:45
  90.0 1.9 copy.69
  91.9 11.7 %scatter_custom_fusion = f32[64,256]{1,0:T(8,128)S(1)} fusion(s32[2048]{0:T(1024)S(1)} %bitcast.159, f32[256,8,2,128]{3,2,1,0:T(2,128)S(1)} %bitcast.149, f32[]{:T(128)} %constant.63.clone.1), kind=kCustom, calls=%fused_computation.6 | custom fusion | flops 524288 | bytes 2162692 | tf_op jit(solution)/shard_map/scatter-add | solution.py:85
  103.7 1.9 collective-permute-start.1
  105.6 3.6 %collective-permute-start = (f32[1,32,2,128]{3,1,2,0:T(8,128)S(1)}, f32[1,32,2,128]{3,1,2,0:T(8,128)S(1)}, u32[]{:S(2)}, u32[]{:S(2)}) collective-permute-start(f32[1,32,2,128]{3,1,2,0:T(8,128)S(1)} %copy.71), channel_id=1, source_target_pairs={{1,0},{2,1},{3,2},{4,3},{5,4},{6,5},{7,6},{8,7},{9,8},{10,9},{11,1... | collective-permute-start | bytes 98312 | tf_op jit(solution)/shard_map/ppermute | solution.py:15
  109.3 0.7 fusion.77
  110.0 0.8 collective-permute-done
  111.0 1.9 fusion.49
  112.9 0.7 broadcast_multiply_fusion
  113.6 0.6 fusion.76
  114.3 78.2 %all-reduce.4.cloned.1.call-done = f32[3,2,32,128]{3,2,1,0:T(8,128)} async-done(((f32[3,2,32,128]{3,2,1,0:T(8,128)}), f32[3,2,32,128]{3,2,1,0:T(8,128)}) %all-reduce.4.cloned.1.call-update) | async-done | bytes 98320 | tf_op jit(solution)/shard_map/psum | solution.py:104
  192.5 2.7 %fusion.56 = (f32[2,32,1,128]{3,1,2,0:T(8,128)S(1)}, f32[2,32,1,128]{3,1,2,0:T(8,128)S(1)}) fusion(f32[2,32,2,128]{3,1,2,0:T(8,128)S(1)} %copy.70, f32[2,32,2,128]{3,1,2,0:T(8,128)S(1)} %bitcast.152, f32[3,2,32,128]{3,2,1,0:T(8,128)} %all-reduce.4.cloned.1.call-done, f32[]{:T(128)} %bitcast.40, f32[]{:T(128)} %bitcast.39, f32[]{:T(128)} %bitcast.34), kind=kLoop, calls=%fused_computation.86 | loop fusion | flops 73728 | bytes 262156 | tf_op jit(solution)/shard_map/sub | solution.py:106
  195.2 0.7 copy.78
  (51 shorter events, 3.9 us)
Async XLA Ops:
  6.5 19.3 %copy-start.2 = (s32[1,1024,1]{1,2,0:T(1,128)S(1)}, s32[1,1024,1]{1,2,0:T(1,128)}, u32[]{:S(2)}) copy-start(s32[1,1024,1]{1,2,0:T(1,128)} %param.8) | copy-start | bytes 12292
  6.5 19.4 %copy-start.3 = (s32[1,1024]{1,0:T(1,128)S(1)}, s32[1,1024]{1,0:T(1,128)}, u32[]{:S(2)}) copy-start(s32[1,1024]{1,0:T(1,128)} %param.10) | copy-start | bytes 12292
  6.5 19.4 %copy-start.4 = (s32[1,1024]{1,0:T(1,128)S(1)}, s32[1,1024]{1,0:T(1,128)}, u32[]{:S(2)}) copy-start(s32[1,1024]{1,0:T(1,128)} %param.9) | copy-start | bytes 12292
  6.5 35.2 %copy-start.6 = (bf16[1,1024,2,128]{3,2,1,0:T(2,128)(2,1)S(1)}, bf16[1,1024,2,128]{3,2,1,0:T(2,128)(2,1)}, u32[]{:S(2)}) copy-start(bf16[1,1024,2,128]{3,2,1,0:T(2,128)(2,1)} %param.7) | copy-start | bytes 1572868
  27.9 21.6 %all-to-all-start = ((s32[64,1,32]{2,1,0:T(1,128)}), s32[64,1,32]{2,1,0:T(1,128)S(1)}, u32[]{:S(2)}, u32[]{:S(2)}) async-start(s32[64,1,32]{2,1,0:T(1,128)} %bitcast.6), calls=%async_computation | async-start | bytes 65536 | tf_op jit(solution)/shard_map/all_to_all | solution.py:80
  44.4 11.7 %copy-start.5 = (f32[8,3]{0,1:T(4,128)S(1)}, f32[8,3]{0,1:T(4,128)}, u32[]{:S(2)}) copy-start(f32[8,3]{0,1:T(4,128)} %param.12) | copy-start | bytes 292
  44.4 40.4 %copy-start = (bf16[8,128,128]{2,1,0:T(8,128)(2,1)S(1)}, bf16[8,128,128]{2,1,0:T(8,128)(2,1)}, u32[]{:S(2)}) copy-start(bf16[8,128,128]{2,1,0:T(8,128)(2,1)} %param.11) | copy-start | bytes 786436
  49.5 35.2 %all-to-all-start.1 = ((bf16[64,32,256]{2,1,0:T(8,128)(2,1)}), bf16[64,32,256]{2,1,0:T(8,128)(2,1)S(1)}, u32[]{:S(2)}, u32[]{:S(2)}) async-start(bf16[64,32,256]{2,1,0:T(8,128)(2,1)} %bitcast.9), calls=%async_computation.1 | async-start | bytes 2097152 | tf_op jit(solution)/shard_map/all_to_all | solution.py:79
  55.8 136.6 %all-reduce.4.cloned.1.call-start = ((), (), s32[]{:S(2)}) async-start(), calls=%async_computation.2 | async-start | bytes 196608 | tf_op jit(solution)/shard_map/psum | solution.py:104
  91.9 18.0 %copy-start.1 = (f32[1,2,32,2,128]{4,3,2,1,0:T(2,128)S(1)}, f32[1,2,32,2,128]{4,3,2,1,0:T(2,128)}, u32[]{:S(2)}) copy-start(f32[1,2,32,2,128]{4,3,2,1,0:T(2,128)} %param.13) | copy-start | bytes 196612
  103.7 6.4 %collective-permute-start.1 = (f32[1,32,2,128]{3,1,2,0:T(8,128)S(1)}, f32[1,32,2,128]{3,1,2,0:T(8,128)S(1)}, u32[]{:S(2)}, u32[]{:S(2)}) collective-permute-start(f32[1,32,2,128]{3,1,2,0:T(8,128)S(1)} %copy.73), channel_id=1, source_target_pairs={{0,1},{1,2},{2,3},{3,4},{4,5},{5,6},{6,7},{7,8},{8,9},{9,10},{10,1... | collective-permute-start | bytes 98312 | tf_op jit(solution)/shard_map/ppermute | solution.py:12
  105.6 5.2 %collective-permute-start = (f32[1,32,2,128]{3,1,2,0:T(8,128)S(1)}, f32[1,32,2,128]{3,1,2,0:T(8,128)S(1)}, u32[]{:S(2)}, u32[]{:S(2)}) collective-permute-start(f32[1,32,2,128]{3,1,2,0:T(8,128)S(1)} %copy.71), channel_id=1, source_target_pairs={{1,0},{2,1},{3,2},{4,3},{5,4},{6,5},{7,6},{8,7},{9,8},{10,9},{11,1... | collective-permute-start | bytes 98312 | tf_op jit(solution)/shard_map/ppermute | solution.py:15
Sparse Core Ops, SparseCore 0:
  113.7 78.6 all-reduce.3
where the time goes:
time: 203 us
  waiting for transfers between devices  112 us (55%)
  other arithmetic  37.9 us (19%)
  starting transfers between devices  25.9 us (13%)
  between operations  13.7 us (7%)
  matrix products  7.87 us (4%)
  local copies, waits for them, and re-layouts  5.25 us (3%)
    psum x1, waiting for transfers between devices, per_device(): total = lax.psum(q_self[:, None, None, None] * phase[None], 'refl')  78.2 us
    all_to_all x1, waiting for transfers between devices, per_device(): lax.all_to_all(sent, 'slab', split_axis=0, concat_axis=0, tiled=True)  27.9 us
    another operation x3, other arithmetic  18.2 us
    all_to_all x1, starting transfers between devices, per_device(): lax.all_to_all(sent_codes, 'slab', split_axis=0, concat_axis=0, tiled=True)  13.8 us
    scatter-add x1, other arithmetic, per_device(): jax.ops.segment_sum(projected.reshape(row_total, 2 * tile_width), blocks,...  11.7 us
    all_to_all x1, starting transfers between devices, per_device(): lax.all_to_all(sent, 'slab', split_axis=0, concat_axis=0, tiled=True)  6.29 us
    dot_general x8, matrix products, project_rows(): jnp.einsum('...cz,zw->...cw', shaped, kernels[kernel_index], preferred_el...  5.24 us
    all_to_all x1, waiting for transfers between devices, per_device(): lax.all_to_all(sent_codes, 'slab', split_axis=0, concat_axis=0, tiled=True)  5.15 us
  transfers between devices with their start and end apart: 5, of which 4 were waited for; matrix products, arithmetic and copies ran while one was open for 2% of the time, Pallas kernels for 0%

commit v1 on v0

--- a/solution.py
+++ b/solution.py
@@ -35,18 +35,14 @@
     return qrow[0] * term_x + qrow[1] * term_y + qrow[2] * term_z
 
 
-def project_rows(row_values, row_codes, kernels):
-    kernel_count = kernels.shape[0]
-    tile_width = kernels.shape[2]
-    shaped = row_values.reshape(row_values.shape[:-1] + (2, tile_width))
-    kernel_of = jnp.maximum(row_codes, 0) % kernel_count
-    result = jnp.zeros(shaped.shape, jnp.float32)
-    for kernel_index in range(kernel_count):
-        product = jnp.einsum(
-            "...cz,zw->...cw", shaped, kernels[kernel_index], preferred_element_type=jnp.float32
-        )
-        result = jnp.where((kernel_of == kernel_index)[..., None, None], product, result)
-    return result
+def butterfly_sum(value, axis):
+    count = lax.axis_size(axis)
+    distance = 1
+    while distance < count:
+        pairs = [(i, i ^ distance) for i in range(count)]
+        value = value + lax.ppermute(value, axis, pairs)
+        distance *= 2
+    return value
 
 
 def per_device(detector, owners, block_ids, kernel_ids, kernels, bragg_vectors, object_field):
@@ -57,33 +53,51 @@
     kernel_count = kernels.shape[0]
     tile_count = detector.shape[1]
     tile_width = detector.shape[3]
+    row_width = 2 * tile_width
     capacity = 2 * tile_count // slab_count
-    values = detector[0].reshape(tile_count, 2 * tile_width)
-    codes = block_ids[0] * kernel_count + kernel_ids[0]
+    values = detector[0].reshape(tile_count, row_width)
     owner = owners[0, :, 0]
-    owner_hot = (owner[:, None] == jnp.arange(slab_count, dtype=jnp.int32)[None, :]).astype(
-        jnp.int32
+    order = lax.broadcasted_iota(jnp.int32, (tile_count, tile_count), 1) < lax.broadcasted_iota(
+        jnp.int32, (tile_count, tile_count), 0
     )
-    ranks = jnp.cumsum(owner_hot, axis=0) - owner_hot
-    slots = jnp.sum(ranks * owner_hot, axis=1)
+    same = (owner[:, None] == owner[None, :]) & order
+    slots = jnp.sum(same.astype(jnp.int32), axis=1)
     flat_slot = owner * capacity + slots
-    placed = flat_slot[None, :] == jnp.arange(slab_count * capacity, dtype=jnp.int32)[:, None]
-    sent = jnp.dot(placed.astype(jnp.bfloat16), values, preferred_element_type=jnp.float32).astype(
-        jnp.bfloat16
-    )
-    sent = sent.reshape(slab_count, capacity, 2 * tile_width)
-    sent_codes = jnp.max(jnp.where(placed, codes[None, :], -1), axis=1).reshape(
-        slab_count, capacity
-    )
-    got_values, got_codes = (
-        lax.all_to_all(sent, "slab", split_axis=0, concat_axis=0, tiled=True),
-        lax.all_to_all(sent_codes, "slab", split_axis=0, concat_axis=0, tiled=True),
-    )
-    projected = project_rows(got_values, got_codes, kernels)
+    placed = (
+        flat_slot[None, :] == lax.broadcasted_iota(jnp.int32, (slab_count * capacity, tile_count), 0)
+    ).astype(jnp.bfloat16)
+    lane = lax.broadcasted_iota(jnp.int32, (tile_count, 128), 1)
+    extra = jnp.where(
+        lane == 0, block_ids[0][:, None], jnp.where(lane == 1, kernel_ids[0][:, None], 0)
+    ).astype(jnp.bfloat16)
+    table = jnp.concatenate([values, extra], axis=1)
+    sent = jnp.dot(placed, table, preferred_element_type=jnp.float32)
+    sent = sent.reshape(slab_count, capacity, row_width + 128)
+    data = sent[:, :, :row_width].astype(jnp.bfloat16).reshape(slab_count, capacity * row_width)
+    code_rows = jnp.concatenate(
+        [sent[:, :, row_width], sent[:, :, row_width + 1], jnp.zeros((slab_count, 128 - 2 * capacity), jnp.float32)],
+        axis=1,
+    ).astype(jnp.bfloat16)
+    packet = jnp.concatenate([data, code_rows], axis=1)
+    got = lax.all_to_all(packet, "slab", split_axis=0, concat_axis=0, tiled=True)
     row_total = slab_count * capacity
-    blocks = (jnp.maximum(got_codes, 0) // kernel_count).reshape(row_total).astype(jnp.int32)
-    gridded = jax.ops.segment_sum(
-        projected.reshape(row_total, 2 * tile_width), blocks, num_segments=block_count
+    rows = got[:, : capacity * row_width].reshape(row_total, row_width)
+    got_blocks = got[:, capacity * row_width : capacity * row_width + capacity].astype(jnp.int32)
+    got_kernels = got[
+        :, capacity * row_width + capacity : capacity * row_width + 2 * capacity
+    ].astype(jnp.int32)
+    got_codes = (got_blocks * kernel_count + got_kernels).reshape(row_total)
+    chosen = (
+        got_codes[None, :]
+        == lax.broadcasted_iota(jnp.int32, (block_count * kernel_count, row_total), 0)
+    ).astype(jnp.bfloat16)
+    summed = jnp.dot(chosen, rows, preferred_element_type=jnp.float32)
+    summed = summed.reshape(block_count, kernel_count, 2, tile_width).transpose(0, 2, 1, 3)
+    gridded = jnp.dot(
+        summed.reshape(block_count * 2, kernel_count * tile_width),
+        kernels.astype(jnp.float32).reshape(kernel_count * tile_width, tile_width),
+        precision=lax.Precision.HIGHEST,
+        preferred_element_type=jnp.float32,
     )
     gridded = gridded.reshape(plane_count, row_count, 2, tile_width)
     padded = extended(gridded, (("slab", 0),), 1)
@@ -101,7 +115,7 @@
     obj_imag = obj[:, :, 1]
     phase = phase_term(obj_real, obj_imag, grad_x, grad_y, grad_z, q_self)
     diff = q_self - q_other
-    total = lax.psum(q_self[:, None, None, None] * phase[None], "refl")
+    total = butterfly_sum(q_self[:, None, None, None] * phase[None], "refl")
     shift = diff[0] * total[0] + diff[1] * total[1] + diff[2] * total[2]
     new_real = obj_real - 0.5 * (gridded[:, :, 0] - obj_imag * shift)
     new_imag = obj_imag - 0.5 * (gridded[:, :, 1] + obj_real * shift)

time: 203 us -> 101 us (0.50)
  the two profiles are of different devices: /device:TPU:6 before, /device:TPU:96 now
where the time goes in v1:
time: 101 us
  waiting for transfers between devices  51.7 us (51%)
  starting transfers between devices  25.5 us (25%)
  local copies, waits for them, and re-layouts  10.6 us (10%)
  other arithmetic  8.9 us (9%)
  matrix products  3.53 us (3%)
    all_to_all x1, waiting for transfers between devices, per_device(): lax.all_to_all(packet, 'slab', split_axis=0, concat_axis=0, tiled=True)  28.4 us
    ppermute x3, waiting for transfers between devices, butterfly_sum(): value = value + lax.ppermute(value, axis, pairs)  18.6 us
    all_to_all x1, starting transfers between devices, per_device(): lax.all_to_all(packet, 'slab', split_axis=0, concat_axis=0, tiled=True)  13 us
    ppermute x3, starting transfers between devices, butterfly_sum(): value = value + lax.ppermute(value, axis, pairs)  7.18 us
    ppermute x1, waiting for transfers between devices, extended(): lax.ppermute(lax.slice_in_dim(block, block.shape[dim] - width, None, axis...  4.72 us
    unnamed x12, local copies, waits for them, and re-layouts  4.68 us
    ppermute x1, starting transfers between devices, extended(): lax.ppermute(lax.slice_in_dim(block, 0, width, axis=dim), axis, backward)  3.37 us
    dot_general x1, matrix products, per_device(): sent = jnp.dot(placed, table, preferred_element_type=jnp.float32)  2.35 us
  transfers between devices with their start and end apart: 6, of which 5 were waited for; matrix products, arithmetic and copies ran while one was open for 1% of the time, Pallas kernels for 0%

profile of v1, /device:TPU:96, one launch (start us, length us, event | category | flops | bytes accessed | tf_op | source)
XLA Modules:
  0.0 100.5 jit_solution(12750471451522075378)
XLA Ops:
  0.0 1.3 %convert_reduce_fusion = s32[1024]{0:T(1024)S(1)} fusion(s32[1024]{0:T(1024)} %bitcast.79), kind=kLoop, calls=%fused_computation.3 | loop fusion | flops 5241856 | bytes 8192 | tf_op jit(solution)/shard_map/reduce_sum | solution.py:64
  1.3 0.7 multiply_add_fusion.1
  2.0 1.1 %copy.71 = bf16[128,8,2,128]{3,1,2,0:T(8,128)(2,1)S(1)} copy(bf16[128,8,2,128]{3,2,1,0:T(2,128)(2,1)} %bitcast.70) | data formatting | bytes 1048576
  3.1 1.0 %select_convert_fusion = bf16[1024,128]{1,0:T(8,128)(2,1)S(1)} fusion(s32[1024]{0:T(1024)} %bitcast.77, s32[1024]{0:T(1024)} %bitcast.78, pred[128]{0:T(512)(128)(4,1)S(1)} %get-tuple-element.24, pred[128]{0:T(512)(128)(4,1)S(1)} %get-tuple-element.25), kind=kLoop, calls=%fused_computation.20 | loop fusion | flops 393216 | bytes 270592 | tf_op jit(solution)/shard_map/convert_element_type | solution.py:72
  4.2 2.3 %fusion.6 = bf16[2048,384]{1,0:T(8,128)(2,1)S(1)} fusion(s32[1024]{0:T(1024)S(1)} %multiply_add_fusion.1, bf16[1024,128]{1,0:T(8,128)(2,1)S(1)} %select_convert_fusion, bf16[1024,256]{1,0:T(8,128)(2,1)S(1)} %bitcast.71), kind=kOutput, calls=%fused_computation.9 | convolution fusion | flops 1615069184 | bytes 2363392 | tf_op jit(solution)/shard_map/dot_general | solution.py:74
  8.5 0.8 concatenate.17
  9.8 1.5 %reduce = bf16[64,8320]{1,0:T(8,128)(2,1)S(1)} reduce(bf16[64,1,8320]{2,0,1:T(8,128)(2,1)S(1)} %bitcast.59, bf16[]{:T(256)} %broadcast.106), dimensions={1}, to_apply=%copy.43.reduce_sub_computation | reduce | bytes 2129922 | tf_op jit(solution)/shard_map/all_to_all | solution.py:82
  11.3 1.6 %reshape.195 = bf16[64,2,4160]{2,1,0:T(2,128)(2,1)} reshape(bf16[64,8320]{1,0:T(8,128)(2,1)S(1)} %reduce) | data formatting | bytes 2129920
  12.9 13.0 %all-to-all-start = ((bf16[64,2,4160]{2,1,0:T(2,128)(2,1)}), bf16[64,2,4160]{2,1,0:T(2,128)(2,1)S(1)}, u32[]{:S(2)}, u32[]{:S(2)}) async-start(bf16[64,2,4160]{2,1,0:T(2,128)(2,1)} %reshape.195), calls=%async_computation | async-start | bytes 2162688 | tf_op jit(solution)/shard_map/all_to_all | solution.py:82
  26.1 28.4 %all-to-all-done = bf16[64,2,4160]{2,1,0:T(2,128)(2,1)S(1)} async-done(((bf16[64,2,4160]{2,1,0:T(2,128)(2,1)}), bf16[64,2,4160]{2,1,0:T(2,128)(2,1)S(1)}, u32[]{:S(2)}, u32[]{:S(2)}) %all-to-all-start) | async-done | bytes 1064992 | tf_op jit(solution)/shard_map/all_to_all | solution.py:82
  54.5 1.2 %reshape.196 = bf16[64,1,8320]{2,1,0:T(2,128)(2,1)S(1)} reshape(bf16[64,2,4160]{2,1,0:T(2,128)(2,1)S(1)} %all-to-all-done) | data formatting | bytes 2129920
  57.2 0.8 fusion.3
  58.4 3.4 %collective-permute-start = (f32[1,32,2,128]{3,1,2,0:T(8,128)S(1)}, f32[1,32,2,128]{3,1,2,0:T(8,128)S(1)}, u32[]{:S(2)}, u32[]{:S(2)}) collective-permute-start(f32[1,32,2,128]{3,1,2,0:T(8,128)S(1)} %copy.46), channel_id=1, source_target_pairs={{1,0},{2,1},{3,2},{4,3},{5,4},{6,5},{7,6},{8,7},{9,8},{10,9},{11,1... | collective-permute-start | bytes 98312 | tf_op jit(solution)/shard_map/ppermute | solution.py:15
  61.8 1.9 %collective-permute-start.1 = (f32[1,32,2,128]{3,1,2,0:T(8,128)S(1)}, f32[1,32,2,128]{3,1,2,0:T(8,128)S(1)}, u32[]{:S(2)}, u32[]{:S(2)}) collective-permute-start(f32[1,32,2,128]{3,1,2,0:T(8,128)S(1)} %copy.48), channel_id=1, source_target_pairs={{0,1},{1,2},{2,3},{3,4},{4,5},{5,6},{6,7},{7,8},{8,9},{9,10},{10,1... | collective-permute-start | bytes 98312 | tf_op jit(solution)/shard_map/ppermute | solution.py:12
  64.5 4.7 %collective-permute-done.1 = f32[1,32,2,128]{3,1,2,0:T(8,128)S(1)} collective-permute-done((f32[1,32,2,128]{3,1,2,0:T(8,128)S(1)}, f32[1,32,2,128]{3,1,2,0:T(8,128)S(1)}, u32[]{:S(2)}, u32[]{:S(2)}) %collective-permute-start.1) | collective-permute-done | bytes 32800 | tf_op jit(solution)/shard_map/ppermute | solution.py:12
  69.3 1.9 %fusion.29 = f32[2,32,128]{2,1,0:T(8,128)S(1)} fusion(f32[2,32,2,128]{3,1,2,0:T(8,128)S(1)} %get-tuple-element.12, f32[2,32,2,128]{3,1,2,0:T(8,128)S(1)} %get-tuple-element.13, f32[2,32,2,128]{3,1,2,0:T(8,128)S(1)} %get-tuple-element.11, f32[2,32,2,128]{3,1,2,0:T(8,128)S(1)} %bitcast.66, f32[]{:T(128)} %bitcast.21, f32[]{:T(128)} %bitcast.20, f32[]{:T(128)} %bitcast.17), kind=kLoop, calls=%fused_computation.49 | loop fusion | flops 114688 | bytes 294924 | tf_op jit(solution)/shard_map/add | solution.py:35
  71.3 2.6 %collective-permute-start.2 = (f32[3,2,32,128]{3,2,1,0:T(8,128)S(1)}, f32[3,2,32,128]{3,2,1,0:T(8,128)S(1)}, u32[]{:S(2)}, u32[]{:S(2)}) collective-permute-start(f32[3,2,32,128]{3,2,1,0:T(8,128)S(1)} %broadcast_multiply_fusion), channel_id=1, source_target_pairs={{0,64},{64,0},{128,192},{192,128},{256,320},{320,256},{384,448},{4... | collective-permute-start | bytes 294920 | tf_op jit(solution)/shard_map/ppermute | solution.py:43
  73.8 3.9 %collective-permute-done.2 = f32[3,2,32,128]{3,2,1,0:T(8,128)S(1)} collective-permute-done((f32[3,2,32,128]{3,2,1,0:T(8,128)S(1)}, f32[3,2,32,128]{3,2,1,0:T(8,128)S(1)}, u32[]{:S(2)}, u32[]{:S(2)}) %collective-permute-start.2) | collective-permute-done | bytes 98336 | tf_op jit(solution)/shard_map/ppermute | solution.py:43
  77.9 2.7 %collective-permute-start.3 = (f32[3,2,32,128]{3,2,1,0:T(8,128)S(1)}, f32[3,2,32,128]{3,2,1,0:T(8,128)S(1)}, u32[]{:S(2)}, u32[]{:S(2)}) collective-permute-start(f32[3,2,32,128]{3,2,1,0:T(8,128)S(1)} %fusion.37), channel_id=1, source_target_pairs={{0,128},{64,192},{128,0},{192,64},{256,384},{320,448},{384,256},{4... | collective-permute-start | bytes 294920 | tf_op jit(solution)/shard_map/ppermute | solution.py:43
  80.6 6.8 %collective-permute-done.3 = f32[3,2,32,128]{3,2,1,0:T(8,128)S(1)} collective-permute-done((f32[3,2,32,128]{3,2,1,0:T(8,128)S(1)}, f32[3,2,32,128]{3,2,1,0:T(8,128)S(1)}, u32[]{:S(2)}, u32[]{:S(2)}) %collective-permute-start.3) | collective-permute-done | bytes 98336 | tf_op jit(solution)/shard_map/ppermute | solution.py:43
  87.5 1.9 %collective-permute-start.4 = (f32[3,2,32,128]{3,2,1,0:T(8,128)S(1)}, f32[3,2,32,128]{3,2,1,0:T(8,128)S(1)}, u32[]{:S(2)}, u32[]{:S(2)}) collective-permute-start(f32[3,2,32,128]{3,2,1,0:T(8,128)S(1)} %fusion.46), channel_id=1, source_target_pairs={{0,256},{64,320},{128,384},{192,448},{256,0},{320,64},{384,128},{4... | collective-permute-start | bytes 294920 | tf_op jit(solution)/shard_map/ppermute | solution.py:43
  90.0 7.8 %collective-permute-done.4 = f32[3,2,32,128]{3,2,1,0:T(8,128)S(1)} collective-permute-done((f32[3,2,32,128]{3,2,1,0:T(8,128)S(1)}, f32[3,2,32,128]{3,2,1,0:T(8,128)S(1)}, u32[]{:S(2)}, u32[]{:S(2)}) %collective-permute-start.4) | collective-permute-done | bytes 98336 | tf_op jit(solution)/shard_map/ppermute | solution.py:43
  97.9 1.9 %fusion.36 = (f32[2,32,1,128]{3,1,2,0:T(8,128)S(1)}, f32[2,32,1,128]{3,1,2,0:T(8,128)S(1)}) fusion(f32[2,32,2,128]{3,1,2,0:T(8,128)S(1)} %copy.45, f32[2,32,2,128]{3,1,2,0:T(8,128)S(1)} %bitcast.67, f32[3,2,32,128]{3,2,1,0:T(8,128)S(1)} %add.90, f32[]{:T(128)} %bitcast.24, f32[]{:T(128)} %bitcast.23, f32[]{:T(128)} %bitcast.16), kind=kLoop, calls=%fused_computation.62 | loop fusion | flops 73728 | bytes 262156 | tf_op jit(solution)/shard_map/sub | solution.py:120
  99.8 0.7 copy.53
  (40 shorter events, 6.3 us)
Async XLA Ops:
  0.0 58.0 %copy-start = (bf16[8,128,128]{2,1,0:T(8,128)(2,1)S(1)}, bf16[8,128,128]{2,1,0:T(8,128)(2,1)}, u32[]{:S(2)}) copy-start(bf16[8,128,128]{2,1,0:T(8,128)(2,1)} %param.11) | copy-start | bytes 786436
  11.2 14.6 %copy-start.2 = (f32[8,3]{0,1:T(4,128)S(1)}, f32[8,3]{0,1:T(4,128)}, u32[]{:S(2)}) copy-start(f32[8,3]{0,1:T(4,128)} %param.12) | copy-start | bytes 292
  12.9 41.6 %all-to-all-start = ((bf16[64,2,4160]{2,1,0:T(2,128)(2,1)}), bf16[64,2,4160]{2,1,0:T(2,128)(2,1)S(1)}, u32[]{:S(2)}, u32[]{:S(2)}) async-start(bf16[64,2,4160]{2,1,0:T(2,128)(2,1)} %reshape.195), calls=%async_computation | async-start | bytes 2162688 | tf_op jit(solution)/shard_map/all_to_all | solution.py:82
  57.2 7.2 %copy-start.1 = (f32[1,2,32,2,128]{4,3,2,1,0:T(2,128)S(1)}, f32[1,2,32,2,128]{4,3,2,1,0:T(2,128)}, u32[]{:S(2)}) copy-start(f32[1,2,32,2,128]{4,3,2,1,0:T(2,128)} %param.13) | copy-start | bytes 196612
  58.4 6.0 %collective-permute-start = (f32[1,32,2,128]{3,1,2,0:T(8,128)S(1)}, f32[1,32,2,128]{3,1,2,0:T(8,128)S(1)}, u32[]{:S(2)}, u32[]{:S(2)}) collective-permute-start(f32[1,32,2,128]{3,1,2,0:T(8,128)S(1)} %copy.46), channel_id=1, source_target_pairs={{1,0},{2,1},{3,2},{4,3},{5,4},{6,5},{7,6},{8,7},{9,8},{10,9},{11,1... | collective-permute-start | bytes 98312 | tf_op jit(solution)/shard_map/ppermute | solution.py:15
  61.8 7.3 %collective-permute-start.1 = (f32[1,32,2,128]{3,1,2,0:T(8,128)S(1)}, f32[1,32,2,128]{3,1,2,0:T(8,128)S(1)}, u32[]{:S(2)}, u32[]{:S(2)}) collective-permute-start(f32[1,32,2,128]{3,1,2,0:T(8,128)S(1)} %copy.48), channel_id=1, source_target_pairs={{0,1},{1,2},{2,3},{3,4},{4,5},{5,6},{6,7},{7,8},{8,9},{9,10},{10,1... | collective-permute-start | bytes 98312 | tf_op jit(solution)/shard_map/ppermute | solution.py:12
  71.3 6.5 %collective-permute-start.2 = (f32[3,2,32,128]{3,2,1,0:T(8,128)S(1)}, f32[3,2,32,128]{3,2,1,0:T(8,128)S(1)}, u32[]{:S(2)}, u32[]{:S(2)}) collective-permute-start(f32[3,2,32,128]{3,2,1,0:T(8,128)S(1)} %broadcast_multiply_fusion), channel_id=1, source_target_pairs={{0,64},{64,0},{128,192},{192,128},{256,320},{320,256},{384,448},{4... | collective-permute-start | bytes 294920 | tf_op jit(solution)/shard_map/ppermute | solution.py:43
  77.9 9.5 %collective-permute-start.3 = (f32[3,2,32,128]{3,2,1,0:T(8,128)S(1)}, f32[3,2,32,128]{3,2,1,0:T(8,128)S(1)}, u32[]{:S(2)}, u32[]{:S(2)}) collective-permute-start(f32[3,2,32,128]{3,2,1,0:T(8,128)S(1)} %fusion.37), channel_id=1, source_target_pairs={{0,128},{64,192},{128,0},{192,64},{256,384},{320,448},{384,256},{4... | collective-permute-start | bytes 294920 | tf_op jit(solution)/shard_map/ppermute | solution.py:43
  87.5 10.4 %collective-permute-start.4 = (f32[3,2,32,128]{3,2,1,0:T(8,128)S(1)}, f32[3,2,32,128]{3,2,1,0:T(8,128)S(1)}, u32[]{:S(2)}, u32[]{:S(2)}) collective-permute-start(f32[3,2,32,128]{3,2,1,0:T(8,128)S(1)} %fusion.46), channel_id=1, source_target_pairs={{0,256},{64,320},{128,384},{192,448},{256,0},{320,64},{384,128},{4... | collective-permute-start | bytes 294920 | tf_op jit(solution)/shard_map/ppermute | solution.py:43

commit v2 on v1

--- a/solution.py
+++ b/solution.py
@@ -1,7 +1,11 @@
 import jax
 import jax.numpy as jnp
 from jax import lax
+from jax.experimental import pallas as pl
+from jax.experimental.pallas import tpu as pltpu
 from jax.sharding import PartitionSpec as P
+
+MESH = pl.DeviceIdType.MESH
 
 
 def extended(block, sides, width):
@@ -35,14 +39,52 @@
     return qrow[0] * term_x + qrow[1] * term_y + qrow[2] * term_z
 
 
-def butterfly_sum(value, axis):
-    count = lax.axis_size(axis)
-    distance = 1
-    while distance < count:
-        pairs = [(i, i ^ distance) for i in range(count)]
-        value = value + lax.ppermute(value, axis, pairs)
-        distance *= 2
-    return value
+def gather_kernel(phase_ref, out_ref, send_sem, recv_sem):
+    count = out_ref.shape[0]
+    me = lax.axis_index("refl")
+    slab = lax.axis_index("slab")
+    barrier = pltpu.get_barrier_semaphore()
+    for step in range(1, count):
+        peer = lax.rem(me + step, count)
+        pl.semaphore_signal(barrier, 1, device_id=(peer, slab), device_id_type=MESH)
+    pl.semaphore_wait(barrier, count - 1)
+    copies = []
+    for step in range(1, count):
+        peer = lax.rem(me + step, count)
+        copy = pltpu.make_async_remote_copy(
+            src_ref=phase_ref,
+            dst_ref=out_ref.at[me],
+            send_sem=send_sem.at[step],
+            recv_sem=recv_sem.at[step],
+            device_id=(peer, slab),
+            device_id_type=MESH,
+        )
+        copy.start()
+        copies.append(copy)
+    out_ref[me] = phase_ref[...]
+    for copy in copies:
+        copy.wait_send()
+    for step in range(1, count):
+        source = lax.rem(me + count - step, count)
+        pltpu.make_async_remote_copy(
+            src_ref=phase_ref,
+            dst_ref=out_ref.at[source],
+            send_sem=send_sem.at[step],
+            recv_sem=recv_sem.at[step],
+            device_id=(source, slab),
+            device_id_type=MESH,
+        ).wait_recv()
+
+
+def gather_refl(phase, count):
+    return pl.pallas_call(
+        gather_kernel,
+        out_shape=jax.ShapeDtypeStruct((count,) + phase.shape, phase.dtype),
+        in_specs=[pl.BlockSpec(memory_space=pltpu.VMEM)],
+        out_specs=pl.BlockSpec(memory_space=pltpu.VMEM),
+        scratch_shapes=[pltpu.SemaphoreType.DMA((count,)), pltpu.SemaphoreType.DMA((count,))],
+        compiler_params=pltpu.CompilerParams(collective_id=0, has_side_effects=True),
+    )(phase)
 
 
 def per_device(detector, owners, block_ids, kernel_ids, kernels, bragg_vectors, object_field):
@@ -115,8 +157,9 @@
     obj_imag = obj[:, :, 1]
     phase = phase_term(obj_real, obj_imag, grad_x, grad_y, grad_z, q_self)
     diff = q_self - q_other
-    total = butterfly_sum(q_self[:, None, None, None] * phase[None], "refl")
-    shift = diff[0] * total[0] + diff[1] * total[1] + diff[2] * total[2]
+    gathered = gather_refl(phase.reshape(plane_count * row_count, tile_width), refl_count)
+    weights = jnp.sum(bragg_vectors * diff[None, :], axis=1)
+    shift = jnp.sum(weights[:, None, None] * gathered, axis=0).reshape(plane_count, row_count, tile_width)
     new_real = obj_real - 0.5 * (gridded[:, :, 0] - obj_imag * shift)
     new_imag = obj_imag - 0.5 * (gridded[:, :, 1] + obj_real * shift)
     return jnp.stack([new_real, new_imag], axis=2)[None]

time: 101 us -> 87.2 us (0.86)
  the two profiles are of different devices: /device:TPU:96 before, /device:TPU:7 now
where the time goes in v2:
time: 87.2 us; the launch traced here: 85.7 us
  waiting for transfers between devices  27.7 us (32%)
  starting transfers between devices  21.8 us (25%)
  Pallas kernels  13.9 us (16%)
  local copies, waits for them, and re-layouts  9.9 us (11%)
  other arithmetic  8.49 us (10%)
  matrix products  3.54 us (4%)
    all_to_all x1, waiting for transfers between devices, per_device(): lax.all_to_all(packet, 'slab', split_axis=0, concat_axis=0, tiled=True)  27.4 us
    all_to_all x1, starting transfers between devices, per_device(): lax.all_to_all(packet, 'slab', split_axis=0, concat_axis=0, tiled=True)  14.1 us
    pallas_call x1, Pallas kernels, gather_refl(): pl.pallas_call(gather_kernel, out_shape=jax.ShapeDtypeStruct((count,) + p...  13.9 us
    unnamed x12, local copies, waits for them, and re-layouts  4.69 us
    ppermute x1, starting transfers between devices, extended(): lax.ppermute(lax.slice_in_dim(block, 0, width, axis=dim), axis, backward)  4.12 us
    ppermute x1, starting transfers between devices, extended(): lax.ppermute(lax.slice_in_dim(block, block.shape[dim] - width, None, axis...  3.55 us
    add x1, other arithmetic, phase_term(): return qrow[0] * term_x + qrow[1] * term_y + qrow[2] * term_z  2.52 us
    dot_general x1, matrix products, per_device(): sent = jnp.dot(placed, table, preferred_element_type=jnp.float32)  2.34 us
  transfers between devices with their start and end apart: 3, of which 2 were waited for; matrix products, arithmetic and copies ran while one was open for 1% of the time, Pallas kernels for 0%

profile of v2, /device:TPU:7, one launch (start us, length us, event | category | flops | bytes accessed | tf_op | source)
XLA Modules:
  0.0 85.7 jit_solution(8794420886828135709)
XLA Ops:
  0.0 1.3 %convert_reduce_fusion = s32[1024]{0:T(1024)S(1)} fusion(s32[1024]{0:T(1024)} %bitcast.74), kind=kLoop, calls=%fused_computation.3 | loop fusion | flops 5241856 | bytes 8192 | tf_op jit(solution)/shard_map/reduce_sum | solution.py:106
  1.3 0.7 multiply_add_fusion.1
  2.0 1.1 %copy.71 = bf16[128,8,2,128]{3,1,2,0:T(8,128)(2,1)S(1)} copy(bf16[128,8,2,128]{3,2,1,0:T(2,128)(2,1)} %bitcast.63) | data formatting | bytes 1048576
  3.1 1.0 %select_convert_fusion = bf16[1024,128]{1,0:T(8,128)(2,1)S(1)} fusion(s32[1024]{0:T(1024)} %bitcast.72, s32[1024]{0:T(1024)} %bitcast.73, pred[128]{0:T(512)(128)(4,1)S(1)} %get-tuple-element.21, pred[128]{0:T(512)(128)(4,1)S(1)} %get-tuple-element.22), kind=kLoop, calls=%fused_computation.20 | loop fusion | flops 393216 | bytes 270592 | tf_op jit(solution)/shard_map/convert_element_type | solution.py:114
  4.2 2.3 %fusion.6 = bf16[2048,384]{1,0:T(8,128)(2,1)S(1)} fusion(s32[1024]{0:T(1024)S(1)} %multiply_add_fusion.1, bf16[1024,128]{1,0:T(8,128)(2,1)S(1)} %select_convert_fusion, bf16[1024,256]{1,0:T(8,128)(2,1)S(1)} %bitcast.64), kind=kOutput, calls=%fused_computation.9 | convolution fusion | flops 1615069184 | bytes 2363392 | tf_op jit(solution)/shard_map/dot_general | solution.py:116
  6.9 0.5 copy.58
  7.8 0.6 copy.61
  8.5 0.8 concatenate.17
  9.3 0.5 broadcast.67
  9.8 1.5 %reduce = bf16[64,8320]{1,0:T(8,128)(2,1)S(1)} reduce(bf16[64,1,8320]{2,0,1:T(8,128)(2,1)S(1)} %bitcast.53, bf16[]{:T(256)} %broadcast.67), dimensions={1}, to_apply=%copy.43.reduce_sub_computation | reduce | bytes 2129922 | tf_op jit(solution)/shard_map/all_to_all | solution.py:124
  11.3 1.6 %reshape.110 = bf16[64,2,4160]{2,1,0:T(2,128)(2,1)} reshape(bf16[64,8320]{1,0:T(8,128)(2,1)S(1)} %reduce) | data formatting | bytes 2129920
  12.9 14.1 %all-to-all-start = ((bf16[64,2,4160]{2,1,0:T(2,128)(2,1)}), bf16[64,2,4160]{2,1,0:T(2,128)(2,1)S(1)}, u32[]{:S(2)}, u32[]{:S(2)}) async-start(bf16[64,2,4160]{2,1,0:T(2,128)(2,1)} %reshape.110), calls=%async_computation | async-start | bytes 2162688 | tf_op jit(solution)/shard_map/all_to_all | solution.py:124
  27.3 27.4 %all-to-all-done = bf16[64,2,4160]{2,1,0:T(2,128)(2,1)S(1)} async-done(((bf16[64,2,4160]{2,1,0:T(2,128)(2,1)}), bf16[64,2,4160]{2,1,0:T(2,128)(2,1)S(1)}, u32[]{:S(2)}, u32[]{:S(2)}) %all-to-all-start) | async-done | bytes 1064992 | tf_op jit(solution)/shard_map/all_to_all | solution.py:124
  54.7 1.2 %reshape.111 = bf16[64,1,8320]{2,1,0:T(2,128)(2,1)S(1)} reshape(bf16[64,2,4160]{2,1,0:T(2,128)(2,1)S(1)} %all-to-all-done) | data formatting | bytes 2129920
  56.1 0.5 reshape.101
  56.7 0.6 copy.44
  57.4 0.8 fusion.3
  58.6 4.1 %collective-permute-start = (f32[1,32,2,128]{3,1,2,0:T(8,128)S(1)}, f32[1,32,2,128]{3,1,2,0:T(8,128)S(1)}, u32[]{:S(2)}, u32[]{:S(2)}) collective-permute-start(f32[1,32,2,128]{3,1,2,0:T(8,128)S(1)} %copy.46), channel_id=1, source_target_pairs={{1,0},{2,1},{3,2},{4,3},{5,4},{6,5},{7,6},{8,7},{9,8},{10,9},{11,1... | collective-permute-start | bytes 98312 | tf_op jit(solution)/shard_map/ppermute | solution.py:19
  62.8 3.5 %collective-permute-start.1 = (f32[1,32,2,128]{3,1,2,0:T(8,128)S(1)}, f32[1,32,2,128]{3,1,2,0:T(8,128)S(1)}, u32[]{:S(2)}, u32[]{:S(2)}) collective-permute-start(f32[1,32,2,128]{3,1,2,0:T(8,128)S(1)} %copy.48), channel_id=1, source_target_pairs={{0,1},{1,2},{2,3},{3,4},{4,5},{5,6},{6,7},{7,8},{8,9},{9,10},{10,1... | collective-permute-start | bytes 98312 | tf_op jit(solution)/shard_map/ppermute | solution.py:16
  66.3 0.6 fusion.36
  67.4 2.5 %fusion.25 = f32[2,32,1,128]{3,1,2,0:T(8,128)} fusion(f32[2,32,2,128]{3,1,2,0:T(8,128)S(1)} %get-tuple-element.12, f32[2,32,2,128]{3,1,2,0:T(8,128)S(1)} %get-tuple-element.13, f32[2,32,2,128]{3,1,2,0:T(8,128)S(1)} %get-tuple-element.11, f32[2,32,2,128]{3,1,2,0:T(8,128)S(1)} %bitcast.60, f32[]{:T(128)} %bitcast.20, f32[]{:T(128)} %bitcast.19, f32[]{:T(128)} %bitcast.16), kind=kLoop, calls=%fused_computation.42 | loop fusion | flops 114688 | bytes 294924 | tf_op jit(solution)/shard_map/add | solution.py:39
  70.0 13.9 %shard_map.73 = f32[8,64,128]{2,1,0:T(8,128)} custom-call(f32[64,128]{1,0:T(8,128)} %bitcast.66), custom_call_target="tpu_custom_call" | custom-call | tf_op jit(solution)/shard_map/pallas_call | solution.py:80
  83.9 1.0 %multiply_reduce_fusion = f32[64,128]{1,0:T(8,128)S(1)} fusion(f32[8,64,128]{2,1,0:T(8,128)} %shard_map.73, f32[8]{0:T(128)S(1)} %multiply_reduce_fusion.1), kind=kLoop, calls=%fused_computation.21 | loop fusion | flops 122880 | bytes 294944 | tf_op jit(solution)/shard_map/reduce_sum | solution.py:162
  85.0 0.7 copy.53
  (31 shorter events, 2.4 us)
Async XLA Ops:
  0.0 58.2 %copy-start = (bf16[8,128,128]{2,1,0:T(8,128)(2,1)S(1)}, bf16[8,128,128]{2,1,0:T(8,128)(2,1)}, u32[]{:S(2)}) copy-start(bf16[8,128,128]{2,1,0:T(8,128)(2,1)} %param.11) | copy-start | bytes 786436
  11.2 15.8 %copy-start.2 = (f32[8,3]{0,1:T(4,128)S(1)}, f32[8,3]{0,1:T(4,128)}, u32[]{:S(2)}) copy-start(f32[8,3]{0,1:T(4,128)} %param.12) | copy-start | bytes 292
  12.9 41.8 %all-to-all-start = ((bf16[64,2,4160]{2,1,0:T(2,128)(2,1)}), bf16[64,2,4160]{2,1,0:T(2,128)(2,1)S(1)}, u32[]{:S(2)}, u32[]{:S(2)}) async-start(bf16[64,2,4160]{2,1,0:T(2,128)(2,1)} %reshape.110), calls=%async_computation | async-start | bytes 2162688 | tf_op jit(solution)/shard_map/all_to_all | solution.py:124
  57.4 9.6 %copy-start.1 = (f32[1,2,32,2,128]{4,3,2,1,0:T(2,128)S(1)}, f32[1,2,32,2,128]{4,3,2,1,0:T(2,128)}, u32[]{:S(2)}) copy-start(f32[1,2,32,2,128]{4,3,2,1,0:T(2,128)} %param.13) | copy-start | bytes 196612
  58.6 8.3 %collective-permute-start = (f32[1,32,2,128]{3,1,2,0:T(8,128)S(1)}, f32[1,32,2,128]{3,1,2,0:T(8,128)S(1)}, u32[]{:S(2)}, u32[]{:S(2)}) collective-permute-start(f32[1,32,2,128]{3,1,2,0:T(8,128)S(1)} %copy.46), channel_id=1, source_target_pairs={{1,0},{2,1},{3,2},{4,3},{5,4},{6,5},{7,6},{8,7},{9,8},{10,9},{11,1... | collective-permute-start | bytes 98312 | tf_op jit(solution)/shard_map/ppermute | solution.py:19
  62.8 4.6 %collective-permute-start.1 = (f32[1,32,2,128]{3,1,2,0:T(8,128)S(1)}, f32[1,32,2,128]{3,1,2,0:T(8,128)S(1)}, u32[]{:S(2)}, u32[]{:S(2)}) collective-permute-start(f32[1,32,2,128]{3,1,2,0:T(8,128)S(1)} %copy.48), channel_id=1, source_target_pairs={{0,1},{1,2},{2,3},{3,4},{4,5},{5,6},{6,7},{7,8},{8,9},{9,10},{10,1... | collective-permute-start | bytes 98312 | tf_op jit(solution)/shard_map/ppermute | solution.py:16

commit v3 on v2

--- a/solution.py
+++ b/solution.py
@@ -85,6 +85,69 @@
         scratch_shapes=[pltpu.SemaphoreType.DMA((count,)), pltpu.SemaphoreType.DMA((count,))],
         compiler_params=pltpu.CompilerParams(collective_id=0, has_side_effects=True),
     )(phase)
+
+
+def exchange_kernel(packet_ref, out_ref, send_sem, recv_sem):
+    count = packet_ref.shape[0]
+    me = lax.axis_index("slab")
+    refl = lax.axis_index("refl")
+    barrier = pltpu.get_barrier_semaphore()
+
+    def greet(step, carry):
+        peer = lax.rem(me + step, count)
+        pl.semaphore_signal(barrier, 1, device_id=(refl, peer), device_id_type=MESH)
+        return carry
+
+    lax.fori_loop(1, count, greet, 0)
+    pl.semaphore_wait(barrier, count - 1)
+
+    def outgoing(step):
+        peer = lax.rem(me + step, count)
+        return pltpu.make_async_remote_copy(
+            src_ref=packet_ref.at[peer],
+            dst_ref=out_ref.at[me],
+            send_sem=send_sem.at[step],
+            recv_sem=recv_sem.at[step],
+            device_id=(refl, peer),
+            device_id_type=MESH,
+        )
+
+    def incoming(step):
+        source = lax.rem(me + count - step, count)
+        return pltpu.make_async_remote_copy(
+            src_ref=packet_ref.at[source],
+            dst_ref=out_ref.at[source],
+            send_sem=send_sem.at[step],
+            recv_sem=recv_sem.at[step],
+            device_id=(refl, source),
+            device_id_type=MESH,
+        )
+
+    def send(step, carry):
+        outgoing(step).start()
+        return carry
+
+    lax.fori_loop(1, count, send, 0)
+    out_ref[me] = packet_ref[me]
+
+    def finish(step, carry):
+        outgoing(step).wait_send()
+        incoming(step).wait_recv()
+        return carry
+
+    lax.fori_loop(1, count, finish, 0)
+
+
+def exchange_slab(packet):
+    count = packet.shape[0]
+    return pl.pallas_call(
+        exchange_kernel,
+        out_shape=jax.ShapeDtypeStruct(packet.shape, packet.dtype),
+        in_specs=[pl.BlockSpec(memory_space=pltpu.VMEM)],
+        out_specs=pl.BlockSpec(memory_space=pltpu.VMEM),
+        scratch_shapes=[pltpu.SemaphoreType.DMA((count,)), pltpu.SemaphoreType.DMA((count,))],
+        compiler_params=pltpu.CompilerParams(collective_id=1, has_side_effects=True),
+    )(packet)
 
 
 def per_device(detector, owners, block_ids, kernel_ids, kernels, bragg_vectors, object_field):
@@ -115,19 +178,18 @@
     table = jnp.concatenate([values, extra], axis=1)
     sent = jnp.dot(placed, table, preferred_element_type=jnp.float32)
     sent = sent.reshape(slab_count, capacity, row_width + 128)
-    data = sent[:, :, :row_width].astype(jnp.bfloat16).reshape(slab_count, capacity * row_width)
+    data = sent[:, :, :row_width].astype(jnp.bfloat16).reshape(slab_count, 2 * capacity, tile_width)
     code_rows = jnp.concatenate(
-        [sent[:, :, row_width], sent[:, :, row_width + 1], jnp.zeros((slab_count, 128 - 2 * capacity), jnp.float32)],
+        [sent[:, :, row_width], sent[:, :, row_width + 1], jnp.zeros((slab_count, tile_width - 2 * capacity), jnp.float32)],
         axis=1,
     ).astype(jnp.bfloat16)
-    packet = jnp.concatenate([data, code_rows], axis=1)
-    got = lax.all_to_all(packet, "slab", split_axis=0, concat_axis=0, tiled=True)
+    code_pad = jnp.zeros((slab_count, 15, tile_width), jnp.bfloat16)
+    packet = jnp.concatenate([data, code_rows[:, None, :], code_pad], axis=1)
+    got = exchange_slab(packet)
     row_total = slab_count * capacity
-    rows = got[:, : capacity * row_width].reshape(row_total, row_width)
-    got_blocks = got[:, capacity * row_width : capacity * row_width + capacity].astype(jnp.int32)
-    got_kernels = got[
-        :, capacity * row_width + capacity : capacity * row_width + 2 * capacity
-    ].astype(jnp.int32)
+    rows = got[:, : 2 * capacity].reshape(row_total, row_width)
+    got_blocks = got[:, 2 * capacity, :capacity].astype(jnp.int32)
+    got_kernels = got[:, 2 * capacity, capacity : 2 * capacity].astype(jnp.int32)
     got_codes = (got_blocks * kernel_count + got_kernels).reshape(row_total)
     chosen = (
         got_codes[None, :]

time: 87.2 us -> 90.8 us (1.041); the launches traced: 85.7 us -> 90.3 us
  Pallas kernels: 13.9 us -> 61.3 us
  waiting for transfers between devices: 27.7 us -> 4 us
  starting transfers between devices: 21.8 us -> 4.33 us
  local copies, waits for them, and re-layouts: 9.9 us -> 7.26 us
  other arithmetic: 8.49 us -> 9.6 us
    pallas_call x0 -> x1, Pallas kernels: none -> 47.8 us  [exchange_slab(): pl.pallas_call(exchange_kernel, out_shape=jax.ShapeDtypeStruct(packet.sha...]
    all_to_all x1 -> x0, waiting for transfers between devices: 27.4 us -> none  [per_device(): lax.all_to_all(packet, 'slab', split_axis=0, concat_axis=0, tiled=True)]
    all_to_all x1 -> x0, starting transfers between devices: 14.1 us -> none  [per_device(): lax.all_to_all(packet, 'slab', split_axis=0, concat_axis=0, tiled=True)]
    ppermute x1, waiting for transfers between devices: 0.01 us -> 4 us  [extended(): lax.ppermute(lax.slice_in_dim(block, 0, width, axis=dim), axis, backward)]
    unnamed x12 -> x8, local copies, waits for them, and re-layouts: 4.69 us -> 1.14 us
    slice x1 -> x3, local copies, waits for them, and re-layouts: 0.07 us -> 2.17 us  [the longest x1 1.3 us: per_device(): rows = got[:, :2 * capacity].reshape(row_total, row_width)]
    ppermute x1, starting transfers between devices: 4.12 us -> 2.41 us  [extended(): lax.ppermute(lax.slice_in_dim(block, 0, width, axis=dim), axis, backward)]
    ppermute x1, starting transfers between devices: 3.55 us -> 1.92 us  [extended(): lax.ppermute(lax.slice_in_dim(block, block.shape[dim] - width, None, axis...]
  transfers between devices with their start and end apart: 3 -> 2, of which waited for: 2 -> 1; matrix products, arithmetic and copies ran while one was open for 1% -> 1% of each run, Pallas kernels for 0% -> 0%
where the time goes in v3:
time: 90.8 us; the launch traced here: 90.3 us
  Pallas kernels  61.3 us (68%)
  other arithmetic  9.6 us (11%)
  local copies, waits for them, and re-layouts  7.26 us (8%)
  starting transfers between devices  4.33 us (5%)
  waiting for transfers between devices  4 us (4%)
  matrix products  3.54 us (4%)
    pallas_call x1, Pallas kernels, exchange_slab(): pl.pallas_call(exchange_kernel, out_shape=jax.ShapeDtypeStruct(packet.sha...  47.8 us
    pallas_call x1, Pallas kernels, gather_refl(): pl.pallas_call(gather_kernel, out_shape=jax.ShapeDtypeStruct((count,) + p...  13.5 us
    ppermute x1, waiting for transfers between devices, extended(): lax.ppermute(lax.slice_in_dim(block, 0, width, axis=dim), axis, backward)  4 us
    add x1, other arithmetic, phase_term(): return qrow[0] * term_x + qrow[1] * term_y + qrow[2] * term_z  2.52 us
    ppermute x1, starting transfers between devices, extended(): lax.ppermute(lax.slice_in_dim(block, 0, width, axis=dim), axis, backward)  2.41 us
    dot_general x1, matrix products, per_device(): sent = jnp.dot(placed, table, preferred_element_type=jnp.float32)  2.34 us
    ppermute x1, starting transfers between devices, extended(): lax.ppermute(lax.slice_in_dim(block, block.shape[dim] - width, None, axis...  1.92 us
  transfers between devices with their start and end apart: 2, of which 1 were waited for; matrix products, arithmetic and copies ran while one was open for 1% of the time, Pallas kernels for 0%

profile of v3, /device:TPU:7, one launch (start us, length us, event | category | flops | bytes accessed | tf_op | source)
XLA Modules:
  0.0 90.3 jit_solution(425348519529792224)
XLA Ops:
  0.0 1.3 %convert_reduce_fusion = s32[1024]{0:T(1024)S(1)} fusion(s32[1024]{0:T(1024)} %bitcast.61), kind=kLoop, calls=%fused_computation.3 | loop fusion | flops 5241856 | bytes 8192 | tf_op jit(solution)/shard_map/reduce_sum | solution.py:169
  1.3 0.7 multiply_add_fusion.1
  2.0 1.1 %copy.56 = bf16[128,8,2,128]{3,1,2,0:T(8,128)(2,1)S(1)} copy(bf16[128,8,2,128]{3,2,1,0:T(2,128)(2,1)} %bitcast.50) | data formatting | bytes 1048576
  3.1 1.0 %select_convert_fusion = bf16[1024,128]{1,0:T(8,128)(2,1)S(1)} fusion(s32[1024]{0:T(1024)} %bitcast.59, s32[1024]{0:T(1024)} %bitcast.60, pred[128]{0:T(512)(128)(4,1)S(1)} %get-tuple-element.21, pred[128]{0:T(512)(128)(4,1)S(1)} %get-tuple-element.22), kind=kLoop, calls=%fused_computation.20 | loop fusion | flops 393216 | bytes 270592 | tf_op jit(solution)/shard_map/convert_element_type | solution.py:177
  4.2 2.3 %fusion.6 = bf16[2048,384]{1,0:T(8,128)(2,1)S(1)} fusion(s32[1024]{0:T(1024)S(1)} %multiply_add_fusion.1, bf16[1024,128]{1,0:T(8,128)(2,1)S(1)} %select_convert_fusion, bf16[1024,256]{1,0:T(8,128)(2,1)S(1)} %bitcast.51), kind=kOutput, calls=%fused_computation.9 | convolution fusion | flops 1615069184 | bytes 2363392 | tf_op jit(solution)/shard_map/dot_general | solution.py:179
  6.9 0.6 copy.34
  7.7 0.6 copy.33
  8.4 0.4 reshape.154
  9.0 1.5 %maximum_maximum_fusion.packet_ref = bf16[64,80,128]{2,1,0:T(8,128)(2,1)} fusion(bf16[64,1,32]{2,1,0:T(2,128)(2,1)S(1)} %copy.36, bf16[64,1,32]{2,1,0:T(2,128)(2,1)S(1)} %copy.35, bf16[64,64,128]{2,1,0:T(8,128)(2,1)S(1)} %reshape.154, bf16[80]{0:T(256)(128)(2,1)S(1)} %pad.20.clone, bf16[80,128]{1,0:T(8,128)(2,1)S(1)} %pad.19.clone), kind=kLoop, calls=%fused_computation.12 | loop fusion | flops 6553600 | bytes 2388128 | tf_op jit(solution)/shard_map/concatenate | solution.py:187
  10.4 47.8 %shard_map.73 = bf16[64,80,128]{2,1,0:T(8,128)(2,1)} custom-call(bf16[64,80,128]{2,1,0:T(8,128)(2,1)} %maximum_maximum_fusion.packet_ref), custom_call_target="tpu_custom_call" | custom-call | tf_op jit(solution)/shard_map/pallas_call | solution.py:143
  58.3 1.3 %slice.98 = bf16[64,64,128]{2,1,0:T(8,128)(2,1)S(1)} slice(bf16[64,80,128]{2,1,0:T(8,128)(2,1)} %shard_map.73), slice={[0:64], [0:64], [0:128]} | slice | bytes 2097152 | tf_op jit(solution)/shard_map/slice | solution.py:190
  59.6 1.2 %add_reduce_fusion = s32[64,32]{1,0:T(8,128)S(1)} fusion(bf16[64,80,128]{2,1,0:T(8,128)(2,1)} %shard_map.73), kind=kLoop, calls=%fused_computation.57 | loop fusion | flops 8192 | bytes 16384 | tf_op jit(solution)/shard_map/add | solution.py:193
  60.7 0.4 reshape.155
  61.1 0.6 copy.37
  61.9 0.8 fusion.3
  62.7 0.4 fusion.12
  63.1 1.9 %collective-permute-start.1 = (f32[1,32,2,128]{3,1,2,0:T(8,128)S(1)}, f32[1,32,2,128]{3,1,2,0:T(8,128)S(1)}, u32[]{:S(2)}, u32[]{:S(2)}) collective-permute-start(f32[1,32,2,128]{3,1,2,0:T(8,128)S(1)} %copy.41), channel_id=1, source_target_pairs={{0,1},{1,2},{2,3},{3,4},{4,5},{5,6},{6,7},{7,8},{8,9},{9,10},{10,1... | collective-permute-start | bytes 98312 | tf_op jit(solution)/shard_map/ppermute | solution.py:16
  65.1 2.4 %collective-permute-start = (f32[1,32,2,128]{3,1,2,0:T(8,128)S(1)}, f32[1,32,2,128]{3,1,2,0:T(8,128)S(1)}, u32[]{:S(2)}, u32[]{:S(2)}) collective-permute-start(f32[1,32,2,128]{3,1,2,0:T(8,128)S(1)} %copy.39), channel_id=1, source_target_pairs={{1,0},{2,1},{3,2},{4,3},{5,4},{6,5},{7,6},{8,7},{9,8},{10,9},{11,1... | collective-permute-start | bytes 98312 | tf_op jit(solution)/shard_map/ppermute | solution.py:19
  67.8 0.6 fusion.36
  68.4 4.0 %collective-permute-done = f32[1,32,2,128]{3,1,2,0:T(8,128)S(1)} collective-permute-done((f32[1,32,2,128]{3,1,2,0:T(8,128)S(1)}, f32[1,32,2,128]{3,1,2,0:T(8,128)S(1)}, u32[]{:S(2)}, u32[]{:S(2)}) %collective-permute-start) | collective-permute-done | bytes 32800 | tf_op jit(solution)/shard_map/ppermute | solution.py:19
  72.5 2.5 %fusion.25 = f32[2,32,1,128]{3,1,2,0:T(8,128)} fusion(f32[2,32,2,128]{3,1,2,0:T(8,128)S(1)} %get-tuple-element.12, f32[2,32,2,128]{3,1,2,0:T(8,128)S(1)} %get-tuple-element.13, f32[2,32,2,128]{3,1,2,0:T(8,128)S(1)} %get-tuple-element.11, f32[2,32,2,128]{3,1,2,0:T(8,128)S(1)} %bitcast.47, f32[]{:T(128)} %bitcast.19, f32[]{:T(128)} %bitcast.18, f32[]{:T(128)} %bitcast.15), kind=kLoop, calls=%fused_computation.42 | loop fusion | flops 114688 | bytes 294924 | tf_op jit(solution)/shard_map/add | solution.py:39
  75.0 13.5 %shard_map.74 = f32[8,64,128]{2,1,0:T(8,128)} custom-call(f32[64,128]{1,0:T(8,128)} %bitcast.53), custom_call_target="tpu_custom_call" | custom-call | tf_op jit(solution)/shard_map/pallas_call | solution.py:80
  88.6 1.0 %multiply_reduce_fusion = f32[64,128]{1,0:T(8,128)S(1)} fusion(f32[8,64,128]{2,1,0:T(8,128)} %shard_map.74, f32[8]{0:T(128)S(1)} %multiply_reduce_fusion.1), kind=kLoop, calls=%fused_computation.21 | loop fusion | flops 122880 | bytes 294944 | tf_op jit(solution)/shard_map/reduce_sum | solution.py:224
  89.6 0.7 copy.46
  (30 shorter events, 1.2 us)
Async XLA Ops:
  0.0 62.7 %copy-start = (bf16[8,128,128]{2,1,0:T(8,128)(2,1)S(1)}, bf16[8,128,128]{2,1,0:T(8,128)(2,1)}, u32[]{:S(2)}) copy-start(bf16[8,128,128]{2,1,0:T(8,128)(2,1)} %param.11) | copy-start | bytes 786436
  61.9 5.6 %copy-start.2 = (f32[8,3]{0,1:T(4,128)S(1)}, f32[8,3]{0,1:T(4,128)}, u32[]{:S(2)}) copy-start(f32[8,3]{0,1:T(4,128)} %param.12) | copy-start | bytes 292
  61.9 6.5 %copy-start.1 = (f32[1,2,32,2,128]{4,3,2,1,0:T(2,128)S(1)}, f32[1,2,32,2,128]{4,3,2,1,0:T(2,128)}, u32[]{:S(2)}) copy-start(f32[1,2,32,2,128]{4,3,2,1,0:T(2,128)} %param.13) | copy-start | bytes 196612
  63.1 5.3 %collective-permute-start.1 = (f32[1,32,2,128]{3,1,2,0:T(8,128)S(1)}, f32[1,32,2,128]{3,1,2,0:T(8,128)S(1)}, u32[]{:S(2)}, u32[]{:S(2)}) collective-permute-start(f32[1,32,2,128]{3,1,2,0:T(8,128)S(1)} %copy.41), channel_id=1, source_target_pairs={{0,1},{1,2},{2,3},{3,4},{4,5},{5,6},{6,7},{7,8},{8,9},{9,10},{10,1... | collective-permute-start | bytes 98312 | tf_op jit(solution)/shard_map/ppermute | solution.py:16
  65.1 7.3 %collective-permute-start = (f32[1,32,2,128]{3,1,2,0:T(8,128)S(1)}, f32[1,32,2,128]{3,1,2,0:T(8,128)S(1)}, u32[]{:S(2)}, u32[]{:S(2)}) collective-permute-start(f32[1,32,2,128]{3,1,2,0:T(8,128)S(1)} %copy.39), channel_id=1, source_target_pairs={{1,0},{2,1},{3,2},{4,3},{5,4},{6,5},{7,6},{8,7},{9,8},{10,9},{11,1... | collective-permute-start | bytes 98312 | tf_op jit(solution)/shard_map/ppermute | solution.py:19

commit v4 on v2

--- a/solution.py
+++ b/solution.py
@@ -87,6 +87,121 @@
     )(phase)
 
 
+def exchange_kernel(
+    slot_ref, values_ref, ids_ref, data_out, code_out,
+    data_buf, code_buf, data_send, data_recv, code_send, code_recv,
+):
+    count, capacity = data_out.shape[0], data_out.shape[1]
+    group = 8 if count >= 16 else count // 2
+    groups = count // group
+    rows = group * capacity
+    me = lax.axis_index("slab")
+    refl = lax.axis_index("refl")
+    barrier = pltpu.get_barrier_semaphore()
+
+    def greet(step, carry):
+        peer = lax.rem(me + step, count)
+        pl.semaphore_signal(barrier, 1, device_id=(refl, peer), device_id_type=MESH)
+        return carry
+
+    lax.fori_loop(1, count, greet, 0)
+
+    def pack(g):
+        target = lax.broadcasted_iota(jnp.int32, (rows, slot_ref.shape[1]), 0) + g * rows
+        chosen = (slot_ref[...] == target).astype(jnp.bfloat16)
+        sent = jnp.dot(chosen, values_ref[...], preferred_element_type=jnp.float32)
+        data_buf[pl.ds(g * group, group)] = sent.astype(jnp.bfloat16).reshape(
+            group, capacity, sent.shape[1]
+        )
+        codes = lax.dot_general(
+            ids_ref[...], chosen, (((1,), (1,)), ((), ())), preferred_element_type=jnp.float32
+        ).astype(jnp.bfloat16)
+        for part in range(group):
+            window = (part * capacity) // 128
+            code_buf[g * group + part] = codes[:, window * 128 : (window + 1) * 128]
+
+    def outgoing(d):
+        data = pltpu.make_async_remote_copy(
+            src_ref=data_buf.at[d], dst_ref=data_out.at[me], send_sem=data_send.at[d],
+            recv_sem=data_recv.at[me], device_id=(refl, d), device_id_type=MESH,
+        )
+        code = pltpu.make_async_remote_copy(
+            src_ref=code_buf.at[d], dst_ref=code_out.at[me], send_sem=code_send.at[d],
+            recv_sem=code_recv.at[me], device_id=(refl, d), device_id_type=MESH,
+        )
+        return data, code
+
+    def incoming(s):
+        data = pltpu.make_async_remote_copy(
+            src_ref=data_buf.at[s], dst_ref=data_out.at[s], send_sem=data_send.at[s],
+            recv_sem=data_recv.at[s], device_id=(refl, s), device_id_type=MESH,
+        )
+        code = pltpu.make_async_remote_copy(
+            src_ref=code_buf.at[s], dst_ref=code_out.at[s], send_sem=code_send.at[s],
+            recv_sem=code_recv.at[s], device_id=(refl, s), device_id_type=MESH,
+        )
+        return data, code
+
+    def send(g):
+        for part in range(group):
+            d = g * group + part
+
+            @pl.when(d != me)
+            def _():
+                data, code = outgoing(d)
+                data.start()
+                code.start()
+
+    home = me // group
+    pack(home)
+    pl.semaphore_wait(barrier, count - 1)
+    send(home)
+
+    def later(j, carry):
+        g = lax.rem(home + j, groups)
+        pack(g)
+        send(g)
+        return carry
+
+    lax.fori_loop(1, groups, later, 0)
+    data_out[me] = data_buf[me]
+    code_out[me] = code_buf[me]
+
+    def finish(step, carry):
+        data, code = outgoing(lax.rem(me + step, count))
+        data.wait_send()
+        code.wait_send()
+        data, code = incoming(lax.rem(me + count - step, count))
+        data.wait_recv()
+        code.wait_recv()
+        return carry
+
+    lax.fori_loop(1, count, finish, 0)
+
+
+def exchange_slab(flat_slot, values, ids, count, capacity):
+    data_shape = (count, capacity, values.shape[1])
+    code_shape = (count, ids.shape[0], 128)
+    return pl.pallas_call(
+        exchange_kernel,
+        out_shape=(
+            jax.ShapeDtypeStruct(data_shape, jnp.bfloat16),
+            jax.ShapeDtypeStruct(code_shape, jnp.bfloat16),
+        ),
+        in_specs=[pl.BlockSpec(memory_space=pltpu.VMEM)] * 3,
+        out_specs=(pl.BlockSpec(memory_space=pltpu.VMEM), pl.BlockSpec(memory_space=pltpu.VMEM)),
+        scratch_shapes=[
+            pltpu.VMEM(data_shape, jnp.bfloat16),
+            pltpu.VMEM(code_shape, jnp.bfloat16),
+            pltpu.SemaphoreType.DMA((count,)),
+            pltpu.SemaphoreType.DMA((count,)),
+            pltpu.SemaphoreType.DMA((count,)),
+            pltpu.SemaphoreType.DMA((count,)),
+        ],
+        compiler_params=pltpu.CompilerParams(collective_id=1, has_side_effects=True),
+    )(flat_slot, values, ids)
+
+
 def per_device(detector, owners, block_ids, kernel_ids, kernels, bragg_vectors, object_field):
     slab_count = lax.axis_size("slab")
     plane_count = object_field.shape[1]
@@ -105,29 +220,15 @@
     same = (owner[:, None] == owner[None, :]) & order
     slots = jnp.sum(same.astype(jnp.int32), axis=1)
     flat_slot = owner * capacity + slots
-    placed = (
-        flat_slot[None, :] == lax.broadcasted_iota(jnp.int32, (slab_count * capacity, tile_count), 0)
+    ids = jnp.concatenate(
+        [block_ids, kernel_ids, jnp.zeros((14, tile_count), jnp.int32)], axis=0
     ).astype(jnp.bfloat16)
-    lane = lax.broadcasted_iota(jnp.int32, (tile_count, 128), 1)
-    extra = jnp.where(
-        lane == 0, block_ids[0][:, None], jnp.where(lane == 1, kernel_ids[0][:, None], 0)
-    ).astype(jnp.bfloat16)
-    table = jnp.concatenate([values, extra], axis=1)
-    sent = jnp.dot(placed, table, preferred_element_type=jnp.float32)
-    sent = sent.reshape(slab_count, capacity, row_width + 128)
-    data = sent[:, :, :row_width].astype(jnp.bfloat16).reshape(slab_count, capacity * row_width)
-    code_rows = jnp.concatenate(
-        [sent[:, :, row_width], sent[:, :, row_width + 1], jnp.zeros((slab_count, 128 - 2 * capacity), jnp.float32)],
-        axis=1,
-    ).astype(jnp.bfloat16)
-    packet = jnp.concatenate([data, code_rows], axis=1)
-    got = lax.all_to_all(packet, "slab", split_axis=0, concat_axis=0, tiled=True)
+    got, got_code = exchange_slab(flat_slot[None, :], values, ids, slab_count, capacity)
     row_total = slab_count * capacity
-    rows = got[:, : capacity * row_width].reshape(row_total, row_width)
-    got_blocks = got[:, capacity * row_width : capacity * row_width + capacity].astype(jnp.int32)
-    got_kernels = got[
-        :, capacity * row_width + capacity : capacity * row_width + 2 * capacity
-    ].astype(jnp.int32)
+    rows = got.reshape(row_total, row_width)
+    offset = lax.rem(lax.axis_index("slab"), 4) * capacity
+    got_blocks = lax.dynamic_slice_in_dim(got_code[:, 0, :], offset, capacity, axis=1).astype(jnp.int32)
+    got_kernels = lax.dynamic_slice_in_dim(got_code[:, 1, :], offset, capacity, axis=1).astype(jnp.int32)
     got_codes = (got_blocks * kernel_count + got_kernels).reshape(row_total)
     chosen = (
         got_codes[None, :]

time: 87.2 us -> 86.9 us (level)
  Pallas kernels: 13.9 us -> 64.7 us
  waiting for transfers between devices: 27.7 us -> 0.07 us
  starting transfers between devices: 21.8 us -> 7.67 us
  local copies, waits for them, and re-layouts: 9.9 us -> 6.02 us
  other arithmetic: 8.49 us -> 5.98 us
  matrix products: 3.54 us -> 1.2 us
    pallas_call x0 -> x1, Pallas kernels: none -> 50.4 us  [exchange_slab(): pl.pallas_call(exchange_kernel, out_shape=(jax.ShapeDtypeStruct(data_shap...]
    all_to_all x1 -> x0, waiting for transfers between devices: 27.4 us -> none  [per_device(): lax.all_to_all(packet, 'slab', split_axis=0, concat_axis=0, tiled=True)]
    all_to_all x1 -> x0, starting transfers between devices: 14.1 us -> none  [per_device(): lax.all_to_all(packet, 'slab', split_axis=0, concat_axis=0, tiled=True)]
    unnamed x12 -> x14, local copies, waits for them, and re-layouts: 4.69 us -> 2.02 us
    dot_general x1 -> x0, matrix products: 2.34 us -> none  [per_device(): sent = jnp.dot(placed, table, preferred_element_type=jnp.float32)]
    ppermute x1, starting transfers between devices: 4.12 us -> 2.38 us  [extended(): lax.ppermute(lax.slice_in_dim(block, 0, width, axis=dim), axis, backward)]
    ppermute x1, starting transfers between devices: 3.55 us -> 5.29 us  [extended(): lax.ppermute(lax.slice_in_dim(block, block.shape[dim] - width, None, axis...]
    all_to_all x1 -> x0, other arithmetic: 1.45 us -> none  [per_device(): lax.all_to_all(packet, 'slab', split_axis=0, concat_axis=0, tiled=True)]
  transfers between devices with their start and end apart: 3 -> 2, of which waited for: 2 -> 1; matrix products, arithmetic and copies ran while one was open for 1% -> 1% of each run, Pallas kernels for 0% -> 0%
where the time goes in v4:
time: 86.9 us; the launch traced here: 85.9 us
  Pallas kernels  64.7 us (74%)
  starting transfers between devices  7.67 us (9%)
  local copies, waits for them, and re-layouts  6.02 us (7%)
  other arithmetic  5.98 us (7%)
  matrix products  1.2 us (1%)
    pallas_call x1, Pallas kernels, exchange_slab(): pl.pallas_call(exchange_kernel, out_shape=(jax.ShapeDtypeStruct(data_shap...  50.4 us
    pallas_call x1, Pallas kernels, gather_refl(): pl.pallas_call(gather_kernel, out_shape=jax.ShapeDtypeStruct((count,) + p...  14.3 us
    ppermute x1, starting transfers between devices, extended(): lax.ppermute(lax.slice_in_dim(block, block.shape[dim] - width, None, axis...  5.29 us
    add x1, other arithmetic, phase_term(): return qrow[0] * term_x + qrow[1] * term_y + qrow[2] * term_z  2.52 us
    ppermute x1, starting transfers between devices, extended(): lax.ppermute(lax.slice_in_dim(block, 0, width, axis=dim), axis, backward)  2.38 us
    unnamed x14, local copies, waits for them, and re-layouts  2.02 us
  transfers between devices with their start and end apart: 2, of which 1 were waited for; matrix products, arithmetic and copies ran while one was open for 1% of the time, Pallas kernels for 0%

profile of v4, /device:TPU:7, one launch (start us, length us, event | category | flops | bytes accessed | tf_op | source)
XLA Modules:
  0.0 85.9 jit_solution(1801762784221709270)
XLA Ops:
  0.0 2.0 %copy.34 = bf16[128,8,2,128]{3,1,2,0:T(8,128)(2,1)} copy(bf16[128,8,2,128]{3,2,1,0:T(2,128)(2,1)} %bitcast.49) | data formatting | bytes 1048576
  2.1 0.5 convert_reduce_fusion
  2.6 0.6 bitcast_add_fusion.slot_ref
  3.2 0.1 pad.18.clone
  3.3 0.7 maximum_maximum_fusion.ids_ref
  4.0 50.4 %shard_map.73 = (bf16[64,32,256]{2,1,0:T(8,128)(2,1)}, bf16[64,16,128]{2,1,0:T(8,128)(2,1)}) custom-call(s32[1,1024]{1,0:T(1,128)} %bitcast_add_fusion.slot_ref, bf16[1024,256]{1,0:T(8,128)(2,1)} %bitcast.43, bf16[16,1024]{1,0:T(8,128)(2,1)} %maximum_maximum_fusion.ids_ref), custom_call_target="tpu_custom_call" | custom-call | tf_op jit(solution)/shard_map/pallas_call | solution.py:185
  54.4 1.0 %fusion.27 = (bf16[64,1,128]{2,1,0:T(2,128)(2,1)S(1)}, bf16[64,1,128]{2,1,0:T(2,128)(2,1)S(1)}) fusion(bf16[64,16,128]{2,1,0:T(8,128)(2,1)} %get-tuple-element.7), kind=kLoop, calls=%fused_computation.56 | loop fusion | bytes 65536 | tf_op jit(solution)/shard_map/slice | solution.py:230
  55.4 0.2 add_reduce_fusion
  55.6 0.1 add.57
  55.7 1.5 %copy.15 = bf16[256,2048]{1,0:T(8,128)(2,1)S(1)} copy(bf16[256,2048]{0,1:T(8,128)(2,1)} %bitcast.44) | data formatting | bytes 2097152 | tf_op jit(solution)/shard_map/dot_general | solution.py:237
  57.2 0.8 fusion.1
  58.0 0.0 copy-start.2
  58.0 0.4 fusion.6
  58.5 2.4 %collective-permute-start = (f32[1,32,2,128]{3,1,2,0:T(8,128)S(1)}, f32[1,32,2,128]{3,1,2,0:T(8,128)S(1)}, u32[]{:S(2)}, u32[]{:S(2)}) collective-permute-start(f32[1,32,2,128]{3,1,2,0:T(8,128)S(1)} %copy.17), channel_id=1, source_target_pairs={{1,0},{2,1},{3,2},{4,3},{5,4},{6,5},{7,6},{8,7},{9,8},{10,9},{11,1... | collective-permute-start | bytes 98312 | tf_op jit(solution)/shard_map/ppermute | solution.py:19
  60.9 5.3 %collective-permute-start.1 = (f32[1,32,2,128]{3,1,2,0:T(8,128)S(1)}, f32[1,32,2,128]{3,1,2,0:T(8,128)S(1)}, u32[]{:S(2)}, u32[]{:S(2)}) collective-permute-start(f32[1,32,2,128]{3,1,2,0:T(8,128)S(1)} %copy.19), channel_id=1, source_target_pairs={{0,1},{1,2},{2,3},{3,4},{4,5},{5,6},{6,7},{7,8},{8,9},{9,10},{10,1... | collective-permute-start | bytes 98312 | tf_op jit(solution)/shard_map/ppermute | solution.py:16
  66.2 0.1 select_reduce_fusion
  66.4 0.1 multiply_reduce_fusion.1
  66.5 0.6 fusion.29
  67.1 0.1 collective-permute-done.1
  67.2 0.1 fusion.14
  67.3 2.5 %fusion.19 = f32[2,32,1,128]{3,1,2,0:T(8,128)} fusion(f32[2,32,2,128]{3,1,2,0:T(8,128)S(1)} %get-tuple-element.16, f32[2,32,2,128]{3,1,2,0:T(8,128)S(1)} %get-tuple-element.17, f32[2,32,2,128]{3,1,2,0:T(8,128)S(1)} %get-tuple-element.15, f32[2,32,2,128]{3,1,2,0:T(8,128)S(1)} %bitcast.46, f32[]{:T(128)} %bitcast.17, f32[]{:T(128)} %bitcast.16, f32[]{:T(128)} %bitcast.13), kind=kLoop, calls=%fused_computation.33 | loop fusion | flops 114688 | bytes 294924 | tf_op jit(solution)/shard_map/add | solution.py:39
  69.8 14.3 %shard_map.74 = f32[8,64,128]{2,1,0:T(8,128)} custom-call(f32[64,128]{1,0:T(8,128)} %bitcast.51), custom_call_target="tpu_custom_call" | custom-call | tf_op jit(solution)/shard_map/pallas_call | solution.py:80
  84.1 1.0 %multiply_reduce_fusion = f32[64,128]{1,0:T(8,128)S(1)} fusion(f32[8,64,128]{2,1,0:T(8,128)} %shard_map.74, f32[8]{0:T(128)S(1)} %multiply_reduce_fusion.1), kind=kLoop, calls=%fused_computation.12 | loop fusion | flops 122880 | bytes 294944 | tf_op jit(solution)/shard_map/reduce_sum | solution.py:263
  85.2 0.7 copy.24
  (25 shorter events, 0.1 us)
Async XLA Ops:
  0.0 58.0 %copy-start = (bf16[8,128,128]{2,1,0:T(8,128)(2,1)S(1)}, bf16[8,128,128]{2,1,0:T(8,128)(2,1)}, u32[]{:S(2)}) copy-start(bf16[8,128,128]{2,1,0:T(8,128)(2,1)} %param.11) | copy-start | bytes 786436
  0.0 2.0 %copy-start.4 = (s32[1,1024]{1,0:T(1,128)S(1)}, s32[1,1024]{1,0:T(1,128)}, u32[]{:S(2)}) copy-start(s32[1,1024]{1,0:T(1,128)} %param.9) | copy-start | bytes 12292
  0.0 2.0 %copy-start.5 = (s32[1,1024]{1,0:T(1,128)S(1)}, s32[1,1024]{1,0:T(1,128)}, u32[]{:S(2)}) copy-start(s32[1,1024]{1,0:T(1,128)} %param.10) | copy-start | bytes 12292
  0.0 2.1 %copy-start.3 = (s32[1,1024,1]{1,2,0:T(1,128)S(1)}, s32[1,1024,1]{1,2,0:T(1,128)}, u32[]{:S(2)}) copy-start(s32[1,1024,1]{1,2,0:T(1,128)} %param.8) | copy-start | bytes 12292
  58.0 8.2 %copy-start.2 = (f32[8,3]{0,1:T(4,128)S(1)}, f32[8,3]{0,1:T(4,128)}, u32[]{:S(2)}) copy-start(f32[8,3]{0,1:T(4,128)} %param.12) | copy-start | bytes 292
  58.0 9.1 %copy-start.1 = (f32[1,2,32,2,128]{4,3,2,1,0:T(2,128)S(1)}, f32[1,2,32,2,128]{4,3,2,1,0:T(2,128)}, u32[]{:S(2)}) copy-start(f32[1,2,32,2,128]{4,3,2,1,0:T(2,128)} %param.13) | copy-start | bytes 196612
  58.5 8.6 %collective-permute-start = (f32[1,32,2,128]{3,1,2,0:T(8,128)S(1)}, f32[1,32,2,128]{3,1,2,0:T(8,128)S(1)}, u32[]{:S(2)}, u32[]{:S(2)}) collective-permute-start(f32[1,32,2,128]{3,1,2,0:T(8,128)S(1)} %copy.17), channel_id=1, source_target_pairs={{1,0},{2,1},{3,2},{4,3},{5,4},{6,5},{7,6},{8,7},{9,8},{10,9},{11,1... | collective-permute-start | bytes 98312 | tf_op jit(solution)/shard_map/ppermute | solution.py:19
  60.9 6.3 %collective-permute-start.1 = (f32[1,32,2,128]{3,1,2,0:T(8,128)S(1)}, f32[1,32,2,128]{3,1,2,0:T(8,128)S(1)}, u32[]{:S(2)}, u32[]{:S(2)}) collective-permute-start(f32[1,32,2,128]{3,1,2,0:T(8,128)S(1)} %copy.19), channel_id=1, source_target_pairs={{0,1},{1,2},{2,3},{3,4},{4,5},{5,6},{6,7},{7,8},{8,9},{9,10},{10,1... | collective-permute-start | bytes 98312 | tf_op jit(solution)/shard_map/ppermute | solution.py:16

commit v5 on v4

--- a/solution.py
+++ b/solution.py
@@ -87,10 +87,7 @@
     )(phase)
 
 
-def exchange_kernel(
-    slot_ref, values_ref, ids_ref, data_out, code_out,
-    data_buf, code_buf, data_send, data_recv, code_send, code_recv,
-):
+def exchange_kernel(slot_ref, values_ref, data_out, data_buf, data_send, data_recv):
     count, capacity = data_out.shape[0], data_out.shape[1]
     group = 8 if count >= 16 else count // 2
     groups = count // group
@@ -113,34 +110,18 @@
         data_buf[pl.ds(g * group, group)] = sent.astype(jnp.bfloat16).reshape(
             group, capacity, sent.shape[1]
         )
-        codes = lax.dot_general(
-            ids_ref[...], chosen, (((1,), (1,)), ((), ())), preferred_element_type=jnp.float32
-        ).astype(jnp.bfloat16)
-        for part in range(group):
-            window = (part * capacity) // 128
-            code_buf[g * group + part] = codes[:, window * 128 : (window + 1) * 128]
 
     def outgoing(d):
-        data = pltpu.make_async_remote_copy(
+        return pltpu.make_async_remote_copy(
             src_ref=data_buf.at[d], dst_ref=data_out.at[me], send_sem=data_send.at[d],
             recv_sem=data_recv.at[me], device_id=(refl, d), device_id_type=MESH,
         )
-        code = pltpu.make_async_remote_copy(
-            src_ref=code_buf.at[d], dst_ref=code_out.at[me], send_sem=code_send.at[d],
-            recv_sem=code_recv.at[me], device_id=(refl, d), device_id_type=MESH,
-        )
-        return data, code
 
     def incoming(s):
-        data = pltpu.make_async_remote_copy(
+        return pltpu.make_async_remote_copy(
             src_ref=data_buf.at[s], dst_ref=data_out.at[s], send_sem=data_send.at[s],
             recv_sem=data_recv.at[s], device_id=(refl, s), device_id_type=MESH,
         )
-        code = pltpu.make_async_remote_copy(
-            src_ref=code_buf.at[s], dst_ref=code_out.at[s], send_sem=code_send.at[s],
-            recv_sem=code_recv.at[s], device_id=(refl, s), device_id_type=MESH,
-        )
-        return data, code
 
     def send(g):
         for part in range(group):
@@ -148,9 +129,7 @@
 
             @pl.when(d != me)
             def _():
-                data, code = outgoing(d)
-                data.start()
-                code.start()
+                outgoing(d).start()
 
     home = me // group
     pack(home)
@@ -165,41 +144,29 @@
 
     lax.fori_loop(1, groups, later, 0)
     data_out[me] = data_buf[me]
-    code_out[me] = code_buf[me]
 
     def finish(step, carry):
-        data, code = outgoing(lax.rem(me + step, count))
-        data.wait_send()
-        code.wait_send()
-        data, code = incoming(lax.rem(me + count - step, count))
-        data.wait_recv()
-        code.wait_recv()
+        outgoing(lax.rem(me + step, count)).wait_send()
+        incoming(lax.rem(me + count - step, count)).wait_recv()
         return carry
 
     lax.fori_loop(1, count, finish, 0)
 
 
-def exchange_slab(flat_slot, values, ids, count, capacity):
+def exchange_slab(flat_slot, values, count, capacity):
     data_shape = (count, capacity, values.shape[1])
-    code_shape = (count, ids.shape[0], 128)
     return pl.pallas_call(
         exchange_kernel,
-        out_shape=(
-            jax.ShapeDtypeStruct(data_shape, jnp.bfloat16),
-            jax.ShapeDtypeStruct(code_shape, jnp.bfloat16),
-        ),
-        in_specs=[pl.BlockSpec(memory_space=pltpu.VMEM)] * 3,
-        out_specs=(pl.BlockSpec(memory_space=pltpu.VMEM), pl.BlockSpec(memory_space=pltpu.VMEM)),
+        out_shape=jax.ShapeDtypeStruct(data_shape, jnp.bfloat16),
+        in_specs=[pl.BlockSpec(memory_space=pltpu.VMEM)] * 2,
+        out_specs=pl.BlockSpec(memory_space=pltpu.VMEM),
         scratch_shapes=[
             pltpu.VMEM(data_shape, jnp.bfloat16),
-            pltpu.VMEM(code_shape, jnp.bfloat16),
-            pltpu.SemaphoreType.DMA((count,)),
-            pltpu.SemaphoreType.DMA((count,)),
             pltpu.SemaphoreType.DMA((count,)),
             pltpu.SemaphoreType.DMA((count,)),
         ],
         compiler_params=pltpu.CompilerParams(collective_id=1, has_side_effects=True),
-    )(flat_slot, values, ids)
+    )(flat_slot, values)
 
 
 def per_device(detector, owners, block_ids, kernel_ids, kernels, bragg_vectors, object_field):
@@ -220,16 +187,14 @@
     same = (owner[:, None] == owner[None, :]) & order
     slots = jnp.sum(same.astype(jnp.int32), axis=1)
     flat_slot = owner * capacity + slots
-    ids = jnp.concatenate(
-        [block_ids, kernel_ids, jnp.zeros((14, tile_count), jnp.int32)], axis=0
-    ).astype(jnp.bfloat16)
-    got, got_code = exchange_slab(flat_slot[None, :], values, ids, slab_count, capacity)
+    codes = block_ids[0] * kernel_count + kernel_ids[0]
+    placed = flat_slot[None, :] == lax.broadcasted_iota(jnp.int32, (slab_count * capacity, tile_count), 0)
+    sent_codes = jnp.max(jnp.where(placed, codes[None, :], -1), axis=1).reshape(slab_count, capacity)
+    got_codes = lax.all_to_all(sent_codes, "slab", split_axis=0, concat_axis=0, tiled=True)
+    got = exchange_slab(flat_slot[None, :], values, slab_count, capacity)
     row_total = slab_count * capacity
     rows = got.reshape(row_total, row_width)
-    offset = lax.rem(lax.axis_index("slab"), 4) * capacity
-    got_blocks = lax.dynamic_slice_in_dim(got_code[:, 0, :], offset, capacity, axis=1).astype(jnp.int32)
-    got_kernels = lax.dynamic_slice_in_dim(got_code[:, 1, :], offset, capacity, axis=1).astype(jnp.int32)
-    got_codes = (got_blocks * kernel_count + got_kernels).reshape(row_total)
+    got_codes = jnp.maximum(got_codes, 0).reshape(row_total)
     chosen = (
         got_codes[None, :]
         == lax.broadcasted_iota(jnp.int32, (block_count * kernel_count, row_total), 0)

time: 86.9 us -> 91.9 us (1.058)
  Pallas kernels: 64.7 us -> 51.1 us
  starting transfers between devices: 7.67 us -> 18.5 us
  other arithmetic: 5.98 us -> 10.6 us
  waiting for transfers between devices: 0.07 us -> 4.28 us
    all_to_all x0 -> x1, starting transfers between devices: none -> 14.1 us  [per_device(): lax.all_to_all(sent_codes, 'slab', split_axis=0, concat_axis=0, tiled=True)]
    pallas_call x1, Pallas kernels: 50.4 us -> 37.6 us  [exchange_slab(): pl.pallas_call(exchange_kernel, out_shape=jax.ShapeDtypeStruct(data_shape...]
    ppermute x1, waiting for transfers between devices: 0.01 us -> 4.28 us  [extended(): lax.ppermute(lax.slice_in_dim(block, 0, width, axis=dim), axis, backward)]
    ppermute x1, starting transfers between devices: 5.29 us -> 1.92 us  [extended(): lax.ppermute(lax.slice_in_dim(block, block.shape[dim] - width, None, axis...]
    add x1 -> x2, other arithmetic: 0.6 us -> 1.98 us  [per_device(): flat_slot = owner * capacity + slots]
    reduce_max x0 -> x1, other arithmetic: none -> 1.19 us  [per_device(): jnp.max(jnp.where(placed, codes[None, :], -1), axis=1)]
    slice x1 -> x0, local copies, waits for them, and re-layouts: 1.04 us -> none  [per_device(): got_code[:, 0, :]]
    unnamed x14 -> x6, local copies, waits for them, and re-layouts: 2.02 us -> 1.96 us
  transfers between devices with their start and end apart: 2 -> 3, of which waited for: 1 -> 1; matrix products, arithmetic and copies ran while one was open for 1% -> 8% of each run, Pallas kernels for 0% -> 41%
where the time goes in v5:
time: 91.9 us; the launch traced here: 91.3 us
  Pallas kernels  51.1 us (56%)
  starting transfers between devices  18.5 us (20%)
  other arithmetic  10.6 us (12%)
  local copies, waits for them, and re-layouts  5.52 us (6%)
  waiting for transfers between devices  4.28 us (5%)
  matrix products  1.19 us (1%)
    pallas_call x1, Pallas kernels, exchange_slab(): pl.pallas_call(exchange_kernel, out_shape=jax.ShapeDtypeStruct(data_shape...  37.6 us
    all_to_all x1, starting transfers between devices, per_device(): lax.all_to_all(sent_codes, 'slab', split_axis=0, concat_axis=0, tiled=True)  14.1 us
    pallas_call x1, Pallas kernels, gather_refl(): pl.pallas_call(gather_kernel, out_shape=jax.ShapeDtypeStruct((count,) + p...  13.5 us
    ppermute x1, waiting for transfers between devices, extended(): lax.ppermute(lax.slice_in_dim(block, 0, width, axis=dim), axis, backward)  4.28 us
    add x1, other arithmetic, phase_term(): return qrow[0] * term_x + qrow[1] * term_y + qrow[2] * term_z  2.52 us
    ppermute x1, starting transfers between devices, extended(): lax.ppermute(lax.slice_in_dim(block, 0, width, axis=dim), axis, backward)  2.41 us
    add x2, other arithmetic, per_device(): flat_slot = owner * capacity + slots  1.98 us
    unnamed x6, local copies, waits for them, and re-layouts  1.96 us
  transfers between devices with their start and end apart: 3, of which 1 were waited for; matrix products, arithmetic and copies ran while one was open for 8% of the time, Pallas kernels for 41%

profile of v5, /device:TPU:7, one launch (start us, length us, event | category | flops | bytes accessed | tf_op | source)
XLA Modules:
  0.0 91.3 jit_solution(743183338581611732)
XLA Ops:
  0.0 1.3 %convert_reduce_fusion = s32[1024]{0:T(1024)S(1)} fusion(s32[1024]{0:T(1024)} %bitcast.57), kind=kLoop, calls=%fused_computation.2 | loop fusion | flops 5241856 | bytes 8192 | tf_op jit(solution)/shard_map/reduce_sum | solution.py:188
  1.3 0.7 multiply_add_fusion.2
  2.0 0.7 multiply_add_fusion.1
  2.7 1.2 %select_reduce_fusion = s32[2048]{0:T(1024)S(1)} fusion(s32[1024]{0:T(1024)S(1)} %bitcast.60, s32[1024]{0:T(1024)S(1)} %multiply_add_fusion.2), kind=kLoop, calls=%fused_computation | loop fusion | flops 6289408 | bytes 16384 | tf_op jit(solution)/shard_map/reduce_max | solution.py:192
  3.9 0.7 all_to_all.6
  4.6 14.1 %all-to-all-start = ((s32[64,1,32]{2,1,0:T(1,128)}), s32[64,1,32]{2,1,0:T(1,128)S(1)}, u32[]{:S(2)}, u32[]{:S(2)}) async-start(s32[64,1,32]{2,1,0:T(1,128)} %bitcast.3), calls=%async_computation | async-start | bytes 65536 | tf_op jit(solution)/shard_map/all_to_all | solution.py:193
  18.7 1.3 %bitcast_add_fusion.slot_ref = s32[1,1024]{1,0:T(1,128)} fusion(s32[1,1024]{1,0:T(1,128)S(1)} %bitcast.59, s32[1,1024,1]{1,2,0:T(1,128)} %param.8), kind=kLoop, calls=%fused_computation.51 | loop fusion | flops 2048 | bytes 12288 | tf_op jit(solution)/shard_map/add | solution.py:189
  20.0 0.8 select_reduce_fusion.1
  20.8 0.8 multiply_reduce_fusion.1
  21.6 1.9 %copy.39 = bf16[128,8,2,128]{3,1,2,0:T(8,128)(2,1)} copy(bf16[128,8,2,128]{3,2,1,0:T(2,128)(2,1)} %bitcast.51) | data formatting | bytes 1048576
  23.6 37.6 %shard_map.73 = bf16[64,32,256]{2,1,0:T(8,128)(2,1)} custom-call(s32[1,1024]{1,0:T(1,128)} %bitcast_add_fusion.slot_ref, bf16[1024,256]{1,0:T(8,128)(2,1)} %bitcast.46), custom_call_target="tpu_custom_call" | custom-call | tf_op jit(solution)/shard_map/pallas_call | solution.py:158
  61.2 1.5 %copy.20 = bf16[256,2048]{1,0:T(8,128)(2,1)S(1)} copy(bf16[256,2048]{0,1:T(8,128)(2,1)} %bitcast.45) | data formatting | bytes 2097152 | tf_op jit(solution)/shard_map/dot_general | solution.py:202
  62.7 0.1 maximum_reduce_fusion
  62.8 0.8 fusion.1
  63.6 0.4 fusion.6
  64.1 1.9 %collective-permute-start.1 = (f32[1,32,2,128]{3,1,2,0:T(8,128)S(1)}, f32[1,32,2,128]{3,1,2,0:T(8,128)S(1)}, u32[]{:S(2)}, u32[]{:S(2)}) collective-permute-start(f32[1,32,2,128]{3,1,2,0:T(8,128)S(1)} %copy.24), channel_id=1, source_target_pairs={{0,1},{1,2},{2,3},{3,4},{4,5},{5,6},{6,7},{7,8},{8,9},{9,10},{10,1... | collective-permute-start | bytes 98312 | tf_op jit(solution)/shard_map/ppermute | solution.py:16
  66.0 2.4 %collective-permute-start = (f32[1,32,2,128]{3,1,2,0:T(8,128)S(1)}, f32[1,32,2,128]{3,1,2,0:T(8,128)S(1)}, u32[]{:S(2)}, u32[]{:S(2)}) collective-permute-start(f32[1,32,2,128]{3,1,2,0:T(8,128)S(1)} %copy.22), channel_id=1, source_target_pairs={{1,0},{2,1},{3,2},{4,3},{5,4},{6,5},{7,6},{8,7},{9,8},{10,9},{11,1... | collective-permute-start | bytes 98312 | tf_op jit(solution)/shard_map/ppermute | solution.py:19
  68.4 0.6 fusion.28
  69.1 4.3 %collective-permute-done = f32[1,32,2,128]{3,1,2,0:T(8,128)S(1)} collective-permute-done((f32[1,32,2,128]{3,1,2,0:T(8,128)S(1)}, f32[1,32,2,128]{3,1,2,0:T(8,128)S(1)}, u32[]{:S(2)}, u32[]{:S(2)}) %collective-permute-start) | collective-permute-done | bytes 32800 | tf_op jit(solution)/shard_map/ppermute | solution.py:19
  73.4 0.1 fusion.14
  73.5 2.5 %fusion.19 = f32[2,32,1,128]{3,1,2,0:T(8,128)} fusion(f32[2,32,2,128]{3,1,2,0:T(8,128)S(1)} %get-tuple-element.10, f32[2,32,2,128]{3,1,2,0:T(8,128)S(1)} %get-tuple-element.11, f32[2,32,2,128]{3,1,2,0:T(8,128)S(1)} %get-tuple-element.9, f32[2,32,2,128]{3,1,2,0:T(8,128)S(1)} %bitcast.48, f32[]{:T(128)} %bitcast.19, f32[]{:T(128)} %bitcast.18, f32[]{:T(128)} %bitcast.15), kind=kLoop, calls=%fused_computation.35 | loop fusion | flops 114688 | bytes 294924 | tf_op jit(solution)/shard_map/add | solution.py:39
  76.0 13.5 %shard_map.74 = f32[8,64,128]{2,1,0:T(8,128)} custom-call(f32[64,128]{1,0:T(8,128)} %bitcast.53), custom_call_target="tpu_custom_call" | custom-call | tf_op jit(solution)/shard_map/pallas_call | solution.py:80
  89.5 1.0 %multiply_reduce_fusion = f32[64,128]{1,0:T(8,128)S(1)} fusion(f32[8,64,128]{2,1,0:T(8,128)} %shard_map.74, f32[8]{0:T(128)S(1)} %multiply_reduce_fusion.1), kind=kLoop, calls=%fused_computation.14 | loop fusion | flops 122880 | bytes 294944 | tf_op jit(solution)/shard_map/reduce_sum | solution.py:228
  90.6 0.7 copy.29
  (17 shorter events, 0.2 us)
Async XLA Ops:
  0.0 63.6 %copy-start = (bf16[8,128,128]{2,1,0:T(8,128)(2,1)S(1)}, bf16[8,128,128]{2,1,0:T(8,128)(2,1)}, u32[]{:S(2)}) copy-start(bf16[8,128,128]{2,1,0:T(8,128)(2,1)} %param.11) | copy-start | bytes 786436
  4.6 58.1 %all-to-all-start = ((s32[64,1,32]{2,1,0:T(1,128)}), s32[64,1,32]{2,1,0:T(1,128)S(1)}, u32[]{:S(2)}, u32[]{:S(2)}) async-start(s32[64,1,32]{2,1,0:T(1,128)} %bitcast.3), calls=%async_computation | async-start | bytes 65536 | tf_op jit(solution)/shard_map/all_to_all | solution.py:193
  63.6 5.4 %copy-start.1 = (f32[1,2,32,2,128]{4,3,2,1,0:T(2,128)S(1)}, f32[1,2,32,2,128]{4,3,2,1,0:T(2,128)}, u32[]{:S(2)}) copy-start(f32[1,2,32,2,128]{4,3,2,1,0:T(2,128)} %param.13) | copy-start | bytes 196612
  64.1 5.0 %collective-permute-start.1 = (f32[1,32,2,128]{3,1,2,0:T(8,128)S(1)}, f32[1,32,2,128]{3,1,2,0:T(8,128)S(1)}, u32[]{:S(2)}, u32[]{:S(2)}) collective-permute-start(f32[1,32,2,128]{3,1,2,0:T(8,128)S(1)} %copy.24), channel_id=1, source_target_pairs={{0,1},{1,2},{2,3},{3,4},{4,5},{5,6},{6,7},{7,8},{8,9},{9,10},{10,1... | collective-permute-start | bytes 98312 | tf_op jit(solution)/shard_map/ppermute | solution.py:16
  66.0 7.3 %collective-permute-start = (f32[1,32,2,128]{3,1,2,0:T(8,128)S(1)}, f32[1,32,2,128]{3,1,2,0:T(8,128)S(1)}, u32[]{:S(2)}, u32[]{:S(2)}) collective-permute-start(f32[1,32,2,128]{3,1,2,0:T(8,128)S(1)} %copy.22), channel_id=1, source_target_pairs={{1,0},{2,1},{3,2},{4,3},{5,4},{6,5},{7,6},{8,7},{9,8},{10,9},{11,1... | collective-permute-start | bytes 98312 | tf_op jit(solution)/shard_map/ppermute | solution.py:19

commit v6 on v4

--- a/solution.py
+++ b/solution.py
@@ -1,3 +1,5 @@
+import functools
+
 import jax
 import jax.numpy as jnp
 from jax import lax
@@ -39,52 +41,115 @@
     return qrow[0] * term_x + qrow[1] * term_y + qrow[2] * term_z
 
 
-def gather_kernel(phase_ref, out_ref, send_sem, recv_sem):
-    count = out_ref.shape[0]
-    me = lax.axis_index("refl")
-    slab = lax.axis_index("slab")
+def post_kernel(
+    scalars, grid_ref, obj_ref, out_ref, halo, gathered, phase_buf, halo_send, halo_recv, send_sem, recv_sem,
+    slab_count,
+):
+    refl_count = gathered.shape[0]
+    planes, rows, width = grid_ref.shape[0], grid_ref.shape[2], grid_ref.shape[3]
+    me = lax.axis_index("slab")
+    refl = lax.axis_index("refl")
+    up = lax.rem(me + 1, slab_count)
+    down = lax.rem(me + slab_count - 1, slab_count)
     barrier = pltpu.get_barrier_semaphore()
-    for step in range(1, count):
-        peer = lax.rem(me + step, count)
-        pl.semaphore_signal(barrier, 1, device_id=(peer, slab), device_id_type=MESH)
-    pl.semaphore_wait(barrier, count - 1)
+    pl.semaphore_signal(barrier, 1, device_id=(refl, up), device_id_type=MESH)
+    pl.semaphore_signal(barrier, 1, device_id=(refl, down), device_id_type=MESH)
+    for step in range(1, refl_count):
+        peer = lax.rem(refl + step, refl_count)
+        pl.semaphore_signal(barrier, 1, device_id=(peer, me), device_id_type=MESH)
+    pl.semaphore_wait(barrier, refl_count + 1)
+    low_copy = pltpu.make_async_remote_copy(
+        src_ref=grid_ref.at[planes - 1], dst_ref=halo.at[0], send_sem=halo_send.at[0],
+        recv_sem=halo_recv.at[0], device_id=(refl, up), device_id_type=MESH,
+    )
+    high_copy = pltpu.make_async_remote_copy(
+        src_ref=grid_ref.at[0], dst_ref=halo.at[1], send_sem=halo_send.at[1],
+        recv_sem=halo_recv.at[1], device_id=(refl, down), device_id_type=MESH,
+    )
+    low_copy.start()
+    high_copy.start()
+    row_of = lax.broadcasted_iota(jnp.int32, (rows, width), 0)
+    lane_of = lax.broadcasted_iota(jnp.int32, (rows, width), 1)
+
+    def along_y(field):
+        after = jnp.where(row_of == rows - 1, 0.0, pltpu.roll(field, rows - 1, 0))
+        before = jnp.where(row_of == 0, 0.0, pltpu.roll(field, 1, 0))
+        return 0.5 * (after - before)
+
+    def along_w(field):
+        after = jnp.where(lane_of == width - 1, 0.0, pltpu.roll(field, width - 1, 1))
+        before = jnp.where(lane_of == 0, 0.0, pltpu.roll(field, 1, 1))
+        return 0.5 * (after - before)
+
+    q0, q1, q2 = scalars[0], scalars[1], scalars[2]
+    partial = []
+    for p in range(planes):
+        obj_re, obj_im = obj_ref[p, 0], obj_ref[p, 1]
+        term_y = obj_re * along_y(grid_ref[p, 1]) - obj_im * along_y(grid_ref[p, 0])
+        term_z = obj_re * along_w(grid_ref[p, 1]) - obj_im * along_w(grid_ref[p, 0])
+        partial.append((term_y, term_z))
+    low_copy.wait_send()
+    high_copy.wait_send()
+    low_copy.wait_recv()
+    high_copy.wait_recv()
+    has_low = me > 0
+    has_high = me < slab_count - 1
+    for p in range(planes):
+        obj_re, obj_im = obj_ref[p, 0], obj_ref[p, 1]
+        grad = []
+        for c in range(2):
+            ahead = grid_ref[p + 1, c] if p + 1 < planes else jnp.where(has_high, halo[1, c], 0.0)
+            behind = grid_ref[p - 1, c] if p > 0 else jnp.where(has_low, halo[0, c], 0.0)
+            grad.append(0.5 * (ahead - behind))
+        term_x = obj_re * grad[1] - obj_im * grad[0]
+        term_y, term_z = partial[p]
+        phase_buf[p] = q0 * term_x + q1 * term_y + q2 * term_z
     copies = []
-    for step in range(1, count):
-        peer = lax.rem(me + step, count)
+    for step in range(1, refl_count):
+        peer = lax.rem(refl + step, refl_count)
         copy = pltpu.make_async_remote_copy(
-            src_ref=phase_ref,
-            dst_ref=out_ref.at[me],
-            send_sem=send_sem.at[step],
-            recv_sem=recv_sem.at[step],
-            device_id=(peer, slab),
-            device_id_type=MESH,
+            src_ref=phase_buf, dst_ref=gathered.at[refl], send_sem=send_sem.at[step],
+            recv_sem=recv_sem.at[step], device_id=(peer, me), device_id_type=MESH,
         )
         copy.start()
         copies.append(copy)
-    out_ref[me] = phase_ref[...]
+    gathered[refl] = phase_buf[...]
     for copy in copies:
         copy.wait_send()
-    for step in range(1, count):
-        source = lax.rem(me + count - step, count)
+    for step in range(1, refl_count):
+        source = lax.rem(refl + refl_count - step, refl_count)
         pltpu.make_async_remote_copy(
-            src_ref=phase_ref,
-            dst_ref=out_ref.at[source],
-            send_sem=send_sem.at[step],
-            recv_sem=recv_sem.at[step],
-            device_id=(source, slab),
-            device_id_type=MESH,
+            src_ref=phase_buf, dst_ref=gathered.at[source], send_sem=send_sem.at[step],
+            recv_sem=recv_sem.at[step], device_id=(source, me), device_id_type=MESH,
         ).wait_recv()
-
-
-def gather_refl(phase, count):
+    shift = scalars[3] * gathered[0]
+    for r in range(1, refl_count):
+        shift = shift + scalars[3 + r] * gathered[r]
+    for p in range(planes):
+        obj_re, obj_im = obj_ref[p, 0], obj_ref[p, 1]
+        out_ref[p, 0] = obj_re - 0.5 * (grid_ref[p, 0] - obj_im * shift[p])
+        out_ref[p, 1] = obj_im - 0.5 * (grid_ref[p, 1] + obj_re * shift[p])
+
+
+def post_step(scalars, grid, obj, slab_count, refl_count):
+    planes, _, rows, width = grid.shape
     return pl.pallas_call(
-        gather_kernel,
-        out_shape=jax.ShapeDtypeStruct((count,) + phase.shape, phase.dtype),
-        in_specs=[pl.BlockSpec(memory_space=pltpu.VMEM)],
+        functools.partial(post_kernel, slab_count=slab_count),
+        out_shape=jax.ShapeDtypeStruct(grid.shape, jnp.float32),
+        in_specs=[pl.BlockSpec(memory_space=pltpu.SMEM)]
+        + [pl.BlockSpec(memory_space=pltpu.VMEM)] * 2,
         out_specs=pl.BlockSpec(memory_space=pltpu.VMEM),
-        scratch_shapes=[pltpu.SemaphoreType.DMA((count,)), pltpu.SemaphoreType.DMA((count,))],
+        scratch_shapes=[
+            pltpu.VMEM((2, 2, rows, width), jnp.float32),
+            pltpu.VMEM((refl_count, planes, rows, width), jnp.float32),
+            pltpu.VMEM((planes, rows, width), jnp.float32),
+            pltpu.SemaphoreType.DMA((2,)),
+            pltpu.SemaphoreType.DMA((2,)),
+            pltpu.SemaphoreType.DMA((refl_count,)),
+            pltpu.SemaphoreType.DMA((refl_count,)),
+        ],
         compiler_params=pltpu.CompilerParams(collective_id=0, has_side_effects=True),
-    )(phase)
+    )(scalars, grid, obj)
 
 
 def exchange_kernel(
@@ -242,28 +307,19 @@
         precision=lax.Precision.HIGHEST,
         preferred_element_type=jnp.float32,
     )
-    gridded = gridded.reshape(plane_count, row_count, 2, tile_width)
-    padded = extended(gridded, (("slab", 0),), 1)
-    grad_x = 0.5 * (padded[2:] - padded[:-2])
-    grad_y = central(gridded, 1)
-    grad_z = central(gridded, 3)
+    gridded = gridded.reshape(plane_count, row_count, 2, tile_width).transpose(0, 2, 1, 3)
     refl_count = bragg_vectors.shape[0]
     places = jnp.arange(refl_count, dtype=jnp.int32)
     my_refl = lax.axis_index("refl")
     q_self = jnp.sum(jnp.where((places == my_refl)[:, None], bragg_vectors, 0.0), axis=0)
     mate = my_refl + 1 - 2 * (my_refl % 2)
     q_other = jnp.sum(jnp.where((places == mate)[:, None], bragg_vectors, 0.0), axis=0)
-    obj = object_field[0]
-    obj_real = obj[:, :, 0]
-    obj_imag = obj[:, :, 1]
-    phase = phase_term(obj_real, obj_imag, grad_x, grad_y, grad_z, q_self)
     diff = q_self - q_other
-    gathered = gather_refl(phase.reshape(plane_count * row_count, tile_width), refl_count)
     weights = jnp.sum(bragg_vectors * diff[None, :], axis=1)
-    shift = jnp.sum(weights[:, None, None] * gathered, axis=0).reshape(plane_count, row_count, tile_width)
-    new_real = obj_real - 0.5 * (gridded[:, :, 0] - obj_imag * shift)
-    new_imag = obj_imag - 0.5 * (gridded[:, :, 1] + obj_real * shift)
-    return jnp.stack([new_real, new_imag], axis=2)[None]
+    scalars = jnp.concatenate([q_self, weights])
+    obj = object_field[0].transpose(0, 2, 1, 3)
+    updated = post_step(scalars, gridded, obj, slab_count, refl_count)
+    return updated.transpose(0, 2, 1, 3)[None]
 
 
 def solution(mesh):

time: 86.9 us -> 82.4 us (0.948)
  the two profiles are of different devices: /device:TPU:7 before, /device:TPU:16 now
where the time goes in v6:
time: 82.4 us; the launch traced here: 82 us
  Pallas kernels  68.6 us (83%)
  local copies, waits for them, and re-layouts  7.05 us (9%)
  other arithmetic  4.38 us (5%)
  matrix products  1.91 us (2%)
    pallas_call x1, Pallas kernels, exchange_slab(): pl.pallas_call(exchange_kernel, out_shape=(jax.ShapeDtypeStruct(data_shap...  47.9 us
    pallas_call x1, Pallas kernels, post_step(): pl.pallas_call(functools.partial(post_kernel, slab_count=slab_count), out...  20.7 us
    unnamed x12, local copies, waits for them, and re-layouts  2.59 us

profile of v6, /device:TPU:16, one launch (start us, length us, event | category | flops | bytes accessed | tf_op | source)
XLA Modules:
  0.0 82.0 jit_solution(9413167050139199034)
XLA Ops:
  0.0 0.0 copy-start
  0.0 0.0 copy-start.2
  0.0 0.9 %select_reduce_fusion = (f32[3]{0:T(128)S(1)}, f32[3]{0:T(128)S(1)}) fusion(f32[8,3]{0,1:T(4,128)} %param.12, pred[8]{0:T(512)(128)(4,1)S(1)} %get-tuple-element.13, pred[8]{0:T(512)(128)(4,1)S(1)} %get-tuple-element.14), kind=kLoop, calls=%fused_computation.18 | loop fusion | flops 90 | bytes 136 | tf_op jit(solution)/shard_map/reduce_sum | solution.py:316
  0.9 0.8 multiply_reduce_fusion
  1.7 0.7 pad_maximum_fusion.scalars
  2.4 1.9 %copy.27 = bf16[128,8,2,128]{3,1,2,0:T(8,128)(2,1)} copy(bf16[128,8,2,128]{3,2,1,0:T(2,128)(2,1)} %bitcast.47) | data formatting | bytes 1048576
  4.3 0.0 copy-done.3
  4.4 0.1 pad.2.clone
  4.4 0.7 maximum_maximum_fusion.ids_ref
  5.1 0.5 convert_reduce_fusion
  5.6 0.6 bitcast_add_fusion.slot_ref
  6.2 47.9 %shard_map.73 = (bf16[64,32,256]{2,1,0:T(8,128)(2,1)}, bf16[64,16,128]{2,1,0:T(8,128)(2,1)}) custom-call(s32[1,1024]{1,0:T(1,128)} %bitcast_add_fusion.slot_ref, bf16[1024,256]{1,0:T(8,128)(2,1)} %bitcast.44, bf16[16,1024]{1,0:T(8,128)(2,1)} %maximum_maximum_fusion.ids_ref), custom_call_target="tpu_custom_call" | custom-call | tf_op jit(solution)/shard_map/pallas_call | solution.py:250
  54.2 1.0 %fusion.10 = (bf16[64,1,128]{2,1,0:T(2,128)(2,1)S(1)}, bf16[64,1,128]{2,1,0:T(2,128)(2,1)S(1)}) fusion(bf16[64,16,128]{2,1,0:T(8,128)(2,1)} %get-tuple-element.7), kind=kLoop, calls=%fused_computation.23 | loop fusion | bytes 65536 | tf_op jit(solution)/shard_map/slice | solution.py:295
  55.2 0.2 add_reduce_fusion
  55.4 0.1 add.40
  55.5 1.5 %copy.16 = bf16[256,2048]{1,0:T(8,128)(2,1)S(1)} copy(bf16[256,2048]{0,1:T(8,128)(2,1)} %bitcast.45) | data formatting | bytes 2097152 | tf_op jit(solution)/shard_map/dot_general | solution.py:302
  57.0 0.8 fusion.6
  57.8 0.0 copy-start.1
  57.8 0.3 dot_general.15
  58.1 1.1 %convolution_bitcast_fusion.grid_ref = f32[2,2,32,128]{3,2,1,0:T(8,128)} fusion(bf16[1024,128,1,1]{1,0,3,2:T(8,128)(2,1)S(1)} %bitcast.43, f32[2,32,2,1024]{3,2,1,0:T(2,128)S(1)} %dot_general.15), kind=kOutput, calls=%fused_computation.9 | convolution fusion | flops 201326592 | bytes 851968 | tf_op jit(solution)/shard_map/dot_general | solution.py:304
  59.2 0.0 copy-done.1
  59.2 0.6 copy.28
  59.8 20.7 %shard_map.74 = f32[2,2,32,128]{3,2,1,0:T(8,128)} custom-call(f32[11]{0:T(128)} %pad_maximum_fusion.scalars, f32[2,2,32,128]{3,2,1,0:T(8,128)} %convolution_bitcast_fusion.grid_ref, f32[2,2,32,128]{3,2,1,0:T(8,128)} %bitcast.49), custom_call_target="tpu_custom_call" | custom-call | tf_op jit(solution)/shard_map/pallas_call | solution.py:136
  80.5 1.5 %copy.19 = f32[1,2,32,2,128]{4,3,2,1,0:T(2,128)} copy(f32[1,2,32,2,128]{4,2,3,1,0:T(8,128)} %bitcast.48) | data formatting | bytes 131072 | tf_op jit(solution)/shard_map/broadcast_in_dim | solution.py:322
  (11 shorter events, 0.0 us)
Async XLA Ops:
  0.0 58.1 %copy-start = (bf16[8,128,128]{2,1,0:T(8,128)(2,1)S(1)}, bf16[8,128,128]{2,1,0:T(8,128)(2,1)}, u32[]{:S(2)}) copy-start(bf16[8,128,128]{2,1,0:T(8,128)(2,1)} %param.11) | copy-start | bytes 786436
  0.0 4.3 %copy-start.3 = (s32[1,1024]{1,0:T(1,128)S(1)}, s32[1,1024]{1,0:T(1,128)}, u32[]{:S(2)}) copy-start(s32[1,1024]{1,0:T(1,128)} %param.9) | copy-start | bytes 12292
  0.0 4.3 %copy-start.4 = (s32[1,1024]{1,0:T(1,128)S(1)}, s32[1,1024]{1,0:T(1,128)}, u32[]{:S(2)}) copy-start(s32[1,1024]{1,0:T(1,128)} %param.10) | copy-start | bytes 12292
  0.0 5.1 %copy-start.2 = (s32[1,1024,1]{1,2,0:T(1,128)S(1)}, s32[1,1024,1]{1,2,0:T(1,128)}, u32[]{:S(2)}) copy-start(s32[1,1024,1]{1,2,0:T(1,128)} %param.8) | copy-start | bytes 12292
  57.8 1.4 %copy-start.1 = (f32[1,2,32,2,128]{4,3,2,1,0:T(2,128)S(1)}, f32[1,2,32,2,128]{4,3,2,1,0:T(2,128)}, u32[]{:S(2)}) copy-start(f32[1,2,32,2,128]{4,3,2,1,0:T(2,128)} %param.13) | copy-start | bytes 196612

commit v7 on v6

--- a/solution.py
+++ b/solution.py
@@ -153,8 +153,7 @@
 
 
 def exchange_kernel(
-    slot_ref, values_ref, ids_ref, data_out, code_out,
-    data_buf, code_buf, data_send, data_recv, code_send, code_recv,
+    slot_ref, values_ref, code_in, data_out, code_out, data_buf, data_send, data_recv, code_send, code_recv,
 ):
     count, capacity = data_out.shape[0], data_out.shape[1]
     group = 8 if count >= 16 else count // 2
@@ -178,12 +177,6 @@
         data_buf[pl.ds(g * group, group)] = sent.astype(jnp.bfloat16).reshape(
             group, capacity, sent.shape[1]
         )
-        codes = lax.dot_general(
-            ids_ref[...], chosen, (((1,), (1,)), ((), ())), preferred_element_type=jnp.float32
-        ).astype(jnp.bfloat16)
-        for part in range(group):
-            window = (part * capacity) // 128
-            code_buf[g * group + part] = codes[:, window * 128 : (window + 1) * 128]
 
     def outgoing(d):
         data = pltpu.make_async_remote_copy(
@@ -191,7 +184,7 @@
             recv_sem=data_recv.at[me], device_id=(refl, d), device_id_type=MESH,
         )
         code = pltpu.make_async_remote_copy(
-            src_ref=code_buf.at[d], dst_ref=code_out.at[me], send_sem=code_send.at[d],
+            src_ref=code_in.at[d], dst_ref=code_out.at[me], send_sem=code_send.at[d],
             recv_sem=code_recv.at[me], device_id=(refl, d), device_id_type=MESH,
         )
         return data, code
@@ -202,7 +195,7 @@
             recv_sem=data_recv.at[s], device_id=(refl, s), device_id_type=MESH,
         )
         code = pltpu.make_async_remote_copy(
-            src_ref=code_buf.at[s], dst_ref=code_out.at[s], send_sem=code_send.at[s],
+            src_ref=code_in.at[s], dst_ref=code_out.at[s], send_sem=code_send.at[s],
             recv_sem=code_recv.at[s], device_id=(refl, s), device_id_type=MESH,
         )
         return data, code
@@ -214,8 +207,8 @@
             @pl.when(d != me)
             def _():
                 data, code = outgoing(d)
+                code.start()
                 data.start()
-                code.start()
 
     home = me // group
     pack(home)
@@ -230,7 +223,8 @@
 
     lax.fori_loop(1, groups, later, 0)
     data_out[me] = data_buf[me]
-    code_out[me] = code_buf[me]
+    local = pltpu.make_async_copy(code_in.at[me], code_out.at[me], code_send.at[me])
+    local.start()
 
     def finish(step, carry):
         data, code = outgoing(lax.rem(me + step, count))
@@ -242,29 +236,28 @@
         return carry
 
     lax.fori_loop(1, count, finish, 0)
-
-
-def exchange_slab(flat_slot, values, ids, count, capacity):
+    local.wait()
+
+
+def exchange_slab(flat_slot, values, codes, count, capacity):
     data_shape = (count, capacity, values.shape[1])
-    code_shape = (count, ids.shape[0], 128)
     return pl.pallas_call(
         exchange_kernel,
         out_shape=(
             jax.ShapeDtypeStruct(data_shape, jnp.bfloat16),
-            jax.ShapeDtypeStruct(code_shape, jnp.bfloat16),
+            jax.ShapeDtypeStruct(codes.shape, codes.dtype),
         ),
-        in_specs=[pl.BlockSpec(memory_space=pltpu.VMEM)] * 3,
-        out_specs=(pl.BlockSpec(memory_space=pltpu.VMEM), pl.BlockSpec(memory_space=pltpu.VMEM)),
+        in_specs=[pl.BlockSpec(memory_space=pltpu.VMEM)] * 2 + [pl.BlockSpec(memory_space=pl.ANY)],
+        out_specs=(pl.BlockSpec(memory_space=pltpu.VMEM), pl.BlockSpec(memory_space=pl.ANY)),
         scratch_shapes=[
             pltpu.VMEM(data_shape, jnp.bfloat16),
-            pltpu.VMEM(code_shape, jnp.bfloat16),
             pltpu.SemaphoreType.DMA((count,)),
             pltpu.SemaphoreType.DMA((count,)),
             pltpu.SemaphoreType.DMA((count,)),
             pltpu.SemaphoreType.DMA((count,)),
         ],
         compiler_params=pltpu.CompilerParams(collective_id=1, has_side_effects=True),
-    )(flat_slot, values, ids)
+    )(flat_slot, values, codes)
 
 
 def per_device(detector, owners, block_ids, kernel_ids, kernels, bragg_vectors, object_field):
@@ -285,16 +278,16 @@
     same = (owner[:, None] == owner[None, :]) & order
     slots = jnp.sum(same.astype(jnp.int32), axis=1)
     flat_slot = owner * capacity + slots
-    ids = jnp.concatenate(
-        [block_ids, kernel_ids, jnp.zeros((14, tile_count), jnp.int32)], axis=0
-    ).astype(jnp.bfloat16)
-    got, got_code = exchange_slab(flat_slot[None, :], values, ids, slab_count, capacity)
+    codes = block_ids[0] * kernel_count + kernel_ids[0]
+    placed = flat_slot[None, :] == lax.broadcasted_iota(jnp.int32, (slab_count * capacity, tile_count), 0)
+    sent_codes = jnp.max(jnp.where(placed, codes[None, :], 0), axis=1).reshape(slab_count, 1, capacity)
+    sent_codes = jnp.concatenate(
+        [sent_codes, jnp.zeros((slab_count, 1, 128 - capacity), jnp.int32)], axis=2
+    )
+    got, got_code = exchange_slab(flat_slot[None, :], values, sent_codes, slab_count, capacity)
     row_total = slab_count * capacity
     rows = got.reshape(row_total, row_width)
-    offset = lax.rem(lax.axis_index("slab"), 4) * capacity
-    got_blocks = lax.dynamic_slice_in_dim(got_code[:, 0, :], offset, capacity, axis=1).astype(jnp.int32)
-    got_kernels = lax.dynamic_slice_in_dim(got_code[:, 1, :], offset, capacity, axis=1).astype(jnp.int32)
-    got_codes = (got_blocks * kernel_count + got_kernels).reshape(row_total)
+    got_codes = got_code[:, 0, :capacity].reshape(row_total)
     chosen = (
         got_codes[None, :]
         == lax.broadcasted_iota(jnp.int32, (block_count * kernel_count, row_total), 0)

time: 82.4 us -> 79.8 us (0.968)
  Pallas kernels: 68.6 us -> 63.1 us
  other arithmetic: 4.38 us -> 7.46 us
    pallas_call x1, Pallas kernels: 47.9 us -> 42.5 us  [exchange_slab(): pl.pallas_call(exchange_kernel, out_shape=(jax.ShapeDtypeStruct(data_shap...]
    add x1 -> x2, other arithmetic: 0.6 us -> 1.97 us  [per_device(): flat_slot = owner * capacity + slots]
    reduce_max x0 -> x1, other arithmetic: none -> 1.19 us  [per_device(): jnp.max(jnp.where(placed, codes[None, :], 0), axis=1)]
    slice x1, local copies, waits for them, and re-layouts: 1.04 us -> 0.08 us  [per_device(): got_codes = got_code[:, 0, :capacity].reshape(row_total)]
    unnamed x12 -> x8, local copies, waits for them, and re-layouts: 2.59 us -> 2.58 us
where the time goes in v7:
time: 79.8 us; the launch traced here: 79.3 us
  Pallas kernels  63.1 us (79%)
  other arithmetic  7.46 us (9%)
  local copies, waits for them, and re-layouts  6.73 us (8%)
  matrix products  1.92 us (2%)
    pallas_call x1, Pallas kernels, exchange_slab(): pl.pallas_call(exchange_kernel, out_shape=(jax.ShapeDtypeStruct(data_shap...  42.5 us
    pallas_call x1, Pallas kernels, post_step(): pl.pallas_call(functools.partial(post_kernel, slab_count=slab_count), out...  20.6 us
    unnamed x8, local copies, waits for them, and re-layouts  2.58 us
    add x2, other arithmetic, per_device(): flat_slot = owner * capacity + slots  1.97 us

profile of v7, /device:TPU:16, one launch (start us, length us, event | category | flops | bytes accessed | tf_op | source)
XLA Modules:
  0.0 79.3 jit_solution(7448563112481016900)
XLA Ops:
  0.0 0.0 copy-start
  0.0 0.9 %select_reduce_fusion.1 = (f32[3]{0:T(128)S(1)}, f32[3]{0:T(128)S(1)}) fusion(f32[8,3]{0,1:T(4,128)} %param.12, pred[8]{0:T(512)(128)(4,1)S(1)} %get-tuple-element.11, pred[8]{0:T(512)(128)(4,1)S(1)} %get-tuple-element.12), kind=kLoop, calls=%fused_computation.21 | loop fusion | flops 90 | bytes 136 | tf_op jit(solution)/shard_map/reduce_sum | solution.py:309
  0.9 0.8 multiply_reduce_fusion
  1.7 0.7 pad_maximum_fusion.scalars
  2.3 1.3 %convert_reduce_fusion = s32[1024]{0:T(1024)S(1)} fusion(s32[1024]{0:T(1024)} %bitcast.53), kind=kLoop, calls=%fused_computation.2 | loop fusion | flops 5241856 | bytes 8192 | tf_op jit(solution)/shard_map/reduce_sum | solution.py:279
  3.6 0.7 multiply_add_fusion.2
  4.3 0.7 multiply_add_fusion.1
  5.0 1.2 %select_reduce_fusion = s32[2048]{0:T(1024)S(1)} fusion(s32[1024]{0:T(1024)S(1)} %bitcast.56, s32[1024]{0:T(1024)S(1)} %multiply_add_fusion.2), kind=kLoop, calls=%fused_computation | loop fusion | flops 6289408 | bytes 16384 | tf_op jit(solution)/shard_map/reduce_max | solution.py:283
  6.2 0.1 reshape.69
  6.3 0.6 concatenate.7.code_in
  6.9 1.3 %bitcast_add_fusion.slot_ref = s32[1,1024]{1,0:T(1,128)} fusion(s32[1,1024]{1,0:T(1,128)S(1)} %bitcast.55, s32[1,1024,1]{1,2,0:T(1,128)} %param.8), kind=kLoop, calls=%fused_computation.17 | loop fusion | flops 2048 | bytes 12288 | tf_op jit(solution)/shard_map/add | solution.py:280
  8.2 1.9 %copy.29 = bf16[128,8,2,128]{3,1,2,0:T(8,128)(2,1)} copy(bf16[128,8,2,128]{3,2,1,0:T(2,128)(2,1)} %bitcast.49) | data formatting | bytes 1048576
  10.1 42.5 %shard_map.73 = (bf16[64,32,256]{2,1,0:T(8,128)(2,1)}, s32[64,1,128]{2,1,0:T(1,128)}) custom-call(s32[1,1024]{1,0:T(1,128)} %bitcast_add_fusion.slot_ref, bf16[1024,256]{1,0:T(8,128)(2,1)} %bitcast.46, s32[64,1,128]{2,1,0:T(1,128)} %concatenate.7.code_in), custom_call_target="tpu_custom_call" | custom-call | tf_op jit(solution)/shard_map/pallas_call | solution.py:244
  52.7 1.5 %copy.18 = bf16[256,2048]{1,0:T(8,128)(2,1)S(1)} copy(bf16[256,2048]{0,1:T(8,128)(2,1)} %bitcast.48) | data formatting | bytes 2097152 | tf_op jit(solution)/shard_map/dot_general | solution.py:295
  54.2 0.1 slice_reduce_fusion
  54.3 0.1 eq.70
  54.3 0.8 fusion.6
  55.1 0.0 copy-start.1
  55.1 0.3 dot_general.15
  55.4 1.1 %convolution_bitcast_fusion.grid_ref = f32[2,2,32,128]{3,2,1,0:T(8,128)} fusion(bf16[1024,128,1,1]{1,0,3,2:T(8,128)(2,1)S(1)} %bitcast.45, f32[2,32,2,1024]{3,2,1,0:T(2,128)S(1)} %dot_general.15), kind=kOutput, calls=%fused_computation.11 | convolution fusion | flops 201326592 | bytes 851968 | tf_op jit(solution)/shard_map/dot_general | solution.py:297
  56.6 0.0 copy-done.1
  56.6 0.6 copy.30
  57.2 20.6 %shard_map.74 = f32[2,2,32,128]{3,2,1,0:T(8,128)} custom-call(f32[11]{0:T(128)} %pad_maximum_fusion.scalars, f32[2,2,32,128]{3,2,1,0:T(8,128)} %convolution_bitcast_fusion.grid_ref, f32[2,2,32,128]{3,2,1,0:T(8,128)} %bitcast.51), custom_call_target="tpu_custom_call" | custom-call | tf_op jit(solution)/shard_map/pallas_call | solution.py:136
  77.8 1.5 %copy.21 = f32[1,2,32,2,128]{4,3,2,1,0:T(2,128)} copy(f32[1,2,32,2,128]{4,2,3,1,0:T(8,128)} %bitcast.50) | data formatting | bytes 131072 | tf_op jit(solution)/shard_map/broadcast_in_dim | solution.py:315
  (6 shorter events, 0.0 us)
Async XLA Ops:
  0.0 55.4 %copy-start = (bf16[8,128,128]{2,1,0:T(8,128)(2,1)S(1)}, bf16[8,128,128]{2,1,0:T(8,128)(2,1)}, u32[]{:S(2)}) copy-start(bf16[8,128,128]{2,1,0:T(8,128)(2,1)} %param.11) | copy-start | bytes 786436
  52.6 1.5 %copy-start.2 = (s32[64,1,128]{2,1,0:T(1,128)S(1)}, s32[64,1,128]{2,1,0:T(1,128)}, u32[]{:S(2)}) copy-start(s32[64,1,128]{2,1,0:T(1,128)} %get-tuple-element.7) | copy-start | bytes 98308
  55.1 1.4 %copy-start.1 = (f32[1,2,32,2,128]{4,3,2,1,0:T(2,128)S(1)}, f32[1,2,32,2,128]{4,3,2,1,0:T(2,128)}, u32[]{:S(2)}) copy-start(f32[1,2,32,2,128]{4,3,2,1,0:T(2,128)} %param.13) | copy-start | bytes 196612

commit v8 on v7

--- a/solution.py
+++ b/solution.py
@@ -81,7 +81,11 @@
         before = jnp.where(lane_of == 0, 0.0, pltpu.roll(field, 1, 1))
         return 0.5 * (after - before)
 
-    q0, q1, q2 = scalars[0], scalars[1], scalars[2]
+    mate = refl + 1 - 2 * lax.rem(refl, 2)
+    q0, q1, q2 = scalars[refl, 0], scalars[refl, 1], scalars[refl, 2]
+    d0 = q0 - scalars[mate, 0]
+    d1 = q1 - scalars[mate, 1]
+    d2 = q2 - scalars[mate, 2]
     partial = []
     for p in range(planes):
         obj_re, obj_im = obj_ref[p, 0], obj_ref[p, 1]
@@ -122,9 +126,12 @@
             src_ref=phase_buf, dst_ref=gathered.at[source], send_sem=send_sem.at[step],
             recv_sem=recv_sem.at[step], device_id=(source, me), device_id_type=MESH,
         ).wait_recv()
-    shift = scalars[3] * gathered[0]
+    def weight(r):
+        return scalars[r, 0] * d0 + scalars[r, 1] * d1 + scalars[r, 2] * d2
+
+    shift = weight(0) * gathered[0]
     for r in range(1, refl_count):
-        shift = shift + scalars[3 + r] * gathered[r]
+        shift = shift + weight(r) * gathered[r]
     for p in range(planes):
         obj_re, obj_im = obj_ref[p, 0], obj_ref[p, 1]
         out_ref[p, 0] = obj_re - 0.5 * (grid_ref[p, 0] - obj_im * shift[p])
@@ -302,16 +309,8 @@
     )
     gridded = gridded.reshape(plane_count, row_count, 2, tile_width).transpose(0, 2, 1, 3)
     refl_count = bragg_vectors.shape[0]
-    places = jnp.arange(refl_count, dtype=jnp.int32)
-    my_refl = lax.axis_index("refl")
-    q_self = jnp.sum(jnp.where((places == my_refl)[:, None], bragg_vectors, 0.0), axis=0)
-    mate = my_refl + 1 - 2 * (my_refl % 2)
-    q_other = jnp.sum(jnp.where((places == mate)[:, None], bragg_vectors, 0.0), axis=0)
-    diff = q_self - q_other
-    weights = jnp.sum(bragg_vectors * diff[None, :], axis=1)
-    scalars = jnp.concatenate([q_self, weights])
     obj = object_field[0].transpose(0, 2, 1, 3)
-    updated = post_step(scalars, gridded, obj, slab_count, refl_count)
+    updated = post_step(bragg_vectors, gridded, obj, slab_count, refl_count)
     return updated.transpose(0, 2, 1, 3)[None]
 
 

time: 79.8 us -> 78.1 us (0.979)
  other arithmetic: 7.46 us -> 5.16 us
    reduce_sum x2 -> x0, other arithmetic: 1.64 us -> none  [the longest x1 0.87 us: per_device(): jnp.sum(jnp.where((places == mate)[:, None], bragg_vectors, 0.0), axis=0)]
    unnamed x8 -> x11, local copies, waits for them, and re-layouts: 2.58 us -> 3.25 us
where the time goes in v8:
time: 78.1 us; the launch traced here: 77.7 us
  Pallas kernels  63.1 us (81%)
  local copies, waits for them, and re-layouts  7.4 us (9%)
  other arithmetic  5.16 us (7%)
  matrix products  1.91 us (2%)
    pallas_call x1, Pallas kernels, exchange_slab(): pl.pallas_call(exchange_kernel, out_shape=(jax.ShapeDtypeStruct(data_shap...  42.5 us
    pallas_call x1, Pallas kernels, post_step(): pl.pallas_call(functools.partial(post_kernel, slab_count=slab_count), out...  20.6 us
    unnamed x11, local copies, waits for them, and re-layouts  3.25 us
    add x2, other arithmetic, per_device(): flat_slot = owner * capacity + slots  1.97 us

profile of v8, /device:TPU:16, one launch (start us, length us, event | category | flops | bytes accessed | tf_op | source)
XLA Modules:
  0.0 77.7 jit_solution(5994857949536479632)
XLA Ops:
  0.0 0.0 copy-start
  0.0 1.3 %convert_reduce_fusion = s32[1024]{0:T(1024)S(1)} fusion(s32[1024]{0:T(1024)} %bitcast.53), kind=kLoop, calls=%fused_computation.2 | loop fusion | flops 5241856 | bytes 8192 | tf_op jit(solution)/shard_map/reduce_sum | solution.py:286
  1.3 0.7 multiply_add_fusion.2
  2.0 0.7 multiply_add_fusion.1
  2.7 1.2 %select_reduce_fusion = s32[2048]{0:T(1024)S(1)} fusion(s32[1024]{0:T(1024)S(1)} %bitcast.56, s32[1024]{0:T(1024)S(1)} %multiply_add_fusion.2), kind=kLoop, calls=%fused_computation | loop fusion | flops 6289408 | bytes 16384 | tf_op jit(solution)/shard_map/reduce_max | solution.py:290
  3.9 0.1 reshape.56
  4.0 0.6 concatenate.3.code_in
  4.6 1.3 %bitcast_add_fusion.slot_ref = s32[1,1024]{1,0:T(1,128)} fusion(s32[1,1024]{1,0:T(1,128)S(1)} %bitcast.55, s32[1,1024,1]{1,2,0:T(1,128)} %param.8), kind=kLoop, calls=%fused_computation.17 | loop fusion | flops 2048 | bytes 12288 | tf_op jit(solution)/shard_map/add | solution.py:287
  5.9 1.9 %copy.32 = bf16[128,8,2,128]{3,1,2,0:T(8,128)(2,1)} copy(bf16[128,8,2,128]{3,2,1,0:T(2,128)(2,1)} %bitcast.49) | data formatting | bytes 1048576
  7.8 42.5 %shard_map.73 = (bf16[64,32,256]{2,1,0:T(8,128)(2,1)}, s32[64,1,128]{2,1,0:T(1,128)}) custom-call(s32[1,1024]{1,0:T(1,128)} %bitcast_add_fusion.slot_ref, bf16[1024,256]{1,0:T(8,128)(2,1)} %bitcast.46, s32[64,1,128]{2,1,0:T(1,128)} %concatenate.3.code_in), custom_call_target="tpu_custom_call" | custom-call | tf_op jit(solution)/shard_map/pallas_call | solution.py:251
  50.4 1.5 %copy.20 = bf16[256,2048]{1,0:T(8,128)(2,1)S(1)} copy(bf16[256,2048]{0,1:T(8,128)(2,1)} %bitcast.48) | data formatting | bytes 2097152 | tf_op jit(solution)/shard_map/dot_general | solution.py:302
  51.8 0.0 copy-done.2
  51.9 0.1 slice_reduce_fusion
  51.9 0.1 eq.44
  52.0 0.8 %fusion.6 = f32[64,2,8,128]{3,2,1,0:T(8,128)S(1)} fusion(bf16[2,128,2048,1]{2,1,0,3:T(8,128)(2,1)S(1)} %bitcast.47, s32[64,8]{1,0:T(8,128)S(1)} %multiply_add_fusion, s32[2048]{0:T(1024)S(1)} %eq.44), kind=kOutput, calls=%fused_computation.10 | convolution fusion | flops 537919488 | bytes 1583104 | tf_op jit(solution)/shard_map/dot_general | solution.py:302
  52.8 0.0 copy-start.1
  52.8 0.0 copy-start.3
  52.8 0.3 dot_general.15
  53.1 1.1 %convolution_bitcast_fusion.grid_ref = f32[2,2,32,128]{3,2,1,0:T(8,128)} fusion(bf16[1024,128,1,1]{1,0,3,2:T(8,128)(2,1)S(1)} %bitcast.45, f32[2,32,2,1024]{3,2,1,0:T(2,128)S(1)} %dot_general.15), kind=kOutput, calls=%fused_computation.11 | convolution fusion | flops 201326592 | bytes 851968 | tf_op jit(solution)/shard_map/dot_general | solution.py:304
  54.3 0.0 copy-done.1
  54.3 0.6 copy.33
  54.9 0.7 copy.23.scalars
  55.6 20.6 %shard_map.74 = f32[2,2,32,128]{3,2,1,0:T(8,128)} custom-call(f32[8,3]{1,0:T(8,128)} %copy.23.scalars, f32[2,2,32,128]{3,2,1,0:T(8,128)} %convolution_bitcast_fusion.grid_ref, f32[2,2,32,128]{3,2,1,0:T(8,128)} %bitcast.51), custom_call_target="tpu_custom_call" | custom-call | tf_op jit(solution)/shard_map/pallas_call | solution.py:143
  76.2 1.5 %copy.24 = f32[1,2,32,2,128]{4,3,2,1,0:T(2,128)} copy(f32[1,2,32,2,128]{4,2,3,1,0:T(8,128)} %bitcast.50) | data formatting | bytes 131072 | tf_op jit(solution)/shard_map/broadcast_in_dim | solution.py:314
  (4 shorter events, 0.0 us)
Async XLA Ops:
  0.0 53.1 %copy-start = (bf16[8,128,128]{2,1,0:T(8,128)(2,1)S(1)}, bf16[8,128,128]{2,1,0:T(8,128)(2,1)}, u32[]{:S(2)}) copy-start(bf16[8,128,128]{2,1,0:T(8,128)(2,1)} %param.11) | copy-start | bytes 786436
  50.3 1.5 %copy-start.2 = (s32[64,1,128]{2,1,0:T(1,128)S(1)}, s32[64,1,128]{2,1,0:T(1,128)}, u32[]{:S(2)}) copy-start(s32[64,1,128]{2,1,0:T(1,128)} %get-tuple-element.7) | copy-start | bytes 98308
  52.8 1.4 %copy-start.1 = (f32[1,2,32,2,128]{4,3,2,1,0:T(2,128)S(1)}, f32[1,2,32,2,128]{4,3,2,1,0:T(2,128)}, u32[]{:S(2)}) copy-start(f32[1,2,32,2,128]{4,3,2,1,0:T(2,128)} %param.13) | copy-start | bytes 196612
  52.8 2.1 %copy-start.3 = (f32[8,3]{0,1:T(4,128)S(1)}, f32[8,3]{0,1:T(4,128)}, u32[]{:S(2)}) copy-start(f32[8,3]{0,1:T(4,128)} %param.12) | copy-start | bytes 292

commit v9 on v8

--- a/solution.py
+++ b/solution.py
@@ -160,7 +160,8 @@
 
 
 def exchange_kernel(
-    slot_ref, values_ref, code_in, data_out, code_out, data_buf, data_send, data_recv, code_send, code_recv,
+    slot_ref, values_ref, ids_ref, data_out, code_out, data_buf, code_in, data_send, data_recv, code_send,
+    code_recv,
 ):
     count, capacity = data_out.shape[0], data_out.shape[1]
     group = 8 if count >= 16 else count // 2
@@ -184,6 +185,13 @@
         data_buf[pl.ds(g * group, group)] = sent.astype(jnp.bfloat16).reshape(
             group, capacity, sent.shape[1]
         )
+        codes = lax.dot_general(
+            ids_ref[...], chosen, (((1,), (1,)), ((), ())), preferred_element_type=jnp.float32
+        )
+        codes = (codes[0:1] * 8.0 + codes[1:2]).astype(jnp.int32)
+        for part in range(group):
+            window = (part * capacity) // 128
+            code_in[g * group + part] = codes[:, window * 128 : (window + 1) * 128]
 
     def outgoing(d):
         data = pltpu.make_async_remote_copy(
@@ -246,25 +254,27 @@
     local.wait()
 
 
-def exchange_slab(flat_slot, values, codes, count, capacity):
+def exchange_slab(flat_slot, values, ids, count, capacity):
     data_shape = (count, capacity, values.shape[1])
+    code_shape = (count, 1, 128)
     return pl.pallas_call(
         exchange_kernel,
         out_shape=(
             jax.ShapeDtypeStruct(data_shape, jnp.bfloat16),
-            jax.ShapeDtypeStruct(codes.shape, codes.dtype),
+            jax.ShapeDtypeStruct(code_shape, jnp.int32),
         ),
-        in_specs=[pl.BlockSpec(memory_space=pltpu.VMEM)] * 2 + [pl.BlockSpec(memory_space=pl.ANY)],
+        in_specs=[pl.BlockSpec(memory_space=pltpu.VMEM)] * 3,
         out_specs=(pl.BlockSpec(memory_space=pltpu.VMEM), pl.BlockSpec(memory_space=pl.ANY)),
         scratch_shapes=[
             pltpu.VMEM(data_shape, jnp.bfloat16),
+            pltpu.VMEM(code_shape, jnp.int32),
             pltpu.SemaphoreType.DMA((count,)),
             pltpu.SemaphoreType.DMA((count,)),
             pltpu.SemaphoreType.DMA((count,)),
             pltpu.SemaphoreType.DMA((count,)),
         ],
         compiler_params=pltpu.CompilerParams(collective_id=1, has_side_effects=True),
-    )(flat_slot, values, codes)
+    )(flat_slot, values, ids)
 
 
 def per_device(detector, owners, block_ids, kernel_ids, kernels, bragg_vectors, object_field):
@@ -285,16 +295,14 @@
     same = (owner[:, None] == owner[None, :]) & order
     slots = jnp.sum(same.astype(jnp.int32), axis=1)
     flat_slot = owner * capacity + slots
-    codes = block_ids[0] * kernel_count + kernel_ids[0]
-    placed = flat_slot[None, :] == lax.broadcasted_iota(jnp.int32, (slab_count * capacity, tile_count), 0)
-    sent_codes = jnp.max(jnp.where(placed, codes[None, :], 0), axis=1).reshape(slab_count, 1, capacity)
-    sent_codes = jnp.concatenate(
-        [sent_codes, jnp.zeros((slab_count, 1, 128 - capacity), jnp.int32)], axis=2
-    )
-    got, got_code = exchange_slab(flat_slot[None, :], values, sent_codes, slab_count, capacity)
+    ids = jnp.concatenate(
+        [block_ids, kernel_ids, jnp.zeros((6, tile_count), jnp.int32)], axis=0
+    ).astype(jnp.bfloat16)
+    got, got_code = exchange_slab(flat_slot[None, :], values, ids, slab_count, capacity)
     row_total = slab_count * capacity
     rows = got.reshape(row_total, row_width)
-    got_codes = got_code[:, 0, :capacity].reshape(row_total)
+    offset = lax.rem(lax.axis_index("slab"), 4) * capacity
+    got_codes = lax.dynamic_slice_in_dim(got_code[:, 0, :], offset, capacity, axis=1).reshape(row_total)
     chosen = (
         got_codes[None, :]
         == lax.broadcasted_iota(jnp.int32, (block_count * kernel_count, row_total), 0)

time: 78.1 us -> 75.4 us (0.965)
  the two profiles are of different devices: /device:TPU:16 before, /device:TPU:7 now
where the time goes in v9:
time: 75.4 us; the launch traced here: 74 us
  Pallas kernels  62.5 us (83%)
  local copies, waits for them, and re-layouts  7.63 us (10%)
  matrix products  1.91 us (3%)
  other arithmetic  1.81 us (2%)
    pallas_call x1, Pallas kernels, exchange_slab(): pl.pallas_call(exchange_kernel, out_shape=(jax.ShapeDtypeStruct(data_shap...  44.9 us
    pallas_call x1, Pallas kernels, post_step(): pl.pallas_call(functools.partial(post_kernel, slab_count=slab_count), out...  17.6 us
    unnamed x15, local copies, waits for them, and re-layouts  3.28 us
    broadcast_in_dim x1, local copies, waits for them, and re-layouts, per_device(): return updated.transpose(0, 2, 1, 3)[None]  1.52 us

profile of v9, /device:TPU:7, one launch (start us, length us, event | category | flops | bytes accessed | tf_op | source)
XLA Modules:
  0.0 74.0 jit_solution(10713983309891164628)
XLA Ops:
  0.0 0.0 copy-start
  0.0 0.0 copy-start.2
  0.0 2.0 %copy.30 = bf16[128,8,2,128]{3,1,2,0:T(8,128)(2,1)} copy(bf16[128,8,2,128]{3,2,1,0:T(2,128)(2,1)} %bitcast.47) | data formatting | bytes 1048576
  2.0 0.0 copy-done.3
  2.0 0.0 copy-done.4
  2.0 0.1 pad.2.clone
  2.1 0.7 maximum_maximum_fusion.ids_ref
  2.8 0.0 copy-done.2
  2.8 0.5 convert_reduce_fusion
  3.3 0.6 bitcast_add_fusion.slot_ref
  3.9 44.9 %shard_map.73 = (bf16[64,32,256]{2,1,0:T(8,128)(2,1)}, s32[64,1,128]{2,1,0:T(1,128)}) custom-call(s32[1,1024]{1,0:T(1,128)} %bitcast_add_fusion.slot_ref, bf16[1024,256]{1,0:T(8,128)(2,1)} %bitcast.44, bf16[8,1024]{1,0:T(8,128)(2,1)} %maximum_maximum_fusion.ids_ref), custom_call_target="tpu_custom_call" | custom-call | tf_op jit(solution)/shard_map/pallas_call | solution.py:260
  48.9 0.9 %dynamic-slice_reduce_fusion = s32[64,32]{1,0:T(8,128)S(1)} fusion(s32[64,1,128]{2,1,0:T(1,128)} %get-tuple-element.7, s32[]{:T(128)S(6)} %select_n.3), kind=kLoop, calls=%fused_computation.14 | loop fusion | bytes 16388 | tf_op jit(solution)/shard_map/dynamic_slice | solution.py:305
  49.8 0.1 eq.34
  49.9 1.5 %copy.18 = bf16[256,2048]{1,0:T(8,128)(2,1)S(1)} copy(bf16[256,2048]{0,1:T(8,128)(2,1)} %bitcast.45) | data formatting | bytes 2097152 | tf_op jit(solution)/shard_map/dot_general | solution.py:310
  51.4 0.8 %fusion.6 = f32[64,2,8,128]{3,2,1,0:T(8,128)S(1)} fusion(bf16[2,128,2048,1]{2,1,0,3:T(8,128)(2,1)S(1)} %bitcast.46, s32[64,8]{1,0:T(8,128)S(1)} %multiply_add_fusion, s32[2048]{0:T(1024)S(1)} %eq.34), kind=kOutput, calls=%fused_computation.8 | convolution fusion | flops 537919488 | bytes 1583104 | tf_op jit(solution)/shard_map/dot_general | solution.py:310
  52.2 0.0 copy-start.1
  52.2 0.0 copy-start.5
  52.2 0.3 dot_general.15
  52.5 0.0 copy-done
  52.5 1.1 %convolution_bitcast_fusion.grid_ref = f32[2,2,32,128]{3,2,1,0:T(8,128)} fusion(bf16[1024,128,1,1]{1,0,3,2:T(8,128)(2,1)S(1)} %bitcast.43, f32[2,32,2,1024]{3,2,1,0:T(2,128)S(1)} %dot_general.15), kind=kOutput, calls=%fused_computation.9 | convolution fusion | flops 201326592 | bytes 851968 | tf_op jit(solution)/shard_map/dot_general | solution.py:312
  53.6 0.6 copy.31
  54.2 0.7 copy.21.scalars
  54.9 17.6 %shard_map.74 = f32[2,2,32,128]{3,2,1,0:T(8,128)} custom-call(f32[8,3]{1,0:T(8,128)} %copy.21.scalars, f32[2,2,32,128]{3,2,1,0:T(8,128)} %convolution_bitcast_fusion.grid_ref, f32[2,2,32,128]{3,2,1,0:T(8,128)} %bitcast.49), custom_call_target="tpu_custom_call" | custom-call | tf_op jit(solution)/shard_map/pallas_call | solution.py:143
  72.5 1.5 %copy.22 = f32[1,2,32,2,128]{4,3,2,1,0:T(2,128)} copy(f32[1,2,32,2,128]{4,2,3,1,0:T(8,128)} %bitcast.48) | data formatting | bytes 131072 | tf_op jit(solution)/shard_map/broadcast_in_dim | solution.py:322
  (8 shorter events, 0.0 us)
Async XLA Ops:
  0.0 52.5 %copy-start = (bf16[8,128,128]{2,1,0:T(8,128)(2,1)S(1)}, bf16[8,128,128]{2,1,0:T(8,128)(2,1)}, u32[]{:S(2)}) copy-start(bf16[8,128,128]{2,1,0:T(8,128)(2,1)} %param.11) | copy-start | bytes 786436
  0.0 2.0 %copy-start.3 = (s32[1,1024]{1,0:T(1,128)S(1)}, s32[1,1024]{1,0:T(1,128)}, u32[]{:S(2)}) copy-start(s32[1,1024]{1,0:T(1,128)} %param.9) | copy-start | bytes 12292
  0.0 2.0 %copy-start.4 = (s32[1,1024]{1,0:T(1,128)S(1)}, s32[1,1024]{1,0:T(1,128)}, u32[]{:S(2)}) copy-start(s32[1,1024]{1,0:T(1,128)} %param.10) | copy-start | bytes 12292
  0.0 2.8 %copy-start.2 = (s32[1,1024,1]{1,2,0:T(1,128)S(1)}, s32[1,1024,1]{1,2,0:T(1,128)}, u32[]{:S(2)}) copy-start(s32[1,1024,1]{1,2,0:T(1,128)} %param.8) | copy-start | bytes 12292
  52.2 1.4 %copy-start.1 = (f32[1,2,32,2,128]{4,3,2,1,0:T(2,128)S(1)}, f32[1,2,32,2,128]{4,3,2,1,0:T(2,128)}, u32[]{:S(2)}) copy-start(f32[1,2,32,2,128]{4,3,2,1,0:T(2,128)} %param.13) | copy-start | bytes 196612
  52.2 2.1 %copy-start.5 = (f32[8,3]{0,1:T(4,128)S(1)}, f32[8,3]{0,1:T(4,128)}, u32[]{:S(2)}) copy-start(f32[8,3]{0,1:T(4,128)} %param.12) | copy-start | bytes 292

commit v10 on v9

--- a/solution.py
+++ b/solution.py
@@ -226,12 +226,18 @@
                 data.start()
 
     home = me // group
-    pack(home)
+    middle = groups // 2
+
+    def order(j):
+        return lax.rem(home + middle + (1 - 2 * lax.rem(j, 2)) * ((j + 1) // 2) + groups, groups)
+
+    first = order(0)
+    pack(first)
     pl.semaphore_wait(barrier, count - 1)
-    send(home)
+    send(first)
 
     def later(j, carry):
-        g = lax.rem(home + j, groups)
+        g = order(j)
         pack(g)
         send(g)
         return carry

time: 75.4 us -> 74.5 us (0.988); the launches traced: 74 us -> 74 us
  no operation moved by 1% of the time
where the time goes in v10:
time: 74.5 us; the launch traced here: 74 us
  Pallas kernels  62.5 us (84%)
  local copies, waits for them, and re-layouts  7.63 us (10%)
  matrix products  1.92 us (3%)
  other arithmetic  1.81 us (2%)
    pallas_call x1, Pallas kernels, exchange_slab(): pl.pallas_call(exchange_kernel, out_shape=(jax.ShapeDtypeStruct(data_shap...  45.5 us
    pallas_call x1, Pallas kernels, post_step(): pl.pallas_call(functools.partial(post_kernel, slab_count=slab_count), out...  16.9 us
    unnamed x15, local copies, waits for them, and re-layouts  3.28 us
    broadcast_in_dim x1, local copies, waits for them, and re-layouts, per_device(): return updated.transpose(0, 2, 1, 3)[None]  1.52 us

profile of v10, /device:TPU:7, one launch (start us, length us, event | category | flops | bytes accessed | tf_op | source)
XLA Modules:
  0.0 74.0 jit_solution(13273920779682624572)
XLA Ops:
  0.0 0.0 copy-start
  0.0 0.0 copy-start.2
  0.0 2.0 %copy.30 = bf16[128,8,2,128]{3,1,2,0:T(8,128)(2,1)} copy(bf16[128,8,2,128]{3,2,1,0:T(2,128)(2,1)} %bitcast.47) | data formatting | bytes 1048576
  2.0 0.0 copy-done.3
  2.0 0.0 copy-done.4
  2.0 0.1 pad.2.clone
  2.1 0.7 maximum_maximum_fusion.ids_ref
  2.8 0.0 copy-done.2
  2.8 0.5 convert_reduce_fusion
  3.3 0.6 bitcast_add_fusion.slot_ref
  3.9 45.5 %shard_map.73 = (bf16[64,32,256]{2,1,0:T(8,128)(2,1)}, s32[64,1,128]{2,1,0:T(1,128)}) custom-call(s32[1,1024]{1,0:T(1,128)} %bitcast_add_fusion.slot_ref, bf16[1024,256]{1,0:T(8,128)(2,1)} %bitcast.44, bf16[8,1024]{1,0:T(8,128)(2,1)} %maximum_maximum_fusion.ids_ref), custom_call_target="tpu_custom_call" | custom-call | tf_op jit(solution)/shard_map/pallas_call | solution.py:266
  49.5 0.9 %dynamic-slice_reduce_fusion = s32[64,32]{1,0:T(8,128)S(1)} fusion(s32[64,1,128]{2,1,0:T(1,128)} %get-tuple-element.7, s32[]{:T(128)S(6)} %select_n.3), kind=kLoop, calls=%fused_computation.14 | loop fusion | bytes 16388 | tf_op jit(solution)/shard_map/dynamic_slice | solution.py:311
  50.4 0.1 eq.34
  50.5 1.5 %copy.18 = bf16[256,2048]{1,0:T(8,128)(2,1)S(1)} copy(bf16[256,2048]{0,1:T(8,128)(2,1)} %bitcast.45) | data formatting | bytes 2097152 | tf_op jit(solution)/shard_map/dot_general | solution.py:316
  52.0 0.8 %fusion.6 = f32[64,2,8,128]{3,2,1,0:T(8,128)S(1)} fusion(bf16[2,128,2048,1]{2,1,0,3:T(8,128)(2,1)S(1)} %bitcast.46, s32[64,8]{1,0:T(8,128)S(1)} %multiply_add_fusion, s32[2048]{0:T(1024)S(1)} %eq.34), kind=kOutput, calls=%fused_computation.8 | convolution fusion | flops 537919488 | bytes 1583104 | tf_op jit(solution)/shard_map/dot_general | solution.py:316
  52.8 0.0 copy-start.1
  52.8 0.0 copy-start.5
  52.8 0.3 dot_general.15
  53.1 0.0 copy-done
  53.1 1.1 %convolution_bitcast_fusion.grid_ref = f32[2,2,32,128]{3,2,1,0:T(8,128)} fusion(bf16[1024,128,1,1]{1,0,3,2:T(8,128)(2,1)S(1)} %bitcast.43, f32[2,32,2,1024]{3,2,1,0:T(2,128)S(1)} %dot_general.15), kind=kOutput, calls=%fused_computation.9 | convolution fusion | flops 201326592 | bytes 851968 | tf_op jit(solution)/shard_map/dot_general | solution.py:318
  54.2 0.6 copy.31
  54.8 0.7 copy.21.scalars
  55.5 16.9 %shard_map.74 = f32[2,2,32,128]{3,2,1,0:T(8,128)} custom-call(f32[8,3]{1,0:T(8,128)} %copy.21.scalars, f32[2,2,32,128]{3,2,1,0:T(8,128)} %convolution_bitcast_fusion.grid_ref, f32[2,2,32,128]{3,2,1,0:T(8,128)} %bitcast.49), custom_call_target="tpu_custom_call" | custom-call | tf_op jit(solution)/shard_map/pallas_call | solution.py:143
  72.4 1.5 %copy.22 = f32[1,2,32,2,128]{4,3,2,1,0:T(2,128)} copy(f32[1,2,32,2,128]{4,2,3,1,0:T(8,128)} %bitcast.48) | data formatting | bytes 131072 | tf_op jit(solution)/shard_map/broadcast_in_dim | solution.py:328
  (8 shorter events, 0.0 us)
Async XLA Ops:
  0.0 53.1 %copy-start = (bf16[8,128,128]{2,1,0:T(8,128)(2,1)S(1)}, bf16[8,128,128]{2,1,0:T(8,128)(2,1)}, u32[]{:S(2)}) copy-start(bf16[8,128,128]{2,1,0:T(8,128)(2,1)} %param.11) | copy-start | bytes 786436
  0.0 2.0 %copy-start.3 = (s32[1,1024]{1,0:T(1,128)S(1)}, s32[1,1024]{1,0:T(1,128)}, u32[]{:S(2)}) copy-start(s32[1,1024]{1,0:T(1,128)} %param.9) | copy-start | bytes 12292
  0.0 2.0 %copy-start.4 = (s32[1,1024]{1,0:T(1,128)S(1)}, s32[1,1024]{1,0:T(1,128)}, u32[]{:S(2)}) copy-start(s32[1,1024]{1,0:T(1,128)} %param.10) | copy-start | bytes 12292
  0.0 2.8 %copy-start.2 = (s32[1,1024,1]{1,2,0:T(1,128)S(1)}, s32[1,1024,1]{1,2,0:T(1,128)}, u32[]{:S(2)}) copy-start(s32[1,1024,1]{1,2,0:T(1,128)} %param.8) | copy-start | bytes 12292
  52.8 1.4 %copy-start.1 = (f32[1,2,32,2,128]{4,3,2,1,0:T(2,128)S(1)}, f32[1,2,32,2,128]{4,3,2,1,0:T(2,128)}, u32[]{:S(2)}) copy-start(f32[1,2,32,2,128]{4,3,2,1,0:T(2,128)} %param.13) | copy-start | bytes 196612
  52.8 2.1 %copy-start.5 = (f32[8,3]{0,1:T(4,128)S(1)}, f32[8,3]{0,1:T(4,128)}, u32[]{:S(2)}) copy-start(f32[8,3]{0,1:T(4,128)} %param.12) | copy-start | bytes 292

commit v11 on v10

--- a/solution.py
+++ b/solution.py
@@ -42,10 +42,10 @@
 
 
 def post_kernel(
-    scalars, grid_ref, obj_ref, out_ref, halo, gathered, phase_buf, halo_send, halo_recv, send_sem, recv_sem,
-    slab_count,
+    scalars, grid_ref, obj_ref, out_ref, halo, gathered, phase_buf, partial_buf, mate_buf,
+    halo_send, halo_recv, send_sem, recv_sem, mate_send, mate_recv, slab_count, refl_count,
 ):
-    refl_count = gathered.shape[0]
+    share = gathered.shape[0]
     planes, rows, width = grid_ref.shape[0], grid_ref.shape[2], grid_ref.shape[3]
     me = lax.axis_index("slab")
     refl = lax.axis_index("refl")
@@ -54,10 +54,12 @@
     barrier = pltpu.get_barrier_semaphore()
     pl.semaphore_signal(barrier, 1, device_id=(refl, up), device_id_type=MESH)
     pl.semaphore_signal(barrier, 1, device_id=(refl, down), device_id_type=MESH)
-    for step in range(1, refl_count):
-        peer = lax.rem(refl + step, refl_count)
+    mate = refl + 1 - 2 * lax.rem(refl, 2)
+    for step in range(1, share):
+        peer = lax.rem(refl + 2 * step, refl_count)
         pl.semaphore_signal(barrier, 1, device_id=(peer, me), device_id_type=MESH)
-    pl.semaphore_wait(barrier, refl_count + 1)
+    pl.semaphore_signal(barrier, 1, device_id=(mate, me), device_id_type=MESH)
+    pl.semaphore_wait(barrier, share + 2)
     low_copy = pltpu.make_async_remote_copy(
         src_ref=grid_ref.at[planes - 1], dst_ref=halo.at[0], send_sem=halo_send.at[0],
         recv_sem=halo_recv.at[0], device_id=(refl, up), device_id_type=MESH,
@@ -109,29 +111,39 @@
         term_y, term_z = partial[p]
         phase_buf[p] = q0 * term_x + q1 * term_y + q2 * term_z
     copies = []
-    for step in range(1, refl_count):
-        peer = lax.rem(refl + step, refl_count)
+    for step in range(1, share):
+        peer = lax.rem(refl + 2 * step, refl_count)
         copy = pltpu.make_async_remote_copy(
-            src_ref=phase_buf, dst_ref=gathered.at[refl], send_sem=send_sem.at[step],
+            src_ref=phase_buf, dst_ref=gathered.at[step], send_sem=send_sem.at[step],
             recv_sem=recv_sem.at[step], device_id=(peer, me), device_id_type=MESH,
         )
         copy.start()
         copies.append(copy)
-    gathered[refl] = phase_buf[...]
+    gathered[0] = phase_buf[...]
     for copy in copies:
         copy.wait_send()
-    for step in range(1, refl_count):
-        source = lax.rem(refl + refl_count - step, refl_count)
+    for step in range(1, share):
+        source = lax.rem(refl + refl_count - 2 * step, refl_count)
         pltpu.make_async_remote_copy(
-            src_ref=phase_buf, dst_ref=gathered.at[source], send_sem=send_sem.at[step],
+            src_ref=phase_buf, dst_ref=gathered.at[step], send_sem=send_sem.at[step],
             recv_sem=recv_sem.at[step], device_id=(source, me), device_id_type=MESH,
         ).wait_recv()
+
     def weight(r):
         return scalars[r, 0] * d0 + scalars[r, 1] * d1 + scalars[r, 2] * d2
 
-    shift = weight(0) * gathered[0]
-    for r in range(1, refl_count):
-        shift = shift + weight(r) * gathered[r]
+    own = weight(refl) * gathered[0]
+    for step in range(1, share):
+        own = own + weight(lax.rem(refl + refl_count - 2 * step, refl_count)) * gathered[step]
+    partial_buf[...] = own
+    to_mate = pltpu.make_async_remote_copy(
+        src_ref=partial_buf, dst_ref=mate_buf, send_sem=mate_send.at[0], recv_sem=mate_recv.at[0],
+        device_id=(mate, me), device_id_type=MESH,
+    )
+    to_mate.start()
+    to_mate.wait_send()
+    to_mate.wait_recv()
+    shift = partial_buf[...] - mate_buf[...]
     for p in range(planes):
         obj_re, obj_im = obj_ref[p, 0], obj_ref[p, 1]
         out_ref[p, 0] = obj_re - 0.5 * (grid_ref[p, 0] - obj_im * shift[p])
@@ -140,20 +152,25 @@
 
 def post_step(scalars, grid, obj, slab_count, refl_count):
     planes, _, rows, width = grid.shape
+    share = refl_count // 2
     return pl.pallas_call(
-        functools.partial(post_kernel, slab_count=slab_count),
+        functools.partial(post_kernel, slab_count=slab_count, refl_count=refl_count),
         out_shape=jax.ShapeDtypeStruct(grid.shape, jnp.float32),
         in_specs=[pl.BlockSpec(memory_space=pltpu.SMEM)]
         + [pl.BlockSpec(memory_space=pltpu.VMEM)] * 2,
         out_specs=pl.BlockSpec(memory_space=pltpu.VMEM),
         scratch_shapes=[
             pltpu.VMEM((2, 2, rows, width), jnp.float32),
-            pltpu.VMEM((refl_count, planes, rows, width), jnp.float32),
+            pltpu.VMEM((share, planes, rows, width), jnp.float32),
+            pltpu.VMEM((planes, rows, width), jnp.float32),
+            pltpu.VMEM((planes, rows, width), jnp.float32),
             pltpu.VMEM((planes, rows, width), jnp.float32),
             pltpu.SemaphoreType.DMA((2,)),
             pltpu.SemaphoreType.DMA((2,)),
-            pltpu.SemaphoreType.DMA((refl_count,)),
-            pltpu.SemaphoreType.DMA((refl_count,)),
+            pltpu.SemaphoreType.DMA((share,)),
+            pltpu.SemaphoreType.DMA((share,)),
+            pltpu.SemaphoreType.DMA((1,)),
+            pltpu.SemaphoreType.DMA((1,)),
         ],
         compiler_params=pltpu.CompilerParams(collective_id=0, has_side_effects=True),
     )(scalars, grid, obj)

time: 74.5 us -> 74.8 us (level)
  no operation moved by 1% of the time
where the time goes in v11:
time: 74.8 us; the launch traced here: 74 us
  Pallas kernels  62.5 us (84%)
  local copies, waits for them, and re-layouts  7.63 us (10%)
  matrix products  1.92 us (3%)
  other arithmetic  1.81 us (2%)
    pallas_call x1, Pallas kernels, exchange_slab(): pl.pallas_call(exchange_kernel, out_shape=(jax.ShapeDtypeStruct(data_shap...  45.5 us
    pallas_call x1, Pallas kernels, post_step(): pl.pallas_call(functools.partial(post_kernel, slab_count=slab_count, refl...  16.9 us
    unnamed x15, local copies, waits for them, and re-layouts  3.28 us
    broadcast_in_dim x1, local copies, waits for them, and re-layouts, per_device(): return updated.transpose(0, 2, 1, 3)[None]  1.52 us

profile of v11, /device:TPU:7, one launch (start us, length us, event | category | flops | bytes accessed | tf_op | source)
XLA Modules:
  0.0 74.0 jit_solution(18217337597305224657)
XLA Ops:
  0.0 0.0 copy-start
  0.0 0.0 copy-start.2
  0.0 2.0 %copy.30 = bf16[128,8,2,128]{3,1,2,0:T(8,128)(2,1)} copy(bf16[128,8,2,128]{3,2,1,0:T(2,128)(2,1)} %bitcast.47) | data formatting | bytes 1048576
  2.0 0.0 copy-done.3
  2.0 0.0 copy-done.4
  2.0 0.1 pad.2.clone
  2.1 0.7 maximum_maximum_fusion.ids_ref
  2.8 0.0 copy-done.2
  2.8 0.5 convert_reduce_fusion
  3.3 0.6 bitcast_add_fusion.slot_ref
  3.9 45.5 %shard_map.73 = (bf16[64,32,256]{2,1,0:T(8,128)(2,1)}, s32[64,1,128]{2,1,0:T(1,128)}) custom-call(s32[1,1024]{1,0:T(1,128)} %bitcast_add_fusion.slot_ref, bf16[1024,256]{1,0:T(8,128)(2,1)} %bitcast.44, bf16[8,1024]{1,0:T(8,128)(2,1)} %maximum_maximum_fusion.ids_ref), custom_call_target="tpu_custom_call" | custom-call | tf_op jit(solution)/shard_map/pallas_call | solution.py:283
  49.5 0.9 %dynamic-slice_reduce_fusion = s32[64,32]{1,0:T(8,128)S(1)} fusion(s32[64,1,128]{2,1,0:T(1,128)} %get-tuple-element.7, s32[]{:T(128)S(6)} %select_n.3), kind=kLoop, calls=%fused_computation.14 | loop fusion | bytes 16388 | tf_op jit(solution)/shard_map/dynamic_slice | solution.py:328
  50.4 0.1 eq.34
  50.5 1.5 %copy.18 = bf16[256,2048]{1,0:T(8,128)(2,1)S(1)} copy(bf16[256,2048]{0,1:T(8,128)(2,1)} %bitcast.45) | data formatting | bytes 2097152 | tf_op jit(solution)/shard_map/dot_general | solution.py:333
  52.0 0.8 %fusion.6 = f32[64,2,8,128]{3,2,1,0:T(8,128)S(1)} fusion(bf16[2,128,2048,1]{2,1,0,3:T(8,128)(2,1)S(1)} %bitcast.46, s32[64,8]{1,0:T(8,128)S(1)} %multiply_add_fusion, s32[2048]{0:T(1024)S(1)} %eq.34), kind=kOutput, calls=%fused_computation.8 | convolution fusion | flops 537919488 | bytes 1583104 | tf_op jit(solution)/shard_map/dot_general | solution.py:333
  52.8 0.0 copy-start.1
  52.8 0.0 copy-start.5
  52.8 0.3 dot_general.15
  53.1 0.0 copy-done
  53.1 1.1 %convolution_bitcast_fusion.grid_ref = f32[2,2,32,128]{3,2,1,0:T(8,128)} fusion(bf16[1024,128,1,1]{1,0,3,2:T(8,128)(2,1)S(1)} %bitcast.43, f32[2,32,2,1024]{3,2,1,0:T(2,128)S(1)} %dot_general.15), kind=kOutput, calls=%fused_computation.9 | convolution fusion | flops 201326592 | bytes 851968 | tf_op jit(solution)/shard_map/dot_general | solution.py:335
  54.2 0.6 copy.31
  54.8 0.7 copy.21.scalars
  55.5 16.9 %shard_map.74 = f32[2,2,32,128]{3,2,1,0:T(8,128)} custom-call(f32[8,3]{1,0:T(8,128)} %copy.21.scalars, f32[2,2,32,128]{3,2,1,0:T(8,128)} %convolution_bitcast_fusion.grid_ref, f32[2,2,32,128]{3,2,1,0:T(8,128)} %bitcast.49), custom_call_target="tpu_custom_call" | custom-call | tf_op jit(solution)/shard_map/pallas_call | solution.py:156
  72.5 1.5 %copy.22 = f32[1,2,32,2,128]{4,3,2,1,0:T(2,128)} copy(f32[1,2,32,2,128]{4,2,3,1,0:T(8,128)} %bitcast.48) | data formatting | bytes 131072 | tf_op jit(solution)/shard_map/broadcast_in_dim | solution.py:345
  (8 shorter events, 0.0 us)
Async XLA Ops:
  0.0 53.1 %copy-start = (bf16[8,128,128]{2,1,0:T(8,128)(2,1)S(1)}, bf16[8,128,128]{2,1,0:T(8,128)(2,1)}, u32[]{:S(2)}) copy-start(bf16[8,128,128]{2,1,0:T(8,128)(2,1)} %param.11) | copy-start | bytes 786436
  0.0 2.0 %copy-start.3 = (s32[1,1024]{1,0:T(1,128)S(1)}, s32[1,1024]{1,0:T(1,128)}, u32[]{:S(2)}) copy-start(s32[1,1024]{1,0:T(1,128)} %param.9) | copy-start | bytes 12292
  0.0 2.0 %copy-start.4 = (s32[1,1024]{1,0:T(1,128)S(1)}, s32[1,1024]{1,0:T(1,128)}, u32[]{:S(2)}) copy-start(s32[1,1024]{1,0:T(1,128)} %param.10) | copy-start | bytes 12292
  0.0 2.8 %copy-start.2 = (s32[1,1024,1]{1,2,0:T(1,128)S(1)}, s32[1,1024,1]{1,2,0:T(1,128)}, u32[]{:S(2)}) copy-start(s32[1,1024,1]{1,2,0:T(1,128)} %param.8) | copy-start | bytes 12292
  52.8 1.4 %copy-start.1 = (f32[1,2,32,2,128]{4,3,2,1,0:T(2,128)S(1)}, f32[1,2,32,2,128]{4,3,2,1,0:T(2,128)}, u32[]{:S(2)}) copy-start(f32[1,2,32,2,128]{4,3,2,1,0:T(2,128)} %param.13) | copy-start | bytes 196612
  52.8 2.1 %copy-start.5 = (f32[8,3]{0,1:T(4,128)S(1)}, f32[8,3]{0,1:T(4,128)}, u32[]{:S(2)}) copy-start(f32[8,3]{0,1:T(4,128)} %param.12) | copy-start | bytes 292

commit v12 on v10

--- a/solution.py
+++ b/solution.py
@@ -42,11 +42,29 @@
 
 
 def post_kernel(
-    scalars, grid_ref, obj_ref, out_ref, halo, gathered, phase_buf, halo_send, halo_recv, send_sem, recv_sem,
-    slab_count,
+    scalars, code_ref, rows_ref, kernels_ref, obj_ref, out_ref, grid_ref, halo, gathered, phase_buf,
+    halo_send, halo_recv, send_sem, recv_sem, slab_count,
 ):
     refl_count = gathered.shape[0]
     planes, rows, width = grid_ref.shape[0], grid_ref.shape[2], grid_ref.shape[3]
+    kernel_count = kernels_ref.shape[0]
+    blocks = planes * rows
+    chosen = (
+        code_ref[...] == lax.broadcasted_iota(jnp.int32, (kernel_count * blocks, code_ref.shape[1]), 0)
+    ).astype(jnp.bfloat16)
+    summed = jnp.dot(chosen, rows_ref[...], preferred_element_type=jnp.float32)
+    for c in range(2):
+        total = None
+        for k in range(kernel_count):
+            part = summed[k * blocks : (k + 1) * blocks, c * width : (c + 1) * width]
+            weights = kernels_ref[k]
+            for _ in range(3):
+                piece = part.astype(jnp.bfloat16)
+                term = jnp.dot(piece, weights, preferred_element_type=jnp.float32)
+                total = term if total is None else total + term
+                part = part - piece.astype(jnp.float32)
+        for p in range(planes):
+            grid_ref[p, c] = total[p * rows : (p + 1) * rows]
     me = lax.axis_index("slab")
     refl = lax.axis_index("refl")
     up = lax.rem(me + 1, slab_count)
@@ -138,25 +156,26 @@
         out_ref[p, 1] = obj_im - 0.5 * (grid_ref[p, 1] + obj_re * shift[p])
 
 
-def post_step(scalars, grid, obj, slab_count, refl_count):
-    planes, _, rows, width = grid.shape
+def post_step(scalars, code_row, rows, kernels, obj, slab_count, refl_count):
+    planes, _, rows_per, width = obj.shape
     return pl.pallas_call(
         functools.partial(post_kernel, slab_count=slab_count),
-        out_shape=jax.ShapeDtypeStruct(grid.shape, jnp.float32),
+        out_shape=jax.ShapeDtypeStruct(obj.shape, jnp.float32),
         in_specs=[pl.BlockSpec(memory_space=pltpu.SMEM)]
-        + [pl.BlockSpec(memory_space=pltpu.VMEM)] * 2,
+        + [pl.BlockSpec(memory_space=pltpu.VMEM)] * 4,
         out_specs=pl.BlockSpec(memory_space=pltpu.VMEM),
         scratch_shapes=[
-            pltpu.VMEM((2, 2, rows, width), jnp.float32),
-            pltpu.VMEM((refl_count, planes, rows, width), jnp.float32),
-            pltpu.VMEM((planes, rows, width), jnp.float32),
+            pltpu.VMEM(obj.shape, jnp.float32),
+            pltpu.VMEM((2, 2, rows_per, width), jnp.float32),
+            pltpu.VMEM((refl_count, planes, rows_per, width), jnp.float32),
+            pltpu.VMEM((planes, rows_per, width), jnp.float32),
             pltpu.SemaphoreType.DMA((2,)),
             pltpu.SemaphoreType.DMA((2,)),
             pltpu.SemaphoreType.DMA((refl_count,)),
             pltpu.SemaphoreType.DMA((refl_count,)),
         ],
         compiler_params=pltpu.CompilerParams(collective_id=0, has_side_effects=True),
-    )(scalars, grid, obj)
+    )(scalars, code_row, rows, kernels, obj)
 
 
 def exchange_kernel(
@@ -309,22 +328,10 @@
     rows = got.reshape(row_total, row_width)
     offset = lax.rem(lax.axis_index("slab"), 4) * capacity
     got_codes = lax.dynamic_slice_in_dim(got_code[:, 0, :], offset, capacity, axis=1).reshape(row_total)
-    chosen = (
-        got_codes[None, :]
-        == lax.broadcasted_iota(jnp.int32, (block_count * kernel_count, row_total), 0)
-    ).astype(jnp.bfloat16)
-    summed = jnp.dot(chosen, rows, preferred_element_type=jnp.float32)
-    summed = summed.reshape(block_count, kernel_count, 2, tile_width).transpose(0, 2, 1, 3)
-    gridded = jnp.dot(
-        summed.reshape(block_count * 2, kernel_count * tile_width),
-        kernels.astype(jnp.float32).reshape(kernel_count * tile_width, tile_width),
-        precision=lax.Precision.HIGHEST,
-        preferred_element_type=jnp.float32,
-    )
-    gridded = gridded.reshape(plane_count, row_count, 2, tile_width).transpose(0, 2, 1, 3)
+    code_row = (lax.rem(got_codes, kernel_count) * block_count + got_codes // kernel_count)[None, :]
     refl_count = bragg_vectors.shape[0]
     obj = object_field[0].transpose(0, 2, 1, 3)
-    updated = post_step(bragg_vectors, gridded, obj, slab_count, refl_count)
+    updated = post_step(bragg_vectors, code_row, rows, kernels, obj, slab_count, refl_count)
     return updated.transpose(0, 2, 1, 3)[None]
 
 

time: 74.5 us -> 73.7 us (0.989)
  Pallas kernels: 62.5 us -> 64.8 us
  matrix products: 1.92 us -> 0 us
  local copies, waits for them, and re-layouts: 7.63 us -> 5.92 us
    pallas_call x1, Pallas kernels: 16.9 us -> 19.2 us  [post_step(): pl.pallas_call(functools.partial(post_kernel, slab_count=slab_count), out...]
    dot_general x2 -> x0, matrix products: 1.92 us -> none  [the longest x1 1.13 us: per_device(): jnp.dot(summed.reshape(block_count * 2, kernel_count * tile_width), kerne...]
    dot_general x2 -> x0, local copies, waits for them, and re-layouts: 1.76 us -> none  [the longest x1 1.48 us: per_device(): summed = jnp.dot(chosen, rows, preferred_element_type=jnp.float32)]
    unnamed x15 -> x13, local copies, waits for them, and re-layouts: 3.28 us -> 3.32 us
where the time goes in v12:
time: 73.7 us; the launch traced here: 73.2 us
  Pallas kernels  64.8 us (88%)
  local copies, waits for them, and re-layouts  5.92 us (8%)
  other arithmetic  2.46 us (3%)
    pallas_call x1, Pallas kernels, exchange_slab(): pl.pallas_call(exchange_kernel, out_shape=(jax.ShapeDtypeStruct(data_shap...  45.6 us
    pallas_call x1, Pallas kernels, post_step(): pl.pallas_call(functools.partial(post_kernel, slab_count=slab_count), out...  19.2 us
    unnamed x13, local copies, waits for them, and re-layouts  3.32 us
    broadcast_in_dim x1, local copies, waits for them, and re-layouts, per_device(): return updated.transpose(0, 2, 1, 3)[None]  1.52 us

profile of v12, /device:TPU:7, one launch (start us, length us, event | category | flops | bytes accessed | tf_op | source)
XLA Modules:
  0.0 73.2 jit_solution(9234113153835218640)
XLA Ops:
  0.0 0.0 copy-start.2
  0.0 0.0 copy-start.3
  0.0 0.0 copy-start.1
  0.0 0.0 copy-start
  0.0 0.0 copy-start.4
  0.0 2.0 %copy.20 = bf16[128,8,2,128]{3,1,2,0:T(8,128)(2,1)} copy(bf16[128,8,2,128]{3,2,1,0:T(2,128)(2,1)} %bitcast.20) | data formatting | bytes 1048576
  2.0 0.0 copy-done.2
  2.0 0.0 copy-done.3
  2.1 0.1 pad.2.clone
  2.2 0.7 maximum_maximum_fusion.ids_ref
  2.8 0.0 copy-done.1
  2.8 0.5 convert_reduce_fusion
  3.4 0.6 bitcast_add_fusion.slot_ref
  4.0 45.6 %shard_map.73 = (bf16[64,32,256]{2,1,0:T(8,128)(2,1)}, s32[64,1,128]{2,1,0:T(1,128)}) custom-call(s32[1,1024]{1,0:T(1,128)} %bitcast_add_fusion.slot_ref, bf16[1024,256]{1,0:T(8,128)(2,1)} %bitcast.18, bf16[8,1024]{1,0:T(8,128)(2,1)} %maximum_maximum_fusion.ids_ref), custom_call_target="tpu_custom_call" | custom-call | tf_op jit(solution)/shard_map/pallas_call | solution.py:285
  49.5 0.9 %dynamic-slice_reduce_fusion = s32[64,32]{1,0:T(8,128)S(1)} fusion(s32[64,1,128]{2,1,0:T(1,128)} %get-tuple-element.7, s32[]{:T(128)S(6)} %select_n.15), kind=kLoop, calls=%fused_computation.5 | loop fusion | bytes 16388 | tf_op jit(solution)/shard_map/dynamic_slice | solution.py:330
  50.5 0.1 reshape.105
  50.5 0.6 multiply_add_fusion.code_ref
  51.2 0.0 copy-done
  51.2 0.6 copy.21
  51.8 0.0 copy-done.4
  51.8 0.7 copy.15.scalars
  52.5 19.2 %shard_map.74 = f32[2,2,32,128]{3,2,1,0:T(8,128)} custom-call(f32[8,3]{1,0:T(8,128)} %copy.15.scalars, s32[1,2048]{1,0:T(1,128)} %multiply_add_fusion.code_ref, bf16[2048,256]{1,0:T(8,128)(2,1)} %bitcast.19, bf16[8,128,128]{2,1,0:T(8,128)(2,1)} %kernels_ref.1, f32[2,2,32,128]{3,2,1,0:T(8,128)} %bitcast.22), custom_call_target="tpu_custom_call" | custom-call | tf_op jit(solution)/shard_map/pallas_call | solution.py:161
  71.7 1.5 %copy.16 = f32[1,2,32,2,128]{4,3,2,1,0:T(2,128)} copy(f32[1,2,32,2,128]{4,2,3,1,0:T(8,128)} %bitcast.21) | data formatting | bytes 131072 | tf_op jit(solution)/shard_map/broadcast_in_dim | solution.py:335
  (3 shorter events, 0.0 us)
Async XLA Ops:
  0.0 2.0 %copy-start.2 = (s32[1,1024]{1,0:T(1,128)S(1)}, s32[1,1024]{1,0:T(1,128)}, u32[]{:S(2)}) copy-start(s32[1,1024]{1,0:T(1,128)} %param.9) | copy-start | bytes 12292
  0.0 2.0 %copy-start.3 = (s32[1,1024]{1,0:T(1,128)S(1)}, s32[1,1024]{1,0:T(1,128)}, u32[]{:S(2)}) copy-start(s32[1,1024]{1,0:T(1,128)} %param.10) | copy-start | bytes 12292
  0.0 2.8 %copy-start.1 = (s32[1,1024,1]{1,2,0:T(1,128)S(1)}, s32[1,1024,1]{1,2,0:T(1,128)}, u32[]{:S(2)}) copy-start(s32[1,1024,1]{1,2,0:T(1,128)} %param.8) | copy-start | bytes 12292
  0.0 51.2 %copy-start = (f32[1,2,32,2,128]{4,3,2,1,0:T(2,128)S(1)}, f32[1,2,32,2,128]{4,3,2,1,0:T(2,128)}, u32[]{:S(2)}) copy-start(f32[1,2,32,2,128]{4,3,2,1,0:T(2,128)} %param.13) | copy-start | bytes 196612
  0.0 51.8 %copy-start.4 = (f32[8,3]{0,1:T(4,128)S(1)}, f32[8,3]{0,1:T(4,128)}, u32[]{:S(2)}) copy-start(f32[8,3]{0,1:T(4,128)} %param.12) | copy-start | bytes 292

commit v13 on v12

--- a/solution.py
+++ b/solution.py
@@ -106,7 +106,7 @@
     d2 = q2 - scalars[mate, 2]
     partial = []
     for p in range(planes):
-        obj_re, obj_im = obj_ref[p, 0], obj_ref[p, 1]
+        obj_re, obj_im = obj_ref[p, :, 0, :], obj_ref[p, :, 1, :]
         term_y = obj_re * along_y(grid_ref[p, 1]) - obj_im * along_y(grid_ref[p, 0])
         term_z = obj_re * along_w(grid_ref[p, 1]) - obj_im * along_w(grid_ref[p, 0])
         partial.append((term_y, term_z))
@@ -117,7 +117,7 @@
     has_low = me > 0
     has_high = me < slab_count - 1
     for p in range(planes):
-        obj_re, obj_im = obj_ref[p, 0], obj_ref[p, 1]
+        obj_re, obj_im = obj_ref[p, :, 0, :], obj_ref[p, :, 1, :]
         grad = []
         for c in range(2):
             ahead = grid_ref[p + 1, c] if p + 1 < planes else jnp.where(has_high, halo[1, c], 0.0)
@@ -151,13 +151,14 @@
     for r in range(1, refl_count):
         shift = shift + weight(r) * gathered[r]
     for p in range(planes):
-        obj_re, obj_im = obj_ref[p, 0], obj_ref[p, 1]
-        out_ref[p, 0] = obj_re - 0.5 * (grid_ref[p, 0] - obj_im * shift[p])
-        out_ref[p, 1] = obj_im - 0.5 * (grid_ref[p, 1] + obj_re * shift[p])
+        obj_re, obj_im = obj_ref[p, :, 0, :], obj_ref[p, :, 1, :]
+        new_re = obj_re - 0.5 * (grid_ref[p, 0] - obj_im * shift[p])
+        new_im = obj_im - 0.5 * (grid_ref[p, 1] + obj_re * shift[p])
+        out_ref[p] = jnp.stack([new_re, new_im], axis=1)
 
 
 def post_step(scalars, code_row, rows, kernels, obj, slab_count, refl_count):
-    planes, _, rows_per, width = obj.shape
+    planes, rows_per, _, width = obj.shape
     return pl.pallas_call(
         functools.partial(post_kernel, slab_count=slab_count),
         out_shape=jax.ShapeDtypeStruct(obj.shape, jnp.float32),
@@ -165,7 +166,7 @@
         + [pl.BlockSpec(memory_space=pltpu.VMEM)] * 4,
         out_specs=pl.BlockSpec(memory_space=pltpu.VMEM),
         scratch_shapes=[
-            pltpu.VMEM(obj.shape, jnp.float32),
+            pltpu.VMEM((planes, 2, rows_per, width), jnp.float32),
             pltpu.VMEM((2, 2, rows_per, width), jnp.float32),
             pltpu.VMEM((refl_count, planes, rows_per, width), jnp.float32),
             pltpu.VMEM((planes, rows_per, width), jnp.float32),
@@ -330,9 +331,9 @@
     got_codes = lax.dynamic_slice_in_dim(got_code[:, 0, :], offset, capacity, axis=1).reshape(row_total)
     code_row = (lax.rem(got_codes, kernel_count) * block_count + got_codes // kernel_count)[None, :]
     refl_count = bragg_vectors.shape[0]
-    obj = object_field[0].transpose(0, 2, 1, 3)
+    obj = object_field[0]
     updated = post_step(bragg_vectors, code_row, rows, kernels, obj, slab_count, refl_count)
-    return updated.transpose(0, 2, 1, 3)[None]
+    return updated[None]
 
 
 def solution(mesh):

time: 73.7 us -> 73 us (level)
    broadcast_in_dim x1 -> x0, local copies, waits for them, and re-layouts: 1.52 us -> none  [per_device(): return updated.transpose(0, 2, 1, 3)[None]]
    unnamed x13 -> x11, local copies, waits for them, and re-layouts: 3.32 us -> 4.13 us
where the time goes in v13:
time: 73 us; the launch traced here: 72.6 us
  Pallas kernels  64.9 us (89%)
  local copies, waits for them, and re-layouts  5.22 us (7%)
  other arithmetic  2.46 us (3%)
    pallas_call x1, Pallas kernels, exchange_slab(): pl.pallas_call(exchange_kernel, out_shape=(jax.ShapeDtypeStruct(data_shap...  45.6 us
    pallas_call x1, Pallas kernels, post_step(): pl.pallas_call(functools.partial(post_kernel, slab_count=slab_count), out...  19.3 us
    unnamed x11, local copies, waits for them, and re-layouts  4.13 us

profile of v13, /device:TPU:7, one launch (start us, length us, event | category | flops | bytes accessed | tf_op | source)
XLA Modules:
  0.0 72.6 jit_solution(10479612521950814207)
XLA Ops:
  0.0 0.0 copy-start.1
  0.0 0.0 copy-start.2
  0.0 0.0 copy-start
  0.0 0.0 copy-start.3
  0.0 2.0 %copy.13 = bf16[128,8,2,128]{3,1,2,0:T(8,128)(2,1)} copy(bf16[128,8,2,128]{3,2,1,0:T(2,128)(2,1)} %bitcast.14) | data formatting | bytes 1048576
  2.0 0.0 copy-done.1
  2.0 0.0 copy-done.2
  2.1 0.1 pad.2.clone
  2.1 0.7 maximum_maximum_fusion.ids_ref
  2.8 0.0 copy-done
  2.8 0.5 convert_reduce_fusion
  3.3 0.6 bitcast_add_fusion.slot_ref
  3.9 45.6 %shard_map.73 = (bf16[64,32,256]{2,1,0:T(8,128)(2,1)}, s32[64,1,128]{2,1,0:T(1,128)}) custom-call(s32[1,1024]{1,0:T(1,128)} %bitcast_add_fusion.slot_ref, bf16[1024,256]{1,0:T(8,128)(2,1)} %bitcast.12, bf16[8,1024]{1,0:T(8,128)(2,1)} %maximum_maximum_fusion.ids_ref), custom_call_target="tpu_custom_call" | custom-call | tf_op jit(solution)/shard_map/pallas_call | solution.py:286
  49.5 0.9 %dynamic-slice_reduce_fusion = s32[64,32]{1,0:T(8,128)S(1)} fusion(s32[64,1,128]{2,1,0:T(1,128)} %get-tuple-element.7, s32[]{:T(128)S(6)} %select_n.15), kind=kLoop, calls=%fused_computation.4 | loop fusion | bytes 16388 | tf_op jit(solution)/shard_map/dynamic_slice | solution.py:331
  50.4 0.1 reshape.105
  50.5 0.6 multiply_add_fusion.code_ref
  51.2 0.0 copy-done.3
  51.2 0.7 copy.10.scalars
  51.8 19.3 %shard_map.74 = f32[2,32,2,128]{3,2,1,0:T(2,128)} custom-call(f32[8,3]{1,0:T(8,128)} %copy.10.scalars, s32[1,2048]{1,0:T(1,128)} %multiply_add_fusion.code_ref, bf16[2048,256]{1,0:T(8,128)(2,1)} %bitcast.13, bf16[8,128,128]{2,1,0:T(8,128)(2,1)} %kernels_ref.1, f32[2,32,2,128]{3,2,1,0:T(2,128)} %bitcast.16), custom_call_target="tpu_custom_call" | custom-call | tf_op jit(solution)/shard_map/pallas_call | solution.py:162
  71.1 1.5 %copy.15 = f32[1,2,32,2,128]{4,3,2,1,0:T(2,128)} copy(f32[1,2,32,2,128]{4,3,2,1,0:T(2,128)} %bitcast.15) | data formatting | bytes 131072
  (3 shorter events, 0.0 us)
Async XLA Ops:
  0.0 2.0 %copy-start.1 = (s32[1,1024]{1,0:T(1,128)S(1)}, s32[1,1024]{1,0:T(1,128)}, u32[]{:S(2)}) copy-start(s32[1,1024]{1,0:T(1,128)} %param.9) | copy-start | bytes 12292
  0.0 2.0 %copy-start.2 = (s32[1,1024]{1,0:T(1,128)S(1)}, s32[1,1024]{1,0:T(1,128)}, u32[]{:S(2)}) copy-start(s32[1,1024]{1,0:T(1,128)} %param.10) | copy-start | bytes 12292
  0.0 2.8 %copy-start = (s32[1,1024,1]{1,2,0:T(1,128)S(1)}, s32[1,1024,1]{1,2,0:T(1,128)}, u32[]{:S(2)}) copy-start(s32[1,1024,1]{1,2,0:T(1,128)} %param.8) | copy-start | bytes 12292
  0.0 51.1 %copy-start.3 = (f32[8,3]{0,1:T(4,128)S(1)}, f32[8,3]{0,1:T(4,128)}, u32[]{:S(2)}) copy-start(f32[8,3]{0,1:T(4,128)} %param.12) | copy-start | bytes 292

commit v14 on v13

--- a/solution.py
+++ b/solution.py
@@ -100,10 +100,10 @@
         return 0.5 * (after - before)
 
     mate = refl + 1 - 2 * lax.rem(refl, 2)
-    q0, q1, q2 = scalars[refl, 0], scalars[refl, 1], scalars[refl, 2]
-    d0 = q0 - scalars[mate, 0]
-    d1 = q1 - scalars[mate, 1]
-    d2 = q2 - scalars[mate, 2]
+    q0, q1, q2 = scalars[0, refl], scalars[1, refl], scalars[2, refl]
+    d0 = q0 - scalars[0, mate]
+    d1 = q1 - scalars[1, mate]
+    d2 = q2 - scalars[2, mate]
     partial = []
     for p in range(planes):
         obj_re, obj_im = obj_ref[p, :, 0, :], obj_ref[p, :, 1, :]
@@ -145,7 +145,7 @@
             recv_sem=recv_sem.at[step], device_id=(source, me), device_id_type=MESH,
         ).wait_recv()
     def weight(r):
-        return scalars[r, 0] * d0 + scalars[r, 1] * d1 + scalars[r, 2] * d2
+        return scalars[0, r] * d0 + scalars[1, r] * d1 + scalars[2, r] * d2
 
     shift = weight(0) * gathered[0]
     for r in range(1, refl_count):
@@ -332,7 +332,7 @@
     code_row = (lax.rem(got_codes, kernel_count) * block_count + got_codes // kernel_count)[None, :]
     refl_count = bragg_vectors.shape[0]
     obj = object_field[0]
-    updated = post_step(bragg_vectors, code_row, rows, kernels, obj, slab_count, refl_count)
+    updated = post_step(bragg_vectors.T, code_row, rows, kernels, obj, slab_count, refl_count)
     return updated[None]
 
 

time: 73 us -> 73.9 us (1.012)
  other arithmetic: 2.46 us -> 3.9 us
    reduce_sum x1, other arithmetic: 0.52 us -> 1.28 us  [per_device(): slots = jnp.sum(same.astype(jnp.int32), axis=1)]
    unnamed x11 -> x6, local copies, waits for them, and re-layouts: 4.13 us -> 3.42 us
where the time goes in v14:
time: 73.9 us; the launch traced here: 73.3 us
  Pallas kernels  64.9 us (88%)
  local copies, waits for them, and re-layouts  4.5 us (6%)
  other arithmetic  3.9 us (5%)
    pallas_call x1, Pallas kernels, exchange_slab(): pl.pallas_call(exchange_kernel, out_shape=(jax.ShapeDtypeStruct(data_shap...  45.6 us
    pallas_call x1, Pallas kernels, post_step(): pl.pallas_call(functools.partial(post_kernel, slab_count=slab_count), out...  19.3 us
    unnamed x6, local copies, waits for them, and re-layouts  3.42 us

profile of v14, /device:TPU:7, one launch (start us, length us, event | category | flops | bytes accessed | tf_op | source)
XLA Modules:
  0.0 73.3 jit_solution(7873052692380305197)
XLA Ops:
  0.0 0.0 copy-start
  0.0 0.0 copy-start.1
  0.0 1.3 %convert_reduce_fusion = s32[1024]{0:T(1024)S(1)} fusion(s32[1024]{0:T(1024)} %bitcast.18), kind=kLoop, calls=%fused_computation | loop fusion | flops 5241856 | bytes 8192 | tf_op jit(solution)/shard_map/reduce_sum | solution.py:322
  1.3 1.3 %bitcast_add_fusion.slot_ref = s32[1,1024]{1,0:T(1,128)} fusion(s32[1,1024]{1,0:T(1,128)S(1)} %bitcast.19, s32[1,1024,1]{1,2,0:T(1,128)} %param.8), kind=kLoop, calls=%fused_computation.11 | loop fusion | flops 2048 | bytes 12288 | tf_op jit(solution)/shard_map/add | solution.py:323
  2.6 1.9 %copy.10 = bf16[128,8,2,128]{3,1,2,0:T(8,128)(2,1)} copy(bf16[128,8,2,128]{3,2,1,0:T(2,128)(2,1)} %bitcast.15) | data formatting | bytes 1048576
  4.5 0.0 copy-done
  4.5 0.0 copy-done.1
  4.6 0.1 pad.2.clone
  4.6 0.7 maximum_maximum_fusion.ids_ref
  5.3 45.6 %shard_map.73 = (bf16[64,32,256]{2,1,0:T(8,128)(2,1)}, s32[64,1,128]{2,1,0:T(1,128)}) custom-call(s32[1,1024]{1,0:T(1,128)} %bitcast_add_fusion.slot_ref, bf16[1024,256]{1,0:T(8,128)(2,1)} %bitcast.13, bf16[8,1024]{1,0:T(8,128)(2,1)} %maximum_maximum_fusion.ids_ref), custom_call_target="tpu_custom_call" | custom-call | tf_op jit(solution)/shard_map/pallas_call | solution.py:286
  50.9 0.9 %dynamic-slice_reduce_fusion = s32[64,32]{1,0:T(8,128)S(1)} fusion(s32[64,1,128]{2,1,0:T(1,128)} %get-tuple-element.7, s32[]{:T(128)S(6)} %select_n.15), kind=kLoop, calls=%fused_computation.4 | loop fusion | bytes 16388 | tf_op jit(solution)/shard_map/dynamic_slice | solution.py:331
  51.8 0.1 reshape.105
  51.9 0.6 multiply_add_fusion.code_ref
  52.5 19.3 %shard_map.74 = f32[2,32,2,128]{3,2,1,0:T(2,128)} custom-call(f32[3,8]{1,0:T(4,128)} %bitcast.20, s32[1,2048]{1,0:T(1,128)} %multiply_add_fusion.code_ref, bf16[2048,256]{1,0:T(8,128)(2,1)} %bitcast.14, bf16[8,128,128]{2,1,0:T(8,128)(2,1)} %kernels_ref.1, f32[2,32,2,128]{3,2,1,0:T(2,128)} %bitcast.17), custom_call_target="tpu_custom_call" | custom-call | tf_op jit(solution)/shard_map/pallas_call | solution.py:162
  71.9 1.5 %copy.12 = f32[1,2,32,2,128]{4,3,2,1,0:T(2,128)} copy(f32[1,2,32,2,128]{4,3,2,1,0:T(2,128)} %bitcast.16) | data formatting | bytes 131072
  (3 shorter events, 0.0 us)
Async XLA Ops:
  0.0 4.5 %copy-start = (s32[1,1024]{1,0:T(1,128)S(1)}, s32[1,1024]{1,0:T(1,128)}, u32[]{:S(2)}) copy-start(s32[1,1024]{1,0:T(1,128)} %param.10) | copy-start | bytes 12292
  0.0 4.5 %copy-start.1 = (s32[1,1024]{1,0:T(1,128)S(1)}, s32[1,1024]{1,0:T(1,128)}, u32[]{:S(2)}) copy-start(s32[1,1024]{1,0:T(1,128)} %param.9) | copy-start | bytes 12292

commit v15 on v14

--- a/solution.py
+++ b/solution.py
@@ -249,7 +249,7 @@
     middle = groups // 2
 
     def order(j):
-        return lax.rem(home + middle + (1 - 2 * lax.rem(j, 2)) * ((j + 1) // 2) + groups, groups)
+        return lax.rem(j + 0 * (home + middle), groups)
 
     first = order(0)
     pack(first)

time: 73.9 us -> 75.5 us (1.022)
  the two profiles are of different devices: /device:TPU:7 before, /device:TPU:16 now
where the time goes in v15:
time: 75.5 us; the launch traced here: 75.1 us
  Pallas kernels  66.6 us (88%)
  local copies, waits for them, and re-layouts  4.5 us (6%)
  other arithmetic  3.9 us (5%)
    pallas_call x1, Pallas kernels, exchange_slab(): pl.pallas_call(exchange_kernel, out_shape=(jax.ShapeDtypeStruct(data_shap...  40.2 us
    pallas_call x1, Pallas kernels, post_step(): pl.pallas_call(functools.partial(post_kernel, slab_count=slab_count), out...  26.4 us
    unnamed x6, local copies, waits for them, and re-layouts  3.42 us

profile of v15, /device:TPU:16, one launch (start us, length us, event | category | flops | bytes accessed | tf_op | source)
XLA Modules:
  0.0 75.1 jit_solution(15968179974631474209)
XLA Ops:
  0.0 0.0 copy-start
  0.0 0.0 copy-start.1
  0.0 1.3 %convert_reduce_fusion = s32[1024]{0:T(1024)S(1)} fusion(s32[1024]{0:T(1024)} %bitcast.18), kind=kLoop, calls=%fused_computation | loop fusion | flops 5241856 | bytes 8192 | tf_op jit(solution)/shard_map/reduce_sum | solution.py:322
  1.3 1.3 %bitcast_add_fusion.slot_ref = s32[1,1024]{1,0:T(1,128)} fusion(s32[1,1024]{1,0:T(1,128)S(1)} %bitcast.19, s32[1,1024,1]{1,2,0:T(1,128)} %param.8), kind=kLoop, calls=%fused_computation.11 | loop fusion | flops 2048 | bytes 12288 | tf_op jit(solution)/shard_map/add | solution.py:323
  2.6 1.9 %copy.10 = bf16[128,8,2,128]{3,1,2,0:T(8,128)(2,1)} copy(bf16[128,8,2,128]{3,2,1,0:T(2,128)(2,1)} %bitcast.15) | data formatting | bytes 1048576
  4.5 0.0 copy-done
  4.5 0.0 copy-done.1
  4.6 0.1 pad.2.clone
  4.6 0.7 maximum_maximum_fusion.ids_ref
  5.3 40.2 %shard_map.73 = (bf16[64,32,256]{2,1,0:T(8,128)(2,1)}, s32[64,1,128]{2,1,0:T(1,128)}) custom-call(s32[1,1024]{1,0:T(1,128)} %bitcast_add_fusion.slot_ref, bf16[1024,256]{1,0:T(8,128)(2,1)} %bitcast.13, bf16[8,1024]{1,0:T(8,128)(2,1)} %maximum_maximum_fusion.ids_ref), custom_call_target="tpu_custom_call" | custom-call | tf_op jit(solution)/shard_map/pallas_call | solution.py:286
  45.6 0.9 %dynamic-slice_reduce_fusion = s32[64,32]{1,0:T(8,128)S(1)} fusion(s32[64,1,128]{2,1,0:T(1,128)} %get-tuple-element.7, s32[]{:T(128)S(6)} %select_n.15), kind=kLoop, calls=%fused_computation.4 | loop fusion | bytes 16388 | tf_op jit(solution)/shard_map/dynamic_slice | solution.py:331
  46.5 0.1 reshape.105
  46.6 0.6 multiply_add_fusion.code_ref
  47.2 26.4 %shard_map.74 = f32[2,32,2,128]{3,2,1,0:T(2,128)} custom-call(f32[3,8]{1,0:T(4,128)} %bitcast.20, s32[1,2048]{1,0:T(1,128)} %multiply_add_fusion.code_ref, bf16[2048,256]{1,0:T(8,128)(2,1)} %bitcast.14, bf16[8,128,128]{2,1,0:T(8,128)(2,1)} %kernels_ref.1, f32[2,32,2,128]{3,2,1,0:T(2,128)} %bitcast.17), custom_call_target="tpu_custom_call" | custom-call | tf_op jit(solution)/shard_map/pallas_call | solution.py:162
  73.6 1.5 %copy.12 = f32[1,2,32,2,128]{4,3,2,1,0:T(2,128)} copy(f32[1,2,32,2,128]{4,3,2,1,0:T(2,128)} %bitcast.16) | data formatting | bytes 131072
  (3 shorter events, 0.0 us)
Async XLA Ops:
  0.0 4.5 %copy-start = (s32[1,1024]{1,0:T(1,128)S(1)}, s32[1,1024]{1,0:T(1,128)}, u32[]{:S(2)}) copy-start(s32[1,1024]{1,0:T(1,128)} %param.10) | copy-start | bytes 12292
  0.0 4.5 %copy-start.1 = (s32[1,1024]{1,0:T(1,128)S(1)}, s32[1,1024]{1,0:T(1,128)}, u32[]{:S(2)}) copy-start(s32[1,1024]{1,0:T(1,128)} %param.9) | copy-start | bytes 12292

commit v16 on v14

--- a/solution.py
+++ b/solution.py
@@ -42,7 +42,7 @@
 
 
 def post_kernel(
-    scalars, code_ref, rows_ref, kernels_ref, obj_ref, out_ref, grid_ref, halo, gathered, phase_buf,
+    scalars, code_ref, rows_ref, kernels_ref, obj_ref, grid_ref, out_ref, halo, gathered, phase_buf,
     halo_send, halo_recv, send_sem, recv_sem, slab_count,
 ):
     refl_count = gathered.shape[0]
@@ -150,23 +150,38 @@
     shift = weight(0) * gathered[0]
     for r in range(1, refl_count):
         shift = shift + weight(r) * gathered[r]
-    for p in range(planes):
+    out_ref[...] = shift
+
+
+def update_kernel(obj_ref, grid_ref, shift_ref, out_ref):
+    for p in range(grid_ref.shape[0]):
         obj_re, obj_im = obj_ref[p, :, 0, :], obj_ref[p, :, 1, :]
-        new_re = obj_re - 0.5 * (grid_ref[p, 0] - obj_im * shift[p])
-        new_im = obj_im - 0.5 * (grid_ref[p, 1] + obj_re * shift[p])
+        new_re = obj_re - 0.5 * (grid_ref[p, 0] - obj_im * shift_ref[p])
+        new_im = obj_im - 0.5 * (grid_ref[p, 1] + obj_re * shift_ref[p])
         out_ref[p] = jnp.stack([new_re, new_im], axis=1)
+
+
+def update_step(obj, grid, shift):
+    return pl.pallas_call(
+        update_kernel,
+        out_shape=jax.ShapeDtypeStruct(obj.shape, jnp.float32),
+        in_specs=[pl.BlockSpec(memory_space=pltpu.VMEM)] * 3,
+        out_specs=pl.BlockSpec(memory_space=pltpu.VMEM),
+    )(obj, grid, shift)
 
 
 def post_step(scalars, code_row, rows, kernels, obj, slab_count, refl_count):
     planes, rows_per, _, width = obj.shape
     return pl.pallas_call(
         functools.partial(post_kernel, slab_count=slab_count),
-        out_shape=jax.ShapeDtypeStruct(obj.shape, jnp.float32),
+        out_shape=(
+            jax.ShapeDtypeStruct((planes, 2, rows_per, width), jnp.float32),
+            jax.ShapeDtypeStruct((planes, rows_per, width), jnp.float32),
+        ),
         in_specs=[pl.BlockSpec(memory_space=pltpu.SMEM)]
         + [pl.BlockSpec(memory_space=pltpu.VMEM)] * 4,
-        out_specs=pl.BlockSpec(memory_space=pltpu.VMEM),
+        out_specs=(pl.BlockSpec(memory_space=pltpu.VMEM), pl.BlockSpec(memory_space=pltpu.VMEM)),
         scratch_shapes=[
-            pltpu.VMEM((planes, 2, rows_per, width), jnp.float32),
             pltpu.VMEM((2, 2, rows_per, width), jnp.float32),
             pltpu.VMEM((refl_count, planes, rows_per, width), jnp.float32),
             pltpu.VMEM((planes, rows_per, width), jnp.float32),
@@ -332,8 +347,8 @@
     code_row = (lax.rem(got_codes, kernel_count) * block_count + got_codes // kernel_count)[None, :]
     refl_count = bragg_vectors.shape[0]
     obj = object_field[0]
-    updated = post_step(bragg_vectors.T, code_row, rows, kernels, obj, slab_count, refl_count)
-    return updated[None]
+    gridded, shift = post_step(bragg_vectors.T, code_row, rows, kernels, obj, slab_count, refl_count)
+    return update_step(obj, gridded, shift)[None]
 
 
 def solution(mesh):

time: 73.9 us -> 73.9 us (level)
  Pallas kernels: 64.9 us -> 66.4 us
  local copies, waits for them, and re-layouts: 4.5 us -> 3.03 us
    pallas_call x0 -> x1, Pallas kernels: none -> 1.6 us  [update_step(): pl.pallas_call(update_kernel, out_shape=jax.ShapeDtypeStruct(obj.shape, j...]
    unnamed x6 -> x5, local copies, waits for them, and re-layouts: 3.42 us -> 1.95 us
where the time goes in v16:
time: 73.9 us; the launch traced here: 73.4 us
  Pallas kernels  66.4 us (90%)
  other arithmetic  3.9 us (5%)
  local copies, waits for them, and re-layouts  3.03 us (4%)
    pallas_call x1, Pallas kernels, exchange_slab(): pl.pallas_call(exchange_kernel, out_shape=(jax.ShapeDtypeStruct(data_shap...  45.6 us
    pallas_call x1, Pallas kernels, post_step(): pl.pallas_call(functools.partial(post_kernel, slab_count=slab_count), out...  19.2 us
    unnamed x5, local copies, waits for them, and re-layouts  1.95 us
    pallas_call x1, Pallas kernels, update_step(): pl.pallas_call(update_kernel, out_shape=jax.ShapeDtypeStruct(obj.shape, j...  1.6 us

profile of v16, /device:TPU:7, one launch (start us, length us, event | category | flops | bytes accessed | tf_op | source)
XLA Modules:
  0.0 73.4 jit_solution(10091383060103818123)
XLA Ops:
  0.0 0.0 copy-start
  0.0 0.0 copy-start.1
  0.0 1.3 %convert_reduce_fusion = s32[1024]{0:T(1024)S(1)} fusion(s32[1024]{0:T(1024)} %bitcast.18), kind=kLoop, calls=%fused_computation | loop fusion | flops 5241856 | bytes 8192 | tf_op jit(solution)/shard_map/reduce_sum | solution.py:337
  1.3 1.3 %bitcast_add_fusion.slot_ref = s32[1,1024]{1,0:T(1,128)} fusion(s32[1,1024]{1,0:T(1,128)S(1)} %bitcast.19, s32[1,1024,1]{1,2,0:T(1,128)} %param.8), kind=kLoop, calls=%fused_computation.11 | loop fusion | flops 2048 | bytes 12288 | tf_op jit(solution)/shard_map/add | solution.py:338
  2.6 1.9 %copy.10 = bf16[128,8,2,128]{3,1,2,0:T(8,128)(2,1)} copy(bf16[128,8,2,128]{3,2,1,0:T(2,128)(2,1)} %bitcast.15) | data formatting | bytes 1048576
  4.5 0.0 copy-done
  4.5 0.0 copy-done.1
  4.6 0.1 pad.2.clone
  4.6 0.7 maximum_maximum_fusion.ids_ref
  5.3 45.6 %shard_map.73 = (bf16[64,32,256]{2,1,0:T(8,128)(2,1)}, s32[64,1,128]{2,1,0:T(1,128)}) custom-call(s32[1,1024]{1,0:T(1,128)} %bitcast_add_fusion.slot_ref, bf16[1024,256]{1,0:T(8,128)(2,1)} %bitcast.13, bf16[8,1024]{1,0:T(8,128)(2,1)} %maximum_maximum_fusion.ids_ref), custom_call_target="tpu_custom_call" | custom-call | tf_op jit(solution)/shard_map/pallas_call | solution.py:301
  50.9 0.9 %dynamic-slice_reduce_fusion = s32[64,32]{1,0:T(8,128)S(1)} fusion(s32[64,1,128]{2,1,0:T(1,128)} %get-tuple-element.9, s32[]{:T(128)S(6)} %select_n.15), kind=kLoop, calls=%fused_computation.4 | loop fusion | bytes 16388 | tf_op jit(solution)/shard_map/dynamic_slice | solution.py:346
  51.8 0.1 reshape.105
  51.9 0.6 multiply_add_fusion.code_ref
  52.5 19.2 %shard_map.74 = (f32[2,2,32,128]{3,2,1,0:T(8,128)}, f32[2,32,128]{2,1,0:T(8,128)}) custom-call(f32[3,8]{1,0:T(4,128)} %bitcast.20, s32[1,2048]{1,0:T(1,128)} %multiply_add_fusion.code_ref, bf16[2048,256]{1,0:T(8,128)(2,1)} %bitcast.14, bf16[8,128,128]{2,1,0:T(8,128)(2,1)} %kernels_ref.1, f32[2,32,2,128]{3,2,1,0:T(2,128)} %bitcast.16), custom_call_target="tpu_custom_call" | custom-call | tf_op jit(solution)/shard_map/pallas_call | solution.py:175
  71.8 1.6 %shard_map.75 = f32[2,32,2,128]{3,2,1,0:T(2,128)} custom-call(f32[2,32,2,128]{3,2,1,0:T(2,128)} %bitcast.17, f32[2,2,32,128]{3,2,1,0:T(8,128)} %get-tuple-element.11.grid_ref, f32[2,32,128]{2,1,0:T(8,128)} %get-tuple-element.12.shift_ref), custom_call_target="tpu_custom_call" | custom-call | tf_op jit(solution)/shard_map/pallas_call | solution.py:165
  (3 shorter events, 0.0 us)
Async XLA Ops:
  0.0 4.5 %copy-start = (s32[1,1024]{1,0:T(1,128)S(1)}, s32[1,1024]{1,0:T(1,128)}, u32[]{:S(2)}) copy-start(s32[1,1024]{1,0:T(1,128)} %param.10) | copy-start | bytes 12292
  0.0 4.5 %copy-start.1 = (s32[1,1024]{1,0:T(1,128)S(1)}, s32[1,1024]{1,0:T(1,128)}, u32[]{:S(2)}) copy-start(s32[1,1024]{1,0:T(1,128)} %param.9) | copy-start | bytes 12292

commit v17 on v13

--- a/solution.py
+++ b/solution.py
@@ -49,6 +49,16 @@
     planes, rows, width = grid_ref.shape[0], grid_ref.shape[2], grid_ref.shape[3]
     kernel_count = kernels_ref.shape[0]
     blocks = planes * rows
+    me = lax.axis_index("slab")
+    refl = lax.axis_index("refl")
+    up = lax.rem(me + 1, slab_count)
+    down = lax.rem(me + slab_count - 1, slab_count)
+    barrier = pltpu.get_barrier_semaphore()
+    pl.semaphore_signal(barrier, 1, device_id=(refl, up), device_id_type=MESH)
+    pl.semaphore_signal(barrier, 1, device_id=(refl, down), device_id_type=MESH)
+    for step in range(1, refl_count):
+        peer = lax.rem(refl + step, refl_count)
+        pl.semaphore_signal(barrier, 1, device_id=(peer, me), device_id_type=MESH)
     chosen = (
         code_ref[...] == lax.broadcasted_iota(jnp.int32, (kernel_count * blocks, code_ref.shape[1]), 0)
     ).astype(jnp.bfloat16)
@@ -65,16 +75,6 @@
                 part = part - piece.astype(jnp.float32)
         for p in range(planes):
             grid_ref[p, c] = total[p * rows : (p + 1) * rows]
-    me = lax.axis_index("slab")
-    refl = lax.axis_index("refl")
-    up = lax.rem(me + 1, slab_count)
-    down = lax.rem(me + slab_count - 1, slab_count)
-    barrier = pltpu.get_barrier_semaphore()
-    pl.semaphore_signal(barrier, 1, device_id=(refl, up), device_id_type=MESH)
-    pl.semaphore_signal(barrier, 1, device_id=(refl, down), device_id_type=MESH)
-    for step in range(1, refl_count):
-        peer = lax.rem(refl + step, refl_count)
-        pl.semaphore_signal(barrier, 1, device_id=(peer, me), device_id_type=MESH)
     pl.semaphore_wait(barrier, refl_count + 1)
     low_copy = pltpu.make_async_remote_copy(
         src_ref=grid_ref.at[planes - 1], dst_ref=halo.at[0], send_sem=halo_send.at[0],

time: 73 us -> 71.2 us (0.975)
  Pallas kernels: 64.9 us -> 63.1 us
    pallas_call x1, Pallas kernels: 19.3 us -> 17.5 us  [post_step(): pl.pallas_call(functools.partial(post_kernel, slab_count=slab_count), out...]
where the time goes in v17:
time: 71.2 us; the launch traced here: 70.8 us
  Pallas kernels  63.1 us (89%)
  local copies, waits for them, and re-layouts  5.22 us (7%)
  other arithmetic  2.46 us (3%)
    pallas_call x1, Pallas kernels, exchange_slab(): pl.pallas_call(exchange_kernel, out_shape=(jax.ShapeDtypeStruct(data_shap...  45.6 us
    pallas_call x1, Pallas kernels, post_step(): pl.pallas_call(functools.partial(post_kernel, slab_count=slab_count), out...  17.5 us
    unnamed x11, local copies, waits for them, and re-layouts  4.13 us

profile of v17, /device:TPU:7, one launch (start us, length us, event | category | flops | bytes accessed | tf_op | source)
XLA Modules:
  0.0 70.8 jit_solution(11605012666306854904)
XLA Ops:
  0.0 0.0 copy-start.1
  0.0 0.0 copy-start.2
  0.0 0.0 copy-start
  0.0 0.0 copy-start.3
  0.0 2.0 %copy.13 = bf16[128,8,2,128]{3,1,2,0:T(8,128)(2,1)} copy(bf16[128,8,2,128]{3,2,1,0:T(2,128)(2,1)} %bitcast.14) | data formatting | bytes 1048576
  2.0 0.0 copy-done.1
  2.0 0.0 copy-done.2
  2.1 0.1 pad.2.clone
  2.1 0.7 maximum_maximum_fusion.ids_ref
  2.8 0.0 copy-done
  2.8 0.5 convert_reduce_fusion
  3.3 0.6 bitcast_add_fusion.slot_ref
  3.9 45.6 %shard_map.73 = (bf16[64,32,256]{2,1,0:T(8,128)(2,1)}, s32[64,1,128]{2,1,0:T(1,128)}) custom-call(s32[1,1024]{1,0:T(1,128)} %bitcast_add_fusion.slot_ref, bf16[1024,256]{1,0:T(8,128)(2,1)} %bitcast.12, bf16[8,1024]{1,0:T(8,128)(2,1)} %maximum_maximum_fusion.ids_ref), custom_call_target="tpu_custom_call" | custom-call | tf_op jit(solution)/shard_map/pallas_call | solution.py:286
  49.5 0.9 %dynamic-slice_reduce_fusion = s32[64,32]{1,0:T(8,128)S(1)} fusion(s32[64,1,128]{2,1,0:T(1,128)} %get-tuple-element.7, s32[]{:T(128)S(6)} %select_n.15), kind=kLoop, calls=%fused_computation.4 | loop fusion | bytes 16388 | tf_op jit(solution)/shard_map/dynamic_slice | solution.py:331
  50.4 0.1 reshape.105
  50.5 0.6 multiply_add_fusion.code_ref
  51.2 0.0 copy-done.3
  51.2 0.7 copy.10.scalars
  51.8 17.5 %shard_map.74 = f32[2,32,2,128]{3,2,1,0:T(2,128)} custom-call(f32[8,3]{1,0:T(8,128)} %copy.10.scalars, s32[1,2048]{1,0:T(1,128)} %multiply_add_fusion.code_ref, bf16[2048,256]{1,0:T(8,128)(2,1)} %bitcast.13, bf16[8,128,128]{2,1,0:T(8,128)(2,1)} %kernels_ref.1, f32[2,32,2,128]{3,2,1,0:T(2,128)} %bitcast.16), custom_call_target="tpu_custom_call" | custom-call | tf_op jit(solution)/shard_map/pallas_call | solution.py:162
  69.4 1.5 %copy.15 = f32[1,2,32,2,128]{4,3,2,1,0:T(2,128)} copy(f32[1,2,32,2,128]{4,3,2,1,0:T(2,128)} %bitcast.15) | data formatting | bytes 131072
  (3 shorter events, 0.0 us)
Async XLA Ops:
  0.0 2.0 %copy-start.1 = (s32[1,1024]{1,0:T(1,128)S(1)}, s32[1,1024]{1,0:T(1,128)}, u32[]{:S(2)}) copy-start(s32[1,1024]{1,0:T(1,128)} %param.9) | copy-start | bytes 12292
  0.0 2.0 %copy-start.2 = (s32[1,1024]{1,0:T(1,128)S(1)}, s32[1,1024]{1,0:T(1,128)}, u32[]{:S(2)}) copy-start(s32[1,1024]{1,0:T(1,128)} %param.10) | copy-start | bytes 12292
  0.0 2.8 %copy-start = (s32[1,1024,1]{1,2,0:T(1,128)S(1)}, s32[1,1024,1]{1,2,0:T(1,128)}, u32[]{:S(2)}) copy-start(s32[1,1024,1]{1,2,0:T(1,128)} %param.8) | copy-start | bytes 12292
  0.0 51.1 %copy-start.3 = (f32[8,3]{0,1:T(4,128)S(1)}, f32[8,3]{0,1:T(4,128)}, u32[]{:S(2)}) copy-start(f32[8,3]{0,1:T(4,128)} %param.12) | copy-start | bytes 292

commit v18 on v17

--- a/solution.py
+++ b/solution.py
@@ -100,10 +100,10 @@
         return 0.5 * (after - before)
 
     mate = refl + 1 - 2 * lax.rem(refl, 2)
-    q0, q1, q2 = scalars[refl, 0], scalars[refl, 1], scalars[refl, 2]
-    d0 = q0 - scalars[mate, 0]
-    d1 = q1 - scalars[mate, 1]
-    d2 = q2 - scalars[mate, 2]
+    q0, q1, q2 = scalars[0, refl], scalars[1, refl], scalars[2, refl]
+    d0 = q0 - scalars[0, mate]
+    d1 = q1 - scalars[1, mate]
+    d2 = q2 - scalars[2, mate]
     partial = []
     for p in range(planes):
         obj_re, obj_im = obj_ref[p, :, 0, :], obj_ref[p, :, 1, :]
@@ -145,7 +145,7 @@
             recv_sem=recv_sem.at[step], device_id=(source, me), device_id_type=MESH,
         ).wait_recv()
     def weight(r):
-        return scalars[r, 0] * d0 + scalars[r, 1] * d1 + scalars[r, 2] * d2
+        return scalars[0, r] * d0 + scalars[1, r] * d1 + scalars[2, r] * d2
 
     shift = weight(0) * gathered[0]
     for r in range(1, refl_count):
@@ -332,7 +332,7 @@
     code_row = (lax.rem(got_codes, kernel_count) * block_count + got_codes // kernel_count)[None, :]
     refl_count = bragg_vectors.shape[0]
     obj = object_field[0]
-    updated = post_step(bragg_vectors, code_row, rows, kernels, obj, slab_count, refl_count)
+    updated = post_step(bragg_vectors.T, code_row, rows, kernels, obj, slab_count, refl_count)
     return updated[None]
 
 

time: 71.2 us -> 72 us (1.011)
  other arithmetic: 2.46 us -> 3.9 us
    reduce_sum x1, other arithmetic: 0.52 us -> 1.28 us  [per_device(): slots = jnp.sum(same.astype(jnp.int32), axis=1)]
    unnamed x11 -> x6, local copies, waits for them, and re-layouts: 4.13 us -> 3.42 us
where the time goes in v18:
time: 72 us; the launch traced here: 71.6 us
  Pallas kernels  63.1 us (88%)
  local copies, waits for them, and re-layouts  4.5 us (6%)
  other arithmetic  3.9 us (5%)
    pallas_call x1, Pallas kernels, exchange_slab(): pl.pallas_call(exchange_kernel, out_shape=(jax.ShapeDtypeStruct(data_shap...  45.6 us
    pallas_call x1, Pallas kernels, post_step(): pl.pallas_call(functools.partial(post_kernel, slab_count=slab_count), out...  17.5 us
    unnamed x6, local copies, waits for them, and re-layouts  3.42 us

profile of v18, /device:TPU:7, one launch (start us, length us, event | category | flops | bytes accessed | tf_op | source)
XLA Modules:
  0.0 71.6 jit_solution(7515398162276621871)
XLA Ops:
  0.0 0.0 copy-start
  0.0 0.0 copy-start.1
  0.0 1.3 %convert_reduce_fusion = s32[1024]{0:T(1024)S(1)} fusion(s32[1024]{0:T(1024)} %bitcast.18), kind=kLoop, calls=%fused_computation | loop fusion | flops 5241856 | bytes 8192 | tf_op jit(solution)/shard_map/reduce_sum | solution.py:322
  1.3 1.3 %bitcast_add_fusion.slot_ref = s32[1,1024]{1,0:T(1,128)} fusion(s32[1,1024]{1,0:T(1,128)S(1)} %bitcast.19, s32[1,1024,1]{1,2,0:T(1,128)} %param.8), kind=kLoop, calls=%fused_computation.11 | loop fusion | flops 2048 | bytes 12288 | tf_op jit(solution)/shard_map/add | solution.py:323
  2.6 1.9 %copy.10 = bf16[128,8,2,128]{3,1,2,0:T(8,128)(2,1)} copy(bf16[128,8,2,128]{3,2,1,0:T(2,128)(2,1)} %bitcast.15) | data formatting | bytes 1048576
  4.5 0.0 copy-done
  4.5 0.0 copy-done.1
  4.6 0.1 pad.2.clone
  4.6 0.7 maximum_maximum_fusion.ids_ref
  5.3 45.6 %shard_map.73 = (bf16[64,32,256]{2,1,0:T(8,128)(2,1)}, s32[64,1,128]{2,1,0:T(1,128)}) custom-call(s32[1,1024]{1,0:T(1,128)} %bitcast_add_fusion.slot_ref, bf16[1024,256]{1,0:T(8,128)(2,1)} %bitcast.13, bf16[8,1024]{1,0:T(8,128)(2,1)} %maximum_maximum_fusion.ids_ref), custom_call_target="tpu_custom_call" | custom-call | tf_op jit(solution)/shard_map/pallas_call | solution.py:286
  50.9 0.9 %dynamic-slice_reduce_fusion = s32[64,32]{1,0:T(8,128)S(1)} fusion(s32[64,1,128]{2,1,0:T(1,128)} %get-tuple-element.7, s32[]{:T(128)S(6)} %select_n.15), kind=kLoop, calls=%fused_computation.4 | loop fusion | bytes 16388 | tf_op jit(solution)/shard_map/dynamic_slice | solution.py:331
  51.8 0.1 reshape.105
  51.9 0.6 multiply_add_fusion.code_ref
  52.5 17.5 %shard_map.74 = f32[2,32,2,128]{3,2,1,0:T(2,128)} custom-call(f32[3,8]{1,0:T(4,128)} %bitcast.20, s32[1,2048]{1,0:T(1,128)} %multiply_add_fusion.code_ref, bf16[2048,256]{1,0:T(8,128)(2,1)} %bitcast.14, bf16[8,128,128]{2,1,0:T(8,128)(2,1)} %kernels_ref.1, f32[2,32,2,128]{3,2,1,0:T(2,128)} %bitcast.17), custom_call_target="tpu_custom_call" | custom-call | tf_op jit(solution)/shard_map/pallas_call | solution.py:162
  70.1 1.5 %copy.12 = f32[1,2,32,2,128]{4,3,2,1,0:T(2,128)} copy(f32[1,2,32,2,128]{4,3,2,1,0:T(2,128)} %bitcast.16) | data formatting | bytes 131072
  (3 shorter events, 0.0 us)
Async XLA Ops:
  0.0 4.5 %copy-start = (s32[1,1024]{1,0:T(1,128)S(1)}, s32[1,1024]{1,0:T(1,128)}, u32[]{:S(2)}) copy-start(s32[1,1024]{1,0:T(1,128)} %param.10) | copy-start | bytes 12292
  0.0 4.5 %copy-start.1 = (s32[1,1024]{1,0:T(1,128)S(1)}, s32[1,1024]{1,0:T(1,128)}, u32[]{:S(2)}) copy-start(s32[1,1024]{1,0:T(1,128)} %param.9) | copy-start | bytes 12292

commit v19 on v17

--- a/solution.py
+++ b/solution.py
@@ -182,6 +182,7 @@
 def exchange_kernel(
     slot_ref, values_ref, ids_ref, data_out, code_out, data_buf, code_in, data_send, data_recv, code_send,
     code_recv,
+    block_count,
 ):
     count, capacity = data_out.shape[0], data_out.shape[1]
     group = 8 if count >= 16 else count // 2
@@ -208,7 +209,7 @@
         codes = lax.dot_general(
             ids_ref[...], chosen, (((1,), (1,)), ((), ())), preferred_element_type=jnp.float32
         )
-        codes = (codes[0:1] * 8.0 + codes[1:2]).astype(jnp.int32)
+        codes = (codes[1:2] * float(block_count) + codes[0:1]).astype(jnp.int32)
         for part in range(group):
             window = (part * capacity) // 128
             code_in[g * group + part] = codes[:, window * 128 : (window + 1) * 128]
@@ -280,11 +281,11 @@
     local.wait()
 
 
-def exchange_slab(flat_slot, values, ids, count, capacity):
+def exchange_slab(flat_slot, values, ids, count, capacity, block_count):
     data_shape = (count, capacity, values.shape[1])
     code_shape = (count, 1, 128)
     return pl.pallas_call(
-        exchange_kernel,
+        functools.partial(exchange_kernel, block_count=block_count),
         out_shape=(
             jax.ShapeDtypeStruct(data_shape, jnp.bfloat16),
             jax.ShapeDtypeStruct(code_shape, jnp.int32),
@@ -324,12 +325,12 @@
     ids = jnp.concatenate(
         [block_ids, kernel_ids, jnp.zeros((6, tile_count), jnp.int32)], axis=0
     ).astype(jnp.bfloat16)
-    got, got_code = exchange_slab(flat_slot[None, :], values, ids, slab_count, capacity)
+    got, got_code = exchange_slab(flat_slot[None, :], values, ids, slab_count, capacity, block_count)
     row_total = slab_count * capacity
     rows = got.reshape(row_total, row_width)
     offset = lax.rem(lax.axis_index("slab"), 4) * capacity
     got_codes = lax.dynamic_slice_in_dim(got_code[:, 0, :], offset, capacity, axis=1).reshape(row_total)
-    code_row = (lax.rem(got_codes, kernel_count) * block_count + got_codes // kernel_count)[None, :]
+    code_row = got_codes[None, :]
     refl_count = bragg_vectors.shape[0]
     obj = object_field[0]
     updated = post_step(bragg_vectors, code_row, rows, kernels, obj, slab_count, refl_count)

time: 71.2 us -> 71.2 us (level)
  no operation moved by 1% of the time
where the time goes in v19:
time: 71.2 us; the launch traced here: 70.8 us
  Pallas kernels  63.1 us (89%)
  local copies, waits for them, and re-layouts  5.81 us (8%)
  other arithmetic  1.81 us (3%)
    pallas_call x1, Pallas kernels, exchange_slab(): pl.pallas_call(functools.partial(exchange_kernel, block_count=block_count...  45.6 us
    pallas_call x1, Pallas kernels, post_step(): pl.pallas_call(functools.partial(post_kernel, slab_count=slab_count), out...  17.5 us
    unnamed x11, local copies, waits for them, and re-layouts  4.13 us

profile of v19, /device:TPU:7, one launch (start us, length us, event | category | flops | bytes accessed | tf_op | source)
XLA Modules:
  0.0 70.8 jit_solution(9927744652863618189)
XLA Ops:
  0.0 0.0 copy-start.1
  0.0 0.0 copy-start.2
  0.0 0.0 copy-start
  0.0 0.0 copy-start.3
  0.0 2.0 %copy.13 = bf16[128,8,2,128]{3,1,2,0:T(8,128)(2,1)} copy(bf16[128,8,2,128]{3,2,1,0:T(2,128)(2,1)} %bitcast.14) | data formatting | bytes 1048576
  2.0 0.0 copy-done.1
  2.0 0.0 copy-done.2
  2.1 0.1 pad.2.clone
  2.1 0.7 maximum_maximum_fusion.ids_ref
  2.8 0.0 copy-done
  2.8 0.5 convert_reduce_fusion
  3.3 0.6 bitcast_add_fusion.slot_ref
  3.9 45.6 %shard_map.73 = (bf16[64,32,256]{2,1,0:T(8,128)(2,1)}, s32[64,1,128]{2,1,0:T(1,128)}) custom-call(s32[1,1024]{1,0:T(1,128)} %bitcast_add_fusion.slot_ref, bf16[1024,256]{1,0:T(8,128)(2,1)} %bitcast.12, bf16[8,1024]{1,0:T(8,128)(2,1)} %maximum_maximum_fusion.ids_ref), custom_call_target="tpu_custom_call" | custom-call | tf_op jit(solution)/shard_map/pallas_call | solution.py:287
  49.5 0.9 %dynamic-slice_reduce_fusion = s32[64,32]{1,0:T(8,128)S(1)} fusion(s32[64,1,128]{2,1,0:T(1,128)} %get-tuple-element.7, s32[]{:T(128)S(6)} %select_n.3), kind=kLoop, calls=%fused_computation.4 | loop fusion | bytes 16388 | tf_op jit(solution)/shard_map/dynamic_slice | solution.py:332
  50.4 0.7 broadcast_in_dim_reshape.3.code_ref
  51.1 0.0 copy-done.3
  51.1 0.7 copy.10.scalars
  51.8 17.5 %shard_map.74 = f32[2,32,2,128]{3,2,1,0:T(2,128)} custom-call(f32[8,3]{1,0:T(8,128)} %copy.10.scalars, s32[1,2048]{1,0:T(1,128)} %broadcast_in_dim_reshape.3.code_ref, bf16[2048,256]{1,0:T(8,128)(2,1)} %bitcast.13, bf16[8,128,128]{2,1,0:T(8,128)(2,1)} %kernels_ref.1, f32[2,32,2,128]{3,2,1,0:T(2,128)} %bitcast.16), custom_call_target="tpu_custom_call" | custom-call | tf_op jit(solution)/shard_map/pallas_call | solution.py:162
  69.3 1.5 %copy.15 = f32[1,2,32,2,128]{4,3,2,1,0:T(2,128)} copy(f32[1,2,32,2,128]{4,3,2,1,0:T(2,128)} %bitcast.15) | data formatting | bytes 131072
  (3 shorter events, 0.0 us)
Async XLA Ops:
  0.0 2.0 %copy-start.1 = (s32[1,1024]{1,0:T(1,128)S(1)}, s32[1,1024]{1,0:T(1,128)}, u32[]{:S(2)}) copy-start(s32[1,1024]{1,0:T(1,128)} %param.9) | copy-start | bytes 12292
  0.0 2.0 %copy-start.2 = (s32[1,1024]{1,0:T(1,128)S(1)}, s32[1,1024]{1,0:T(1,128)}, u32[]{:S(2)}) copy-start(s32[1,1024]{1,0:T(1,128)} %param.10) | copy-start | bytes 12292
  0.0 2.8 %copy-start = (s32[1,1024,1]{1,2,0:T(1,128)S(1)}, s32[1,1024,1]{1,2,0:T(1,128)}, u32[]{:S(2)}) copy-start(s32[1,1024,1]{1,2,0:T(1,128)} %param.8) | copy-start | bytes 12292
  0.0 51.1 %copy-start.3 = (f32[8,3]{0,1:T(4,128)S(1)}, f32[8,3]{0,1:T(4,128)}, u32[]{:S(2)}) copy-start(f32[8,3]{0,1:T(4,128)} %param.12) | copy-start | bytes 292

commit v20 on v18

--- a/solution.py
+++ b/solution.py
@@ -182,6 +182,7 @@
 def exchange_kernel(
     slot_ref, values_ref, ids_ref, data_out, code_out, data_buf, code_in, data_send, data_recv, code_send,
     code_recv,
+    block_count,
 ):
     count, capacity = data_out.shape[0], data_out.shape[1]
     group = 8 if count >= 16 else count // 2
@@ -208,7 +209,7 @@
         codes = lax.dot_general(
             ids_ref[...], chosen, (((1,), (1,)), ((), ())), preferred_element_type=jnp.float32
         )
-        codes = (codes[0:1] * 8.0 + codes[1:2]).astype(jnp.int32)
+        codes = (codes[1:2] * float(block_count) + codes[0:1]).astype(jnp.int32)
         for part in range(group):
             window = (part * capacity) // 128
             code_in[g * group + part] = codes[:, window * 128 : (window + 1) * 128]
@@ -280,11 +281,11 @@
     local.wait()
 
 
-def exchange_slab(flat_slot, values, ids, count, capacity):
+def exchange_slab(flat_slot, values, ids, count, capacity, block_count):
     data_shape = (count, capacity, values.shape[1])
     code_shape = (count, 1, 128)
     return pl.pallas_call(
-        exchange_kernel,
+        functools.partial(exchange_kernel, block_count=block_count),
         out_shape=(
             jax.ShapeDtypeStruct(data_shape, jnp.bfloat16),
             jax.ShapeDtypeStruct(code_shape, jnp.int32),
@@ -324,12 +325,12 @@
     ids = jnp.concatenate(
         [block_ids, kernel_ids, jnp.zeros((6, tile_count), jnp.int32)], axis=0
     ).astype(jnp.bfloat16)
-    got, got_code = exchange_slab(flat_slot[None, :], values, ids, slab_count, capacity)
+    got, got_code = exchange_slab(flat_slot[None, :], values, ids, slab_count, capacity, block_count)
     row_total = slab_count * capacity
     rows = got.reshape(row_total, row_width)
     offset = lax.rem(lax.axis_index("slab"), 4) * capacity
     got_codes = lax.dynamic_slice_in_dim(got_code[:, 0, :], offset, capacity, axis=1).reshape(row_total)
-    code_row = (lax.rem(got_codes, kernel_count) * block_count + got_codes // kernel_count)[None, :]
+    code_row = got_codes[None, :]
     refl_count = bragg_vectors.shape[0]
     obj = object_field[0]
     updated = post_step(bragg_vectors.T, code_row, rows, kernels, obj, slab_count, refl_count)

time: 72 us -> 72 us (level)
  no operation moved by 1% of the time
where the time goes in v20:
time: 72 us; the launch traced here: 71.5 us
  Pallas kernels  63.1 us (88%)
  local copies, waits for them, and re-layouts  5.1 us (7%)
  other arithmetic  3.25 us (5%)
    pallas_call x1, Pallas kernels, exchange_slab(): pl.pallas_call(functools.partial(exchange_kernel, block_count=block_count...  45.6 us
    pallas_call x1, Pallas kernels, post_step(): pl.pallas_call(functools.partial(post_kernel, slab_count=slab_count), out...  17.5 us
    unnamed x6, local copies, waits for them, and re-layouts  3.42 us

profile of v20, /device:TPU:7, one launch (start us, length us, event | category | flops | bytes accessed | tf_op | source)
XLA Modules:
  0.0 71.5 jit_solution(2858639037249255892)
XLA Ops:
  0.0 0.0 copy-start
  0.0 0.0 copy-start.1
  0.0 1.3 %convert_reduce_fusion = s32[1024]{0:T(1024)S(1)} fusion(s32[1024]{0:T(1024)} %bitcast.18), kind=kLoop, calls=%fused_computation | loop fusion | flops 5241856 | bytes 8192 | tf_op jit(solution)/shard_map/reduce_sum | solution.py:323
  1.3 1.3 %bitcast_add_fusion.slot_ref = s32[1,1024]{1,0:T(1,128)} fusion(s32[1,1024]{1,0:T(1,128)S(1)} %bitcast.19, s32[1,1024,1]{1,2,0:T(1,128)} %param.8), kind=kLoop, calls=%fused_computation.6 | loop fusion | flops 2048 | bytes 12288 | tf_op jit(solution)/shard_map/add | solution.py:324
  2.6 1.9 %copy.10 = bf16[128,8,2,128]{3,1,2,0:T(8,128)(2,1)} copy(bf16[128,8,2,128]{3,2,1,0:T(2,128)(2,1)} %bitcast.15) | data formatting | bytes 1048576
  4.5 0.0 copy-done
  4.5 0.0 copy-done.1
  4.6 0.1 pad.2.clone
  4.6 0.7 maximum_maximum_fusion.ids_ref
  5.3 45.6 %shard_map.73 = (bf16[64,32,256]{2,1,0:T(8,128)(2,1)}, s32[64,1,128]{2,1,0:T(1,128)}) custom-call(s32[1,1024]{1,0:T(1,128)} %bitcast_add_fusion.slot_ref, bf16[1024,256]{1,0:T(8,128)(2,1)} %bitcast.13, bf16[8,1024]{1,0:T(8,128)(2,1)} %maximum_maximum_fusion.ids_ref), custom_call_target="tpu_custom_call" | custom-call | tf_op jit(solution)/shard_map/pallas_call | solution.py:287
  50.9 0.9 %dynamic-slice_reduce_fusion = s32[64,32]{1,0:T(8,128)S(1)} fusion(s32[64,1,128]{2,1,0:T(1,128)} %get-tuple-element.7, s32[]{:T(128)S(6)} %select_n.3), kind=kLoop, calls=%fused_computation.4 | loop fusion | bytes 16388 | tf_op jit(solution)/shard_map/dynamic_slice | solution.py:332
  51.8 0.7 broadcast_in_dim_reshape.3.code_ref
  52.5 17.5 %shard_map.74 = f32[2,32,2,128]{3,2,1,0:T(2,128)} custom-call(f32[3,8]{1,0:T(4,128)} %bitcast.20, s32[1,2048]{1,0:T(1,128)} %broadcast_in_dim_reshape.3.code_ref, bf16[2048,256]{1,0:T(8,128)(2,1)} %bitcast.14, bf16[8,128,128]{2,1,0:T(8,128)(2,1)} %kernels_ref.1, f32[2,32,2,128]{3,2,1,0:T(2,128)} %bitcast.17), custom_call_target="tpu_custom_call" | custom-call | tf_op jit(solution)/shard_map/pallas_call | solution.py:162
  70.0 1.5 %copy.12 = f32[1,2,32,2,128]{4,3,2,1,0:T(2,128)} copy(f32[1,2,32,2,128]{4,3,2,1,0:T(2,128)} %bitcast.16) | data formatting | bytes 131072
  (3 shorter events, 0.0 us)
Async XLA Ops:
  0.0 4.5 %copy-start = (s32[1,1024]{1,0:T(1,128)S(1)}, s32[1,1024]{1,0:T(1,128)}, u32[]{:S(2)}) copy-start(s32[1,1024]{1,0:T(1,128)} %param.10) | copy-start | bytes 12292
  0.0 4.5 %copy-start.1 = (s32[1,1024]{1,0:T(1,128)S(1)}, s32[1,1024]{1,0:T(1,128)}, u32[]{:S(2)}) copy-start(s32[1,1024]{1,0:T(1,128)} %param.9) | copy-start | bytes 12292

commit v21 on v17

--- a/solution.py
+++ b/solution.py
@@ -63,19 +63,21 @@
         code_ref[...] == lax.broadcasted_iota(jnp.int32, (kernel_count * blocks, code_ref.shape[1]), 0)
     ).astype(jnp.bfloat16)
     summed = jnp.dot(chosen, rows_ref[...], preferred_element_type=jnp.float32)
-    for c in range(2):
-        total = None
-        for k in range(kernel_count):
-            part = summed[k * blocks : (k + 1) * blocks, c * width : (c + 1) * width]
-            weights = kernels_ref[k]
-            for _ in range(3):
-                piece = part.astype(jnp.bfloat16)
-                term = jnp.dot(piece, weights, preferred_element_type=jnp.float32)
-                total = term if total is None else total + term
-                part = part - piece.astype(jnp.float32)
-        for p in range(planes):
-            grid_ref[p, c] = total[p * rows : (p + 1) * rows]
-    pl.semaphore_wait(barrier, refl_count + 1)
+
+    def grid_plane(p):
+        for c in range(2):
+            total = None
+            for k in range(kernel_count):
+                start = k * blocks + p * rows
+                part = summed[start : start + rows, c * width : (c + 1) * width]
+                weights = kernels_ref[k]
+                for _ in range(3):
+                    piece = part.astype(jnp.bfloat16)
+                    term = jnp.dot(piece, weights, preferred_element_type=jnp.float32)
+                    total = term if total is None else total + term
+                    part = part - piece.astype(jnp.float32)
+            grid_ref[p, c] = total
+
     low_copy = pltpu.make_async_remote_copy(
         src_ref=grid_ref.at[planes - 1], dst_ref=halo.at[0], send_sem=halo_send.at[0],
         recv_sem=halo_recv.at[0], device_id=(refl, up), device_id_type=MESH,
@@ -84,8 +86,12 @@
         src_ref=grid_ref.at[0], dst_ref=halo.at[1], send_sem=halo_send.at[1],
         recv_sem=halo_recv.at[1], device_id=(refl, down), device_id_type=MESH,
     )
+    grid_plane(0)
+    pl.semaphore_wait(barrier, refl_count + 1)
+    high_copy.start()
+    for p in range(1, planes):
+        grid_plane(p)
     low_copy.start()
-    high_copy.start()
     row_of = lax.broadcasted_iota(jnp.int32, (rows, width), 0)
     lane_of = lax.broadcasted_iota(jnp.int32, (rows, width), 1)
 

time: 71.2 us -> 72.2 us (1.014)
  Pallas kernels: 63.1 us -> 64.1 us
    pallas_call x1, Pallas kernels: 17.5 us -> 18.6 us  [post_step(): pl.pallas_call(functools.partial(post_kernel, slab_count=slab_count), out...]
where the time goes in v21:
time: 72.2 us; the launch traced here: 71.9 us
  Pallas kernels  64.1 us (89%)
  local copies, waits for them, and re-layouts  5.22 us (7%)
  other arithmetic  2.46 us (3%)
    pallas_call x1, Pallas kernels, exchange_slab(): pl.pallas_call(exchange_kernel, out_shape=(jax.ShapeDtypeStruct(data_shap...  45.6 us
    pallas_call x1, Pallas kernels, post_step(): pl.pallas_call(functools.partial(post_kernel, slab_count=slab_count), out...  18.6 us
    unnamed x11, local copies, waits for them, and re-layouts  4.13 us

profile of v21, /device:TPU:7, one launch (start us, length us, event | category | flops | bytes accessed | tf_op | source)
XLA Modules:
  0.0 71.9 jit_solution(2471828732827536391)
XLA Ops:
  0.0 0.0 copy-start.1
  0.0 0.0 copy-start.2
  0.0 0.0 copy-start
  0.0 0.0 copy-start.3
  0.0 2.0 %copy.13 = bf16[128,8,2,128]{3,1,2,0:T(8,128)(2,1)} copy(bf16[128,8,2,128]{3,2,1,0:T(2,128)(2,1)} %bitcast.14) | data formatting | bytes 1048576
  2.0 0.0 copy-done.1
  2.0 0.0 copy-done.2
  2.1 0.1 pad.2.clone
  2.1 0.7 maximum_maximum_fusion.ids_ref
  2.8 0.0 copy-done
  2.8 0.5 convert_reduce_fusion
  3.3 0.6 bitcast_add_fusion.slot_ref
  3.9 45.6 %shard_map.73 = (bf16[64,32,256]{2,1,0:T(8,128)(2,1)}, s32[64,1,128]{2,1,0:T(1,128)}) custom-call(s32[1,1024]{1,0:T(1,128)} %bitcast_add_fusion.slot_ref, bf16[1024,256]{1,0:T(8,128)(2,1)} %bitcast.12, bf16[8,1024]{1,0:T(8,128)(2,1)} %maximum_maximum_fusion.ids_ref), custom_call_target="tpu_custom_call" | custom-call | tf_op jit(solution)/shard_map/pallas_call | solution.py:292
  49.5 0.9 %dynamic-slice_reduce_fusion = s32[64,32]{1,0:T(8,128)S(1)} fusion(s32[64,1,128]{2,1,0:T(1,128)} %get-tuple-element.7, s32[]{:T(128)S(6)} %select_n.15), kind=kLoop, calls=%fused_computation.4 | loop fusion | bytes 16388 | tf_op jit(solution)/shard_map/dynamic_slice | solution.py:337
  50.4 0.1 reshape.105
  50.5 0.6 multiply_add_fusion.code_ref
  51.2 0.0 copy-done.3
  51.2 0.7 copy.10.scalars
  51.8 18.6 %shard_map.74 = f32[2,32,2,128]{3,2,1,0:T(2,128)} custom-call(f32[8,3]{1,0:T(8,128)} %copy.10.scalars, s32[1,2048]{1,0:T(1,128)} %multiply_add_fusion.code_ref, bf16[2048,256]{1,0:T(8,128)(2,1)} %bitcast.13, bf16[8,128,128]{2,1,0:T(8,128)(2,1)} %kernels_ref.1, f32[2,32,2,128]{3,2,1,0:T(2,128)} %bitcast.16), custom_call_target="tpu_custom_call" | custom-call | tf_op jit(solution)/shard_map/pallas_call | solution.py:168
  70.4 1.5 %copy.15 = f32[1,2,32,2,128]{4,3,2,1,0:T(2,128)} copy(f32[1,2,32,2,128]{4,3,2,1,0:T(2,128)} %bitcast.15) | data formatting | bytes 131072
  (3 shorter events, 0.0 us)
Async XLA Ops:
  0.0 2.0 %copy-start.1 = (s32[1,1024]{1,0:T(1,128)S(1)}, s32[1,1024]{1,0:T(1,128)}, u32[]{:S(2)}) copy-start(s32[1,1024]{1,0:T(1,128)} %param.9) | copy-start | bytes 12292
  0.0 2.0 %copy-start.2 = (s32[1,1024]{1,0:T(1,128)S(1)}, s32[1,1024]{1,0:T(1,128)}, u32[]{:S(2)}) copy-start(s32[1,1024]{1,0:T(1,128)} %param.10) | copy-start | bytes 12292
  0.0 2.8 %copy-start = (s32[1,1024,1]{1,2,0:T(1,128)S(1)}, s32[1,1024,1]{1,2,0:T(1,128)}, u32[]{:S(2)}) copy-start(s32[1,1024,1]{1,2,0:T(1,128)} %param.8) | copy-start | bytes 12292
  0.0 51.1 %copy-start.3 = (f32[8,3]{0,1:T(4,128)S(1)}, f32[8,3]{0,1:T(4,128)}, u32[]{:S(2)}) copy-start(f32[8,3]{0,1:T(4,128)} %param.12) | copy-start | bytes 292
